TPU v7x, 32 devices: a whole 2x2x4 slice. The times are simulated.
32 devices in a mesh: day: 2 (over x), sta: 16 (over z, y, core).
Axes of the slice: x: 2, y: 2, z: 4, core: 2. Of those that a mesh axis runs over, the one named last changes fastest.
Arguments:
- spectra: bfloat16 [256, 4, 2, 8192], P(('day', 'sta')), parts along dimension 0, may hold values from -6 to 6
- window_mask: int32 [256, 4], P(('day', 'sta')), parts along dimension 0, may hold values from 0 to 1, as said below
- pair_slots: int32 [32, 2], P('sta'), may hold values from -1 to 15, as said below
Outputs:
- stacks: bfloat16 [64, 8, 8, 1024], P(('day', 'sta')), parts along dimension 0
There are 2 independent parts, one for each index of `day`. A program takes and returns all parts, laid end to end along the dimension named above; an argument that names none is the same for every part. Nothing has to cross between parts.
Inputs may be any that keep to these rules, and one draw needn't show every extreme that they name: `pair_slots`: row o * 2 + c is slot c of owner block o: either (-1, -1), an empty slot, or two blocks a <= b, each within 2 blocks of o. An owner's live slots come before its empty ones; some owner fills all 2 slots and some owner has none. `window_mask`: in every draw some stations have no valid window at all.
All inputs are finite; a program needn't handle non-finite values.
Results may differ from a plain program's by a relative error of at most 0.0047.
Values may be sent and summed in bfloat16 or wider, within the bound.
No kernel may reach another device: no remote copies, remote signals or barrier semaphores. Data moves between devices by JAX's collectives and lax.ppermute only.
A program may use at most 128 MiB of HBM per device.

v0:
```python
import functools
import math

import jax
import jax.numpy as jnp
from jax import lax
from jax.experimental import pallas as pl
from jax.experimental.pallas import tpu as pltpu
from jax.sharding import PartitionSpec as P

LAGS = 1024
REACH = 2
CHUNKS = 4
SUB = 512
FINE = 64
LANES = 128


def permute(array, pairs):
    return lax.ppermute(array, "sta", pairs)


def angle_tables(index, lag_half, frequency_values):
    lag_index = jnp.arange(1, lag_half + 1, dtype=jnp.int32)
    phase_index = jnp.mod(index[:, None] * lag_index[None, :], 2 * frequency_values)
    phase_angle = phase_index.astype(jnp.float32) * (math.pi / frequency_values)
    return jnp.cos(phase_angle), jnp.sin(phase_angle)


def table_kernel(fine_cos, fine_sin, coarse_cos, coarse_sin, cos_ref, sin_ref):
    rows = cos_ref.shape[0]
    fc = fine_cos[...]
    fs = fine_sin[...]
    for group in range(rows // FINE):
        cc = coarse_cos[group : group + 1, :]
        cs = coarse_sin[group : group + 1, :]
        at = pl.ds(group * FINE, FINE)
        cos_ref[at, :] = (cc * fc - cs * fs).astype(jnp.bfloat16)
        sin_ref[at, :] = (cs * fc + cc * fs).astype(jnp.bfloat16)


def lag_tables(start, count, frequency_values, lag_half):
    fine = angle_tables(jnp.arange(FINE, dtype=jnp.int32), lag_half, frequency_values)
    coarse = angle_tables(
        start + FINE * jnp.arange(count // FINE, dtype=jnp.int32), lag_half, frequency_values
    )
    step = SUB
    table = jax.ShapeDtypeStruct((count, lag_half), jnp.bfloat16)
    return pl.pallas_call(
        table_kernel,
        grid=(count // step,),
        in_specs=[pl.BlockSpec((FINE, lag_half), lambda i: (0, 0))] * 2
        + [pl.BlockSpec((step // FINE, lag_half), lambda i: (i, 0))] * 2,
        out_specs=[pl.BlockSpec((step, lag_half), lambda i: (i, 0))] * 2,
        out_shape=[table, table],
        cost_estimate=pl.CostEstimate(
            flops=6 * count * lag_half, bytes_accessed=4 * count * lag_half, transcendentals=0
        ),
        name="lag_tables",
    )(*fine, *coarse)


def chunk_kernel(
    slots_ref, own_ref, par_ref, near_ref, far_ref, cos_ref, sin_ref, *rest, windows, stations, slot_count, first
):
    if first:
        acc_ref, stage, real_rows, imag_rows = rest
    else:
        before_ref, acc_ref, stage, real_rows, imag_rows = rest
    step = pl.program_id(0)
    lag_half = cos_ref.shape[1]
    pairs = stations * stations

    @pl.when(step == 0)
    def _():
        if first:
            acc_ref[...] = jnp.zeros_like(acc_ref)
        else:
            acc_ref[...] = before_ref[...]

    views = [own_ref, par_ref, near_ref.at[0], near_ref.at[1], far_ref.at[0], far_ref.at[1]]
    for at, view in enumerate(views):
        for window in range(windows):
            stage[at, window] = view[window].astype(jnp.float32)

    wide = 256

    def one_slot(slot, carry):
        first_at = slots_ref[slot, 0]
        second_at = slots_ref[slot, 1]
        base = pl.multiple_of(slot * pairs, pairs)

        @pl.when(slots_ref[slot, 2] > 0)
        def _():
            live_slot(first_at, second_at, base)

        @pl.when((slots_ref[slot, 2] == 0) & (step == 0))
        def _():
            empty = jnp.zeros((pairs, real_rows.shape[1]), jnp.bfloat16)
            real_rows[pl.ds(base, pairs), :] = empty
            imag_rows[pl.ds(base, pairs), :] = empty

        return carry

    def live_slot(first_at, second_at, base):
        for tile in range(own_ref.shape[-1] // wide):
            lanes = pl.ds(tile * wide, wide)
            second = [
                [
                    stage[second_at, window, pl.ds(part * stations, stations), lanes]
                    for part in range(2)
                ]
                for window in range(windows)
            ]
            for couple in range(0, stations, 2):
                real_out = []
                imag_out = []
                for station in (couple, couple + 1):
                    real = imag = None
                    for window in range(windows):
                        xr = stage[first_at, window, pl.ds(station, 1), lanes]
                        xi = stage[first_at, window, pl.ds(stations + station, 1), lanes]
                        yr, yi = second[window]
                        r = xr * yr + xi * yi
                        i = xi * yr - xr * yi
                        real = r if real is None else real + r
                        imag = i if imag is None else imag + i
                    real_out.append(real)
                    imag_out.append(imag)
                rows = pl.ds(base + couple * stations, 2 * stations)
                real = jnp.concatenate(real_out, axis=0)
                imag = jnp.concatenate(imag_out, axis=0)
                real_rows[rows, lanes] = real.astype(jnp.bfloat16)
                imag_rows[rows, lanes] = imag.astype(jnp.bfloat16)
                total = real[:, :LANES]
                for lane in range(LANES, wide, LANES):
                    total = total + real[:, lane : lane + LANES]
                acc_ref[rows, pl.ds(2 * lag_half, LANES)] += total

    lax.fori_loop(0, slot_count, one_slot, 0)
    acc_ref[:, :lag_half] += jnp.dot(
        real_rows[...], cos_ref[...], preferred_element_type=jnp.float32
    )
    acc_ref[:, lag_half : 2 * lag_half] += jnp.dot(
        imag_rows[...], sin_ref[...], preferred_element_type=jnp.float32
    )


def chunk_call(at, slots, own, par, near, far, cos_table, sin_table, before, windows, stations):
    slot_count = slots.shape[0]
    count = cos_table.shape[0] // CHUNKS
    lag_half = cos_table.shape[1]
    steps = count // SUB
    rows = slot_count * stations * stations
    acc = jax.ShapeDtypeStruct((rows, 2 * lag_half + LANES), jnp.float32)
    acc_spec = pl.BlockSpec(acc.shape, lambda i, s: (0, 0))
    single = (windows, 2 * stations, SUB)
    in_specs = [
        pl.BlockSpec(single, lambda i, s: (0, 0, i)),
        pl.BlockSpec(single, lambda i, s: (0, 0, i + at * steps)),
        pl.BlockSpec((2,) + single, lambda i, s: (0, 0, 0, i)),
        pl.BlockSpec((2,) + single, lambda i, s: (0, 0, 0, i)),
        pl.BlockSpec((SUB, lag_half), lambda i, s: (i + at * steps, 0)),
        pl.BlockSpec((SUB, lag_half), lambda i, s: (i + at * steps, 0)),
    ]
    operands = [own, par, near, far, cos_table, sin_table]
    aliases = {}
    if before is not None:
        in_specs.append(acc_spec)
        operands.append(before)
        aliases = {len(operands): 0}
    return pl.pallas_call(
        functools.partial(
            chunk_kernel, windows=windows, stations=stations, slot_count=slot_count, first=before is None
        ),
        grid_spec=pltpu.PrefetchScalarGridSpec(
            num_scalar_prefetch=1,
            grid=(steps,),
            in_specs=in_specs,
            out_specs=acc_spec,
            scratch_shapes=[
                pltpu.VMEM((6, windows, 2 * stations, SUB), jnp.float32),
                pltpu.VMEM((rows, SUB), jnp.bfloat16),
                pltpu.VMEM((rows, SUB), jnp.bfloat16),
            ],
        ),
        out_shape=acc,
        input_output_aliases=aliases,
        cost_estimate=pl.CostEstimate(
            flops=4 * rows * count * lag_half, bytes_accessed=4 * count * lag_half, transcendentals=0
        ),
        name="cross_chunk",
    )(slots, *operands)


def finish_kernel(
    slots_ref, mine_ref, other_ref, own_ref, par_ref, near_ref, far_ref, out_ref, marks, *, windows, stations, norm
):
    lag_half = out_ref.shape[1] // 2
    pairs = stations * stations
    views = [own_ref, par_ref, near_ref.at[0], near_ref.at[1], far_ref.at[0], far_ref.at[1]]
    for at, view in enumerate(views):
        for window in range(windows):
            marks[at, window] = view[window].astype(jnp.float32)[:stations]
    half = 256
    rows_at = lax.broadcasted_iota(jnp.int32, (half, half), 0)
    lanes_at = lax.broadcasted_iota(jnp.int32, (half, half), 1)
    flip = (rows_at + lanes_at == half - 1).astype(jnp.bfloat16)
    lane = lax.broadcasted_iota(jnp.int32, (stations, lag_half), 1)
    for slot in range(out_ref.shape[0] // pairs):
        first_at = slots_ref[slot, 0]
        second_at = slots_ref[slot, 1]
        left_rows = []
        for station in range(stations):
            count = None
            for window in range(windows):
                term = marks[first_at, window, pl.ds(station, 1), :] * marks[second_at, window]
                count = term if count is None else count + term
            weight = 1.0 / (norm * jnp.maximum(count, 1.0))
            weight = weight[:, :1]
            rows = pl.ds(slot * pairs + station * stations, stations)
            even = mine_ref[rows, :lag_half] + other_ref[rows, :lag_half]
            odd = (
                mine_ref[rows, lag_half : 2 * lag_half] + other_ref[rows, lag_half : 2 * lag_half]
            )
            still = jnp.sum(
                mine_ref[rows, 2 * lag_half :] + other_ref[rows, 2 * lag_half :], axis=1, keepdims=True
            )
            right = pltpu.roll(even - odd, 1, 1)
            right = jnp.where(lane == 0, still, right)
            out_ref[rows, lag_half:] = (right * weight).astype(jnp.bfloat16)
            left_rows.append((even + odd) * weight)
        left = jnp.concatenate(left_rows, axis=0).astype(jnp.bfloat16)
        rows = pl.ds(slot * pairs, pairs)
        for start in range(0, lag_half, half):
            out_ref[rows, lag_half - start - half : lag_half - start] = jnp.dot(
                left[:, start : start + half], flip, preferred_element_type=jnp.float32
            ).astype(jnp.bfloat16)


def finish_call(slots, mine, other, own, par, near, far, at, par_at, windows, stations, frequency_values):
    rows = mine.shape[0]
    lag_count = mine.shape[1] - LANES
    single = (windows, 2 * stations, LANES)
    whole = pl.BlockSpec(mine.shape, lambda i, s: (0, 0))
    return pl.pallas_call(
        functools.partial(
            finish_kernel, windows=windows, stations=stations, norm=math.sqrt(frequency_values)
        ),
        grid_spec=pltpu.PrefetchScalarGridSpec(
            num_scalar_prefetch=1,
            grid=(1,),
            in_specs=[
                whole,
                whole,
                pl.BlockSpec(single, lambda i, s: (0, 0, at)),
                pl.BlockSpec(single, lambda i, s: (0, 0, par_at)),
                pl.BlockSpec((2,) + single, lambda i, s: (0, 0, 0, at)),
                pl.BlockSpec((2,) + single, lambda i, s: (0, 0, 0, at)),
            ],
            out_specs=pl.BlockSpec((rows, lag_count), lambda i, s: (0, 0)),
            scratch_shapes=[pltpu.VMEM((6, windows, stations, LANES), jnp.float32)],
        ),
        out_shape=jax.ShapeDtypeStruct((rows, lag_count), jnp.bfloat16),
        cost_estimate=pl.CostEstimate(
            flops=4 * rows * lag_count, bytes_accessed=10 * rows * lag_count, transcendentals=0
        ),
        name="finish",
    )(slots, mine, other, own, par, near, far)


def shards(spectra, window_mask, pair_slots):
    stations, windows, _, frequency_values = spectra.shape
    slot_count = pair_slots.shape[0]
    half = frequency_values // 2
    count = half // CHUNKS
    peers = lax.axis_size("sta")
    me = lax.axis_index("sta")
    core = me % 2
    chip = me // 2
    core_pairs = [(i, i ^ 1) for i in range(peers)]
    near_pairs = [(i, i ^ 2) for i in range(peers)]
    far_pairs = [
        (i, i + 4 - 8 * ((i // 2) % 2))
        for i in range(peers)
        if 0 <= i + 4 - 8 * ((i // 2) % 2) < peers
    ]
    valid = window_mask.astype(jnp.bfloat16).T[:, None, :, None]
    mark = jnp.broadcast_to(valid, (windows, 2, stations, LANES)).reshape(
        windows, 2 * stations, LANES
    )

    def rows_of(start, size):
        piece = lax.dynamic_slice_in_dim(spectra, start, size, 3)
        return (piece.transpose(1, 2, 0, 3) * valid).reshape(windows, 2 * stations, size)

    sent = jnp.concatenate([rows_of((1 - core) * half, half), mark], axis=2)
    par = permute(sent, core_pairs)
    other_slots = permute(pair_slots, core_pairs)
    own = [rows_of(core * half + at * count, count) for at in range(CHUNKS)]
    own[0] = jnp.concatenate([own[0], mark], axis=2)
    near = []
    for at in range(CHUNKS):
        piece = par[:, :, at * count : (at + 1) * count]
        if at == 0:
            piece = jnp.concatenate([piece, par[:, :, half:]], axis=2)
        near.append(permute(jnp.stack([own[at], piece]), near_pairs))
    far = [permute(piece, far_pairs) for piece in near]

    cos_table, sin_table = lag_tables(core * half, half, frequency_values, LAGS // 2)
    slots = jnp.concatenate([pair_slots, other_slots], axis=0)
    slot_chip = slots // 2
    group = jnp.where(slot_chip == chip, 0, jnp.where(slot_chip == (chip ^ 1), 1, 2))
    other_core = (slots % 2 != core).astype(jnp.int32)
    index = group * 2 + other_core
    live = (slots[:, :1] >= 0).astype(jnp.int32)
    table = jnp.concatenate([index, live], axis=1)
    acc = None
    for at in range(CHUNKS):
        acc = chunk_call(
            at, table, own[at], par, near[at], far[at], cos_table, sin_table, acc, windows, stations
        )
    rows = slot_count * stations * stations
    mine = acc[:rows]
    other = permute(acc[rows:], core_pairs)
    out = finish_call(
        table, mine, other, own[0], par, near[0], far[0], count // LANES, half // LANES, windows, stations, frequency_values
    )
    return out.reshape(slot_count, stations, stations, LAGS)


def solution(mesh):
    placed = (P(("day", "sta"), None, None, None), P(("day", "sta"), None), P("sta", None))
    return jax.shard_map(
        shards,
        mesh=mesh,
        in_specs=placed,
        out_specs=P(("day", "sta"), None, None, None),
        check_vma=False,
    )
```

profile of v0, /device:TPU:23, one launch (start us, length us, event | category | flops | bytes accessed | tf_op | source)
XLA Modules:
  0.0 78.6 jit_solution(4760701915370766504)
XLA Ops:
  0.0 0.7 convert_bitcast_fusion
  0.7 0.1 copy.7
  0.8 1.6 %bitcast_multiply_fusion = bf16[4,2,8,4096]{3,1,0,2:T(2,128)(2,1)S(1)} fusion(bf16[8,4,2,8192]{3,2,1,0:T(2,128)(2,1)} %param.3, s32[]{:T(128)S(6)} %select_n.64, bf16[4,8]{0,1:T(8,128)(2,1)S(1)} %copy.7), kind=kLoop, calls=%fused_computation.1 | loop fusion | flops 1048576 | bytes 1048644 | tf_op jit(solution)/shard_map/mul | solution.py:295
  2.4 0.0 copy-start.14
  2.4 0.0 copy-start.6
  2.4 0.3 copy.25
  2.7 0.1 broadcast_in_dim.12
  2.8 0.1 broadcast_in_dim.22
  3.0 0.7 collective-permute-start.1
  3.7 0.1 collective-permute-start
  3.8 0.7 bitcast_multiply_fusion.1
  4.5 0.1 copy.26
  4.6 0.1 copy.27
  4.6 0.1 copy.28
  4.8 0.7 fusion.16
  5.4 0.1 fusion.18
  5.6 0.3 collective-permute-start.8
  5.9 0.3 copy-done
  6.2 1.0 %collective-permute-start.6 = (bf16[2,4,16,1024]{3,2,1,0:T(8,128)(2,1)S(1)}, bf16[2,4,16,1024]{3,2,1,0:T(8,128)(2,1)S(1)}, u32[]{:S(2)}, u32[]{:S(2)}) collective-permute-start(bf16[2,4,16,1024]{3,2,1,0:T(8,128)(2,1)S(1)} %pad_maximum_fusion.4), channel_id=1, source_target_pairs={{0,2},{1,3},{2,0},{3,1},{4,6},{5,7},{6,4},{7,5},{8,10},{9,11},{10,... | collective-permute-start | bytes 786440 | tf_op jit(solution)/shard_map/ppermute | solution.py:20
  7.3 0.5 collective-permute-start.4
  7.8 1.9 %fusion.11 = (f32[64,512]{1,0:T(8,128)}, f32[64,512]{1,0:T(8,128)}, f32[64,512]{1,0:T(8,128)}, f32[64,512]{1,0:T(8,128)}) fusion(s32[512]{0:T(512)S(1)} %iota_add_fusion, s32[64]{0:T(128)S(1)} %multiply_add_fusion), kind=kLoop, calls=%fused_computation.42 | loop fusion | flops 917504 | bytes 526592 | tf_op jit(solution)/shard_map/sin | solution.py:27
  9.7 0.1 copy.29
  9.8 6.8 %lag_tables.1 = (bf16[4096,512]{1,0:T(8,128)(2,1)}, bf16[4096,512]{1,0:T(8,128)(2,1)}) custom-call(f32[64,512]{1,0:T(8,128)} %get-tuple-element.30.fine_cos, f32[64,512]{1,0:T(8,128)} %get-tuple-element.29.fine_sin, f32[64,512]{1,0:T(8,128)} %get-tuple-element.28.coarse_cos, f32[64,512]{1,0:T(8,128)} %get-tuple-element.27.coarse_sin), custom_call_target="tpu_custom_call" | custom-call | flops 12582912 | bytes 8388608 | tf_op jit(solution)/shard_map/lag_tables/pallas_call | solution.py:49
  16.6 1.1 %collective-permute-start.2 = (bf16[2,4,16,1024]{3,2,1,0:T(8,128)(2,1)S(1)}, bf16[2,4,16,1024]{3,2,1,0:T(8,128)(2,1)S(1)}, u32[]{:S(2)}, u32[]{:S(2)}) collective-permute-start(bf16[2,4,16,1024]{3,2,1,0:T(8,128)(2,1)S(1)} %pad_maximum_fusion.2), channel_id=1, source_target_pairs={{0,2},{1,3},{2,0},{3,1},{4,6},{5,7},{6,4},{7,5},{8,10},{9,11},{10,... | collective-permute-start | bytes 786440 | tf_op jit(solution)/shard_map/ppermute | solution.py:20
  17.7 0.0 collective-permute-done
  17.7 1.6 %collective-permute-done.6.near_ref = bf16[2,4,16,1024]{3,2,1,0:T(8,128)(2,1)S(1)} collective-permute-done((bf16[2,4,16,1024]{3,2,1,0:T(8,128)(2,1)S(1)}, bf16[2,4,16,1024]{3,2,1,0:T(8,128)(2,1)S(1)}, u32[]{:S(2)}, u32[]{:S(2)}) %collective-permute-start.6) | collective-permute-done | bytes 262176 | tf_op jit(solution)/shard_map/ppermute | solution.py:20
  19.3 2.1 %collective-permute-start.7 = (bf16[2,4,16,1024]{3,2,1,0:T(8,128)(2,1)S(1)}, bf16[2,4,16,1024]{3,2,1,0:T(8,128)(2,1)S(1)}, u32[]{:S(2)}, u32[]{:S(2)}) collective-permute-start(bf16[2,4,16,1024]{3,2,1,0:T(8,128)(2,1)S(1)} %collective-permute-done.6.near_ref), channel_id=1, source_target_pairs={{0,4},{1,5},{4,8},{5,9},{6,2},{7,3},{8,12},{9,13},{10,6},{11,7},{1... | collective-permute-start | bytes 786440 | tf_op jit(solution)/shard_map/ppermute | solution.py:20
  21.4 3.5 %collective-permute-done.4.near_ref = bf16[2,4,16,1024]{3,2,1,0:T(8,128)(2,1)S(1)} collective-permute-done((bf16[2,4,16,1024]{3,2,1,0:T(8,128)(2,1)S(1)}, bf16[2,4,16,1024]{3,2,1,0:T(8,128)(2,1)S(1)}, u32[]{:S(2)}, u32[]{:S(2)}) %collective-permute-start.4) | collective-permute-done | bytes 262176 | tf_op jit(solution)/shard_map/ppermute | solution.py:20
  24.9 2.1 %collective-permute-start.5 = (bf16[2,4,16,1024]{3,2,1,0:T(8,128)(2,1)S(1)}, bf16[2,4,16,1024]{3,2,1,0:T(8,128)(2,1)S(1)}, u32[]{:S(2)}, u32[]{:S(2)}) collective-permute-start(bf16[2,4,16,1024]{3,2,1,0:T(8,128)(2,1)S(1)} %collective-permute-done.4.near_ref), channel_id=1, source_target_pairs={{0,4},{1,5},{4,8},{5,9},{6,2},{7,3},{8,12},{9,13},{10,6},{11,7},{1... | collective-permute-start | bytes 786440 | tf_op jit(solution)/shard_map/ppermute | solution.py:20
  27.0 0.0 collective-permute-done.8.near_ref
  27.0 2.1 %collective-permute-start.9 = (bf16[2,4,16,1152]{3,2,1,0:T(8,128)(2,1)S(1)}, bf16[2,4,16,1152]{3,2,1,0:T(8,128)(2,1)S(1)}, u32[]{:S(2)}, u32[]{:S(2)}) collective-permute-start(bf16[2,4,16,1152]{3,2,1,0:T(8,128)(2,1)S(1)} %collective-permute-done.8.near_ref), channel_id=1, source_target_pairs={{0,4},{1,5},{4,8},{5,9},{6,2},{7,3},{8,12},{9,13},{10,6},{11,7},{1... | collective-permute-start | bytes 884744 | tf_op jit(solution)/shard_map/ppermute | solution.py:20
  29.1 1.4 %collective-permute-done.2.near_ref = bf16[2,4,16,1024]{3,2,1,0:T(8,128)(2,1)S(1)} collective-permute-done((bf16[2,4,16,1024]{3,2,1,0:T(8,128)(2,1)S(1)}, bf16[2,4,16,1024]{3,2,1,0:T(8,128)(2,1)S(1)}, u32[]{:S(2)}, u32[]{:S(2)}) %collective-permute-start.2) | collective-permute-done | bytes 262176 | tf_op jit(solution)/shard_map/ppermute | solution.py:20
  30.5 2.1 %collective-permute-start.3 = (bf16[2,4,16,1024]{3,2,1,0:T(8,128)(2,1)S(1)}, bf16[2,4,16,1024]{3,2,1,0:T(8,128)(2,1)S(1)}, u32[]{:S(2)}, u32[]{:S(2)}) collective-permute-start(bf16[2,4,16,1024]{3,2,1,0:T(8,128)(2,1)S(1)} %collective-permute-done.2.near_ref), channel_id=1, source_target_pairs={{0,4},{1,5},{4,8},{5,9},{6,2},{7,3},{8,12},{9,13},{10,6},{11,7},{1... | collective-permute-start | bytes 786440 | tf_op jit(solution)/shard_map/ppermute | solution.py:20
  32.6 0.7 pad_add_fusion.1.slots_ref
  33.3 5.4 %collective-permute-done.9.far_ref = bf16[2,4,16,1152]{3,2,1,0:T(8,128)(2,1)S(1)} collective-permute-done((bf16[2,4,16,1152]{3,2,1,0:T(8,128)(2,1)S(1)}, bf16[2,4,16,1152]{3,2,1,0:T(8,128)(2,1)S(1)}, u32[]{:S(2)}, u32[]{:S(2)}) %collective-permute-start.9) | collective-permute-done | bytes 294944 | tf_op jit(solution)/shard_map/ppermute | solution.py:20
  38.7 0.7 copy-done.5
  39.4 5.6 %cross_chunk.4.rest_0_ = f32[256,1152]{1,0:T(8,128)} custom-call(s32[4,3]{1,0:T(4,128)} %pad_add_fusion.1.slots_ref, bf16[4,16,1152]{2,1,0:T(8,128)(2,1)} %get-tuple-element.20.own_ref, bf16[4,16,4224]{2,1,0:T(8,128)(2,1)} %copy-done, bf16[2,4,16,1152]{3,2,1,0:T(8,128)(2,1)} %copy-done.4, bf16[2,4,16,1152]{3,2,1,0:T(8,128)(2,1)} %copy-done.5, ...), custom_call_target="tpu_custom_call" | custom-call | flops 536870912 | bytes 2097152 | tf_op jit(solution)/shard_map/cross_chunk/pallas_call | solution.py:172
  45.0 0.7 copy-done.11
  45.7 6.0 %cross_chunk.5.rest_0_ = f32[256,1152]{1,0:T(8,128)} custom-call(s32[4,3]{1,0:T(4,128)} %pad_add_fusion.1.slots_ref, bf16[4,16,1024]{2,1,0:T(8,128)(2,1)} %bitcast.48, bf16[4,16,4224]{2,1,0:T(8,128)(2,1)} %copy-done, bf16[2,4,16,1024]{3,2,1,0:T(8,128)(2,1)} %copy-done.9, bf16[2,4,16,1024]{3,2,1,0:T(8,128)(2,1)} %copy-done.11, ...), custom_call_target="tpu_custom_call", output_to_operand_aliasing={{}: (7, {})} | custom-call | flops 536870912 | bytes 2097152 | tf_op jit(solution)/shard_map/cross_chunk/pallas_call | solution.py:172
  51.6 0.7 copy-done.12
  52.3 6.0 %cross_chunk.6.rest_0_ = f32[256,1152]{1,0:T(8,128)} custom-call(s32[4,3]{1,0:T(4,128)} %pad_add_fusion.1.slots_ref, bf16[4,16,1024]{2,1,0:T(8,128)(2,1)} %bitcast.46, bf16[4,16,4224]{2,1,0:T(8,128)(2,1)} %copy-done, bf16[2,4,16,1024]{3,2,1,0:T(8,128)(2,1)} %copy-done.8, bf16[2,4,16,1024]{3,2,1,0:T(8,128)(2,1)} %copy-done.12, ...), custom_call_target="tpu_custom_call", output_to_operand_aliasing={{}: (7, {})} | custom-call | flops 536870912 | bytes 2097152 | tf_op jit(solution)/shard_map/cross_chunk/pallas_call | solution.py:172
  58.3 0.7 copy-done.13
  59.0 6.0 %cross_chunk.7 = f32[256,1152]{1,0:T(8,128)} custom-call(s32[4,3]{1,0:T(4,128)} %pad_add_fusion.1.slots_ref, bf16[4,16,1024]{2,1,0:T(8,128)(2,1)} %bitcast.50, bf16[4,16,4224]{2,1,0:T(8,128)(2,1)} %copy-done, bf16[2,4,16,1024]{3,2,1,0:T(8,128)(2,1)} %copy-done.10, bf16[2,4,16,1024]{3,2,1,0:T(8,128)(2,1)} %copy-done.13, ...), custom_call_target="tpu_custom_call", output_to_operand_aliasing={{}: (7, {})} | custom-call | flops 536870912 | bytes 2097152 | tf_op jit(solution)/shard_map/cross_chunk/pallas_call | solution.py:172
  65.0 2.1 %fusion.17 = (f32[128,1152]{1,0:T(8,128)S(1)}, f32[128,1152]{1,0:T(8,128)}) fusion(f32[256,1152]{1,0:T(8,128)} %cross_chunk.7), kind=kLoop, calls=%fused_computation.61 | loop fusion | bytes 2359296 | tf_op jit(solution)/shard_map/slice | solution.py:325
  67.1 6.0 %collective-permute-start.10 = (f32[128,1152]{1,0:T(8,128)S(1)}, f32[128,1152]{1,0:T(8,128)S(1)}, u32[]{:S(2)}, u32[]{:S(2)}) collective-permute-start(f32[128,1152]{1,0:T(8,128)S(1)} %get-tuple-element.9), channel_id=1, source_target_pairs={{0,1},{1,0},{2,3},{3,2},{4,5},{5,4},{6,7},{7,6},{8,9},{9,8},{10,11... | collective-permute-start | bytes 1769480 | tf_op jit(solution)/shard_map/ppermute | solution.py:20
  73.1 1.6 %collective-permute-done.10.other_ref = f32[128,1152]{1,0:T(8,128)S(1)} collective-permute-done((f32[128,1152]{1,0:T(8,128)S(1)}, f32[128,1152]{1,0:T(8,128)S(1)}, u32[]{:S(2)}, u32[]{:S(2)}) %collective-permute-start.10) | collective-permute-done | bytes 589856 | tf_op jit(solution)/shard_map/ppermute | solution.py:20
  74.8 0.8 %copy-done.7 = f32[128,1152]{1,0:T(8,128)} copy-done((f32[128,1152]{1,0:T(8,128)}, f32[128,1152]{1,0:T(8,128)S(1)}, u32[]{:S(2)}) %copy-start.7) | copy-done | bytes 589848
  75.6 3.0 %finish.1 = bf16[128,1024]{1,0:T(8,128)(2,1)} custom-call(s32[4,3]{1,0:T(4,128)} %pad_add_fusion.1.slots_ref, f32[128,1152]{1,0:T(8,128)} %get-tuple-element.10.mine_ref, f32[128,1152]{1,0:T(8,128)} %copy-done.7, bf16[4,16,1152]{2,1,0:T(8,128)(2,1)} %get-tuple-element.20.own_ref, bf16[4,16,4224]{2,1,0:T(8,128)(2,1)} %copy-done, ...), custom_call_target="tpu_custom_call" | custom-call | flops 524288 | bytes 1310720 | tf_op jit(solution)/shard_map/finish/pallas_call | solution.py:246
  (38 shorter events, 0.3 us)
Async XLA Ops:
  2.4 1.3 %copy-start.14 = (s32[2,2]{1,0:T(2,128)S(1)}, s32[2,2]{1,0:T(2,128)}, u32[]{:S(2)}) copy-start(s32[2,2]{1,0:T(2,128)} %param.5) | copy-start | bytes 52
  2.4 1.4 %copy-start.6 = (bf16[8,4,2,8192]{3,2,1,0:T(2,128)(2,1)S(1)}, bf16[8,4,2,8192]{3,2,1,0:T(2,128)(2,1)}, u32[]{:S(2)}) copy-start(bf16[8,4,2,8192]{3,2,1,0:T(2,128)(2,1)} %param.3) | copy-start | bytes 3145732
  3.0 2.5 %collective-permute-start.1 = (bf16[4,16,4224]{2,1,0:T(8,128)(2,1)S(1)}, bf16[4,16,4224]{2,1,0:T(8,128)(2,1)S(1)}, u32[]{:S(2)}, u32[]{:S(2)}) collective-permute-start(bf16[4,16,4224]{2,1,0:T(8,128)(2,1)S(1)} %pad_maximum_fusion), channel_id=1, source_target_pairs={{0,1},{1,0},{2,3},{3,2},{4,5},{5,4},{6,7},{7,6},{8,9},{9,8},{10,11... | collective-permute-start | bytes 1622024 | tf_op jit(solution)/shard_map/ppermute | solution.py:20
  3.7 14.0 %collective-permute-start = (s32[2,2]{1,0:T(2,128)S(1)}, s32[2,2]{1,0:T(2,128)S(1)}, u32[]{:S(2)}, u32[]{:S(2)}) collective-permute-start(s32[2,2]{1,0:T(2,128)S(1)} %copy-done.14), channel_id=1, source_target_pairs={{0,1},{1,0},{2,3},{3,2},{4,5},{5,4},{6,7},{7,6},{8,9},{9,8},{10,11... | collective-permute-start | bytes 56 | tf_op jit(solution)/shard_map/ppermute | solution.py:20
  4.6 1.2 %copy-start.2 = (bf16[4,2,8,1024]{3,2,1,0:T(8,128)(2,1)}, bf16[4,2,8,1024]{3,2,1,0:T(8,128)(2,1)S(1)}, u32[]{:S(2)}) copy-start(bf16[4,2,8,1024]{3,2,1,0:T(8,128)(2,1)S(1)} %copy.27) | copy-start | bytes 393220
  4.7 2.5 %copy-start.1 = (bf16[4,2,8,1024]{3,2,1,0:T(8,128)(2,1)}, bf16[4,2,8,1024]{3,2,1,0:T(8,128)(2,1)S(1)}, u32[]{:S(2)}) copy-start(bf16[4,2,8,1024]{3,2,1,0:T(8,128)(2,1)S(1)} %copy.28) | copy-start | bytes 393220
  5.4 0.8 %copy-start = (bf16[4,16,4224]{2,1,0:T(8,128)(2,1)}, bf16[4,16,4224]{2,1,0:T(8,128)(2,1)S(1)}, u32[]{:S(2)}) copy-start(bf16[4,16,4224]{2,1,0:T(8,128)(2,1)S(1)} %collective-permute-done.1.par_ref) | copy-start | bytes 1622020
  5.6 21.4 %collective-permute-start.8 = (bf16[2,4,16,1152]{3,2,1,0:T(8,128)(2,1)S(1)}, bf16[2,4,16,1152]{3,2,1,0:T(8,128)(2,1)S(1)}, u32[]{:S(2)}, u32[]{:S(2)}) collective-permute-start(bf16[2,4,16,1152]{3,2,1,0:T(8,128)(2,1)S(1)} %pad_maximum_fusion.1), channel_id=1, source_target_pairs={{0,2},{1,3},{2,0},{3,1},{4,6},{5,7},{6,4},{7,5},{8,10},{9,11},{10,... | collective-permute-start | bytes 884744 | tf_op jit(solution)/shard_map/ppermute | solution.py:20
  6.2 13.1 %collective-permute-start.6 = (bf16[2,4,16,1024]{3,2,1,0:T(8,128)(2,1)S(1)}, bf16[2,4,16,1024]{3,2,1,0:T(8,128)(2,1)S(1)}, u32[]{:S(2)}, u32[]{:S(2)}) collective-permute-start(bf16[2,4,16,1024]{3,2,1,0:T(8,128)(2,1)S(1)} %pad_maximum_fusion.4), channel_id=1, source_target_pairs={{0,2},{1,3},{2,0},{3,1},{4,6},{5,7},{6,4},{7,5},{8,10},{9,11},{10,... | collective-permute-start | bytes 786440 | tf_op jit(solution)/shard_map/ppermute | solution.py:20
  7.3 17.7 %collective-permute-start.4 = (bf16[2,4,16,1024]{3,2,1,0:T(8,128)(2,1)S(1)}, bf16[2,4,16,1024]{3,2,1,0:T(8,128)(2,1)S(1)}, u32[]{:S(2)}, u32[]{:S(2)}) collective-permute-start(bf16[2,4,16,1024]{3,2,1,0:T(8,128)(2,1)S(1)} %pad_maximum_fusion.3), channel_id=1, source_target_pairs={{0,2},{1,3},{2,0},{3,1},{4,6},{5,7},{6,4},{7,5},{8,10},{9,11},{10,... | collective-permute-start | bytes 786440 | tf_op jit(solution)/shard_map/ppermute | solution.py:20
  9.8 35.2 %copy-start.3 = (bf16[4,2,8,1024]{3,2,1,0:T(8,128)(2,1)}, bf16[4,2,8,1024]{3,2,1,0:T(8,128)(2,1)S(1)}, u32[]{:S(2)}) copy-start(bf16[4,2,8,1024]{3,2,1,0:T(8,128)(2,1)S(1)} %copy.29) | copy-start | bytes 393220
  16.6 13.9 %collective-permute-start.2 = (bf16[2,4,16,1024]{3,2,1,0:T(8,128)(2,1)S(1)}, bf16[2,4,16,1024]{3,2,1,0:T(8,128)(2,1)S(1)}, u32[]{:S(2)}, u32[]{:S(2)}) collective-permute-start(bf16[2,4,16,1024]{3,2,1,0:T(8,128)(2,1)S(1)} %pad_maximum_fusion.2), channel_id=1, source_target_pairs={{0,2},{1,3},{2,0},{3,1},{4,6},{5,7},{6,4},{7,5},{8,10},{9,11},{10,... | collective-permute-start | bytes 786440 | tf_op jit(solution)/shard_map/ppermute | solution.py:20
  19.3 25.7 %copy-start.9 = (bf16[2,4,16,1024]{3,2,1,0:T(8,128)(2,1)}, bf16[2,4,16,1024]{3,2,1,0:T(8,128)(2,1)S(1)}, u32[]{:S(2)}) copy-start(bf16[2,4,16,1024]{3,2,1,0:T(8,128)(2,1)S(1)} %collective-permute-done.6.near_ref) | copy-start | bytes 786436
  19.3 25.7 %collective-permute-start.7 = (bf16[2,4,16,1024]{3,2,1,0:T(8,128)(2,1)S(1)}, bf16[2,4,16,1024]{3,2,1,0:T(8,128)(2,1)S(1)}, u32[]{:S(2)}, u32[]{:S(2)}) collective-permute-start(bf16[2,4,16,1024]{3,2,1,0:T(8,128)(2,1)S(1)} %collective-permute-done.6.near_ref), channel_id=1, source_target_pairs={{0,4},{1,5},{4,8},{5,9},{6,2},{7,3},{8,12},{9,13},{10,6},{11,7},{1... | collective-permute-start | bytes 786440 | tf_op jit(solution)/shard_map/ppermute | solution.py:20
  24.9 20.0 %copy-start.8 = (bf16[2,4,16,1024]{3,2,1,0:T(8,128)(2,1)}, bf16[2,4,16,1024]{3,2,1,0:T(8,128)(2,1)S(1)}, u32[]{:S(2)}) copy-start(bf16[2,4,16,1024]{3,2,1,0:T(8,128)(2,1)S(1)} %collective-permute-done.4.near_ref) | copy-start | bytes 786436
  24.9 26.7 %collective-permute-start.5 = (bf16[2,4,16,1024]{3,2,1,0:T(8,128)(2,1)S(1)}, bf16[2,4,16,1024]{3,2,1,0:T(8,128)(2,1)S(1)}, u32[]{:S(2)}, u32[]{:S(2)}) collective-permute-start(bf16[2,4,16,1024]{3,2,1,0:T(8,128)(2,1)S(1)} %collective-permute-done.4.near_ref), channel_id=1, source_target_pairs={{0,4},{1,5},{4,8},{5,9},{6,2},{7,3},{8,12},{9,13},{10,6},{11,7},{1... | collective-permute-start | bytes 786440 | tf_op jit(solution)/shard_map/ppermute | solution.py:20
  27.0 11.7 %copy-start.4 = (bf16[2,4,16,1152]{3,2,1,0:T(8,128)(2,1)}, bf16[2,4,16,1152]{3,2,1,0:T(8,128)(2,1)S(1)}, u32[]{:S(2)}) copy-start(bf16[2,4,16,1152]{3,2,1,0:T(8,128)(2,1)S(1)} %collective-permute-done.8.near_ref) | copy-start | bytes 884740
  27.0 11.7 %collective-permute-start.9 = (bf16[2,4,16,1152]{3,2,1,0:T(8,128)(2,1)S(1)}, bf16[2,4,16,1152]{3,2,1,0:T(8,128)(2,1)S(1)}, u32[]{:S(2)}, u32[]{:S(2)}) collective-permute-start(bf16[2,4,16,1152]{3,2,1,0:T(8,128)(2,1)S(1)} %collective-permute-done.8.near_ref), channel_id=1, source_target_pairs={{0,4},{1,5},{4,8},{5,9},{6,2},{7,3},{8,12},{9,13},{10,6},{11,7},{1... | collective-permute-start | bytes 884744 | tf_op jit(solution)/shard_map/ppermute | solution.py:20
  30.5 14.4 %copy-start.10 = (bf16[2,4,16,1024]{3,2,1,0:T(8,128)(2,1)}, bf16[2,4,16,1024]{3,2,1,0:T(8,128)(2,1)S(1)}, u32[]{:S(2)}) copy-start(bf16[2,4,16,1024]{3,2,1,0:T(8,128)(2,1)S(1)} %collective-permute-done.2.near_ref) | copy-start | bytes 786436
  30.5 27.8 %collective-permute-start.3 = (bf16[2,4,16,1024]{3,2,1,0:T(8,128)(2,1)S(1)}, bf16[2,4,16,1024]{3,2,1,0:T(8,128)(2,1)S(1)}, u32[]{:S(2)}, u32[]{:S(2)}) collective-permute-start(bf16[2,4,16,1024]{3,2,1,0:T(8,128)(2,1)S(1)} %collective-permute-done.2.near_ref), channel_id=1, source_target_pairs={{0,4},{1,5},{4,8},{5,9},{6,2},{7,3},{8,12},{9,13},{10,6},{11,7},{1... | collective-permute-start | bytes 786440 | tf_op jit(solution)/shard_map/ppermute | solution.py:20
  38.7 0.7 copy-start.5
  45.0 0.7 copy-start.11
  51.6 0.7 copy-start.12
  58.3 0.7 copy-start.13
  67.1 7.6 %collective-permute-start.10 = (f32[128,1152]{1,0:T(8,128)S(1)}, f32[128,1152]{1,0:T(8,128)S(1)}, u32[]{:S(2)}, u32[]{:S(2)}) collective-permute-start(f32[128,1152]{1,0:T(8,128)S(1)} %get-tuple-element.9), channel_id=1, source_target_pairs={{0,1},{1,0},{2,3},{3,2},{4,5},{5,4},{6,7},{7,6},{8,9},{9,8},{10,11... | collective-permute-start | bytes 1769480 | tf_op jit(solution)/shard_map/ppermute | solution.py:20
  74.8 0.8 %copy-start.7 = (f32[128,1152]{1,0:T(8,128)}, f32[128,1152]{1,0:T(8,128)S(1)}, u32[]{:S(2)}) copy-start(f32[128,1152]{1,0:T(8,128)S(1)} %collective-permute-done.10.other_ref) | copy-start | bytes 1769476
where the time goes:
time: 79.4 us; the launch traced here: 78.6 us
  Pallas kernels  33.3 us (42%)
  starting transfers between devices  18 us (23%)
  waiting for transfers between devices  13.6 us (17%)
  local copies, waits for them, and re-layouts  7.06 us (9%)
  other arithmetic  6.38 us (8%)
    pallas_call x4, Pallas kernels, chunk_call(): pl.pallas_call(functools.partial(chunk_kernel, windows=windows, stations=...  23.4 us
    ppermute x11, starting transfers between devices, permute(): return lax.ppermute(array, 'sta', pairs)  18 us
    ppermute x11, waiting for transfers between devices, permute(): return lax.ppermute(array, 'sta', pairs)  13.6 us
    pallas_call x1, Pallas kernels, lag_tables(): pl.pallas_call(table_kernel, grid=(count // step,), in_specs=[pl.BlockSpe...  6.81 us
    unnamed x30, local copies, waits for them, and re-layouts  3.99 us
    pallas_call x1, Pallas kernels, finish_call(): pl.pallas_call(functools.partial(finish_kernel, windows=windows, stations...  3.02 us
    mul x2, other arithmetic, rows_of(): piece.transpose(1, 2, 0, 3) * valid  2.29 us
    slice x1, local copies, waits for them, and re-layouts, shards(): other = permute(acc[rows:], core_pairs)  2.14 us
  transfers between devices with their start and end apart: 11, of which 5 were waited for; matrix products, arithmetic and copies ran while one was open for 6% of the time, Pallas kernels for 31%

commit v1 on v0

v1 whole, which is shorter than its diff:
```python
import functools
import math

import jax
import jax.numpy as jnp
from jax import lax
from jax.experimental import pallas as pl
from jax.experimental.pallas import tpu as pltpu
from jax.sharding import PartitionSpec as P


LAGS = 1024
CUTS = (0, 8, 12, 16)
SUB = 512
FINE = 64
LANES = 128
GRANT = 24 << 20


def permute(array, pairs):
    return lax.ppermute(array, "sta", pairs)


def angle_tables(index, lag_half, frequency_values):
    lag_index = jnp.arange(1, lag_half + 1, dtype=jnp.int32)
    phase_index = jnp.mod(index[:, None] * lag_index[None, :], 2 * frequency_values)
    phase_angle = phase_index.astype(jnp.float32) * (math.pi / frequency_values)
    return jnp.cos(phase_angle), jnp.sin(phase_angle)


def chunk_kernel(*refs, views_at, slot_count, windows, stations, first, last, low):
    refs = list(refs)
    slots_ref = refs.pop(0)
    sources = [refs.pop(0) for _ in range(1 + max(which for which, _, _ in views_at))]
    fine_cos, fine_sin, coarse_cos, coarse_sin = (refs.pop(0) for _ in range(4))
    before_ref = None if first else refs.pop(0)
    outs = [refs.pop(0) for _ in range(2 if last else 1)]
    stage, real_rows, imag_rows, cos_rows, sin_rows, still = refs
    count = stage.shape[-1]
    lag_half = cos_rows.shape[1]
    pairs = stations * stations
    rows = slot_count * pairs

    for at, (which, part, lane) in enumerate(views_at):
        view = sources[which] if part is None else sources[which].at[part]
        for window in range(windows):
            stage[at, window] = view[window, :, lane : lane + count].astype(jnp.float32)

    fc = fine_cos[...]
    fs = fine_sin[...]
    for group in range(count // FINE):
        coarse = slice(low // FINE + group, low // FINE + group + 1)
        cc = coarse_cos[coarse, :]
        cs = coarse_sin[coarse, :]
        at = pl.ds(group * FINE, FINE)
        cos_rows[at, :] = (cc * fc - cs * fs).astype(jnp.bfloat16)
        sin_rows[at, :] = (cs * fc + cc * fs).astype(jnp.bfloat16)

    def one_slot(slot, carry):
        base = pl.multiple_of(slot * pairs, pairs)
        still[pl.ds(base, pairs), :] = jnp.zeros((pairs, LANES), jnp.float32)

        @pl.when(slots_ref[slot, 2] > 0)
        def _():
            first_at = slots_ref[slot, 0]
            second_at = slots_ref[slot, 1]

            def one_sub(sub, carry):
                live_slot(first_at, second_at, base, sub * SUB)
                return carry

            lax.fori_loop(0, count // SUB, one_sub, 0)

        @pl.when(slots_ref[slot, 2] == 0)
        def _():
            empty = jnp.zeros((pairs, count), jnp.bfloat16)
            real_rows[pl.ds(base, pairs), :] = empty
            imag_rows[pl.ds(base, pairs), :] = empty

        return carry

    wide = 256

    def live_slot(first_at, second_at, base, start):
        for tile in range(SUB // wide):
            lanes = pl.ds(pl.multiple_of(start + tile * wide, wide), wide)
            second = [
                [
                    stage[second_at, window, pl.ds(part * stations, stations), lanes]
                    for part in range(2)
                ]
                for window in range(windows)
            ]
            for couple in range(0, stations, 2):
                real_out = []
                imag_out = []
                for station in (couple, couple + 1):
                    real = imag = None
                    for window in range(windows):
                        xr = stage[first_at, window, pl.ds(station, 1), lanes]
                        xi = stage[first_at, window, pl.ds(stations + station, 1), lanes]
                        yr, yi = second[window]
                        r = xr * yr + xi * yi
                        i = xi * yr - xr * yi
                        real = r if real is None else real + r
                        imag = i if imag is None else imag + i
                    real_out.append(real)
                    imag_out.append(imag)
                at = pl.ds(base + couple * stations, 2 * stations)
                real = jnp.concatenate(real_out, axis=0)
                imag = jnp.concatenate(imag_out, axis=0)
                real_rows[at, lanes] = real.astype(jnp.bfloat16)
                imag_rows[at, lanes] = imag.astype(jnp.bfloat16)
                total = real[:, :LANES]
                for lane in range(LANES, wide, LANES):
                    total = total + real[:, lane : lane + LANES]
                still[at, :] += total

    lax.fori_loop(0, slot_count, one_slot, 0)
    share = rows // len(outs)
    even = jnp.dot(real_rows[...], cos_rows[...], preferred_element_type=jnp.float32)
    odd = jnp.dot(imag_rows[...], sin_rows[...], preferred_element_type=jnp.float32)
    for lane, value in ((0, even), (lag_half, odd), (2 * lag_half, still[...])):
        lanes = slice(lane, lane + value.shape[1])
        if not first:
            value = value + before_ref[:, lanes]
        for at, out in enumerate(outs):
            out[:, lanes] = value[at * share : (at + 1) * share]


def chunk_call(slots, sources, views_at, tables, before, last, low, count, lag_half, windows, stations):
    slot_count = slots.shape[0]
    rows = slot_count * stations * stations
    outs = 2 if last else 1
    acc = jax.ShapeDtypeStruct((rows // outs, 2 * lag_half + LANES), jnp.float32)
    operands = list(sources) + list(tables)
    if before is not None:
        operands.append(before)
    vmem = pl.BlockSpec(memory_space=pltpu.VMEM)
    return pl.pallas_call(
        functools.partial(
            chunk_kernel,
            views_at=views_at,
            slot_count=slot_count,
            windows=windows,
            stations=stations,
            first=before is None,
            last=last,
            low=low,
        ),
        in_specs=[pl.BlockSpec(memory_space=pltpu.SMEM)] + [vmem] * len(operands),
        out_specs=[vmem] * outs,
        scratch_shapes=[
            pltpu.VMEM((6, windows, 2 * stations, count), jnp.float32),
            pltpu.VMEM((rows, count), jnp.bfloat16),
            pltpu.VMEM((rows, count), jnp.bfloat16),
            pltpu.VMEM((count, lag_half), jnp.bfloat16),
            pltpu.VMEM((count, lag_half), jnp.bfloat16),
            pltpu.VMEM((rows, LANES), jnp.float32),
        ],
        out_shape=[acc] * outs,
        input_output_aliases={} if before is None or last else {len(operands): 0},
        cost_estimate=pl.CostEstimate(
            flops=4 * rows * count * lag_half, bytes_accessed=4 * count * lag_half, transcendentals=0
        ),
        compiler_params=pltpu.CompilerParams(vmem_limit_bytes=GRANT),
    )(slots, *operands)


def finish_kernel(
    slots_ref, mine_ref, other_ref, own_ref, par_ref, near_own, near_par, far_own, far_par, out_ref, marks, *, windows, stations, norm
):
    lag_half = out_ref.shape[1] // 2
    pairs = stations * stations
    for at, view in enumerate([own_ref, par_ref, near_own, near_par, far_own, far_par]):
        for window in range(windows):
            marks[at, window] = view[window, :, :LANES].astype(jnp.float32)[:stations]
    half = 256
    rows_at = lax.broadcasted_iota(jnp.int32, (half, half), 0)
    lanes_at = lax.broadcasted_iota(jnp.int32, (half, half), 1)
    flip = (rows_at + lanes_at == half - 1).astype(jnp.bfloat16)
    lane = lax.broadcasted_iota(jnp.int32, (stations, lag_half), 1)
    for slot in range(out_ref.shape[0] // pairs):
        first_at = slots_ref[slot, 0]
        second_at = slots_ref[slot, 1]
        left_rows = []
        for station in range(stations):
            count = None
            for window in range(windows):
                term = marks[first_at, window, pl.ds(station, 1), :] * marks[second_at, window]
                count = term if count is None else count + term
            weight = 1.0 / (norm * jnp.maximum(count, 1.0))
            weight = weight[:, :1]
            rows = pl.ds(slot * pairs + station * stations, stations)
            even = mine_ref[rows, :lag_half] + other_ref[rows, :lag_half]
            odd = (
                mine_ref[rows, lag_half : 2 * lag_half] + other_ref[rows, lag_half : 2 * lag_half]
            )
            still = jnp.sum(
                mine_ref[rows, 2 * lag_half :] + other_ref[rows, 2 * lag_half :], axis=1, keepdims=True
            )
            right = pltpu.roll(even - odd, 1, 1)
            right = jnp.where(lane == 0, still, right)
            out_ref[rows, lag_half:] = (right * weight).astype(jnp.bfloat16)
            left_rows.append((even + odd) * weight)
        left = jnp.concatenate(left_rows, axis=0).astype(jnp.bfloat16)
        rows = pl.ds(slot * pairs, pairs)
        for start in range(0, lag_half, half):
            out_ref[rows, lag_half - start - half : lag_half - start] = jnp.dot(
                left[:, start : start + half], flip, preferred_element_type=jnp.float32
            ).astype(jnp.bfloat16)


def finish_call(slots, mine, other, marked, windows, stations, frequency_values):
    rows = mine.shape[0]
    lag_count = mine.shape[1] - LANES
    vmem = pl.BlockSpec(memory_space=pltpu.VMEM)
    return pl.pallas_call(
        functools.partial(
            finish_kernel, windows=windows, stations=stations, norm=math.sqrt(frequency_values)
        ),
        in_specs=[pl.BlockSpec(memory_space=pltpu.SMEM)] + [vmem] * 8,
        out_specs=vmem,
        scratch_shapes=[pltpu.VMEM((6, windows, stations, LANES), jnp.float32)],
        out_shape=jax.ShapeDtypeStruct((rows, lag_count), jnp.bfloat16),
        cost_estimate=pl.CostEstimate(
            flops=4 * rows * lag_count, bytes_accessed=10 * rows * lag_count, transcendentals=0
        ),
        compiler_params=pltpu.CompilerParams(vmem_limit_bytes=GRANT // 2),
        name="finish",
    )(slots, mine, other, *marked)


def owner_stacks(spectra, window_mask, pair_slots):
    stations, windows, _, frequency_values = spectra.shape
    slot_count = pair_slots.shape[0]
    half = frequency_values // 2
    lag_half = LAGS // 2
    peers = lax.axis_size("sta")
    me = lax.axis_index("sta")
    core = me & 1
    chip = me >> 1
    core_pairs = [(i, i ^ 1) for i in range(peers)]
    near_pairs = [(i, i ^ 2) for i in range(peers)]
    far_pairs = [
        (i, i + 4 - 8 * ((i // 2) % 2))
        for i in range(peers)
        if 0 <= i + 4 - 8 * ((i // 2) % 2) < peers
    ]
    valid = window_mask.astype(jnp.bfloat16).T[:, None, :, None]
    mark = jnp.broadcast_to(valid, (windows, 2, stations, LANES)).reshape(
        windows, 2 * stations, LANES
    )

    def rows_of(start, size):
        piece = lax.dynamic_slice_in_dim(spectra, start, size, 3)
        return (piece.transpose(1, 2, 0, 3) * valid).reshape(windows, 2 * stations, size)

    splits = [half * cut // 16 for cut in CUTS]
    lead = splits[1]
    own_lead = jnp.concatenate([mark, rows_of(core * half, lead)], axis=2)
    sent = jnp.concatenate([mark, rows_of((1 - core) * half, half)], axis=2)
    par = permute(sent, core_pairs)
    other_slots = permute(pair_slots, core_pairs)
    near = [permute(own_lead, near_pairs), permute(par[:, :, : LANES + lead], near_pairs)]
    own = []
    for at in range(1, len(splits) - 1):
        low, high = splits[at], splits[at + 1]
        own.append(rows_of(core * half + low, high - low))
        piece = jnp.stack([own[-1], par[:, :, LANES + low : LANES + high]])
        if high == half:
            piece, base = lax.optimization_barrier((piece, core * half))
        near.append(permute(piece, near_pairs))
    far = [permute(piece, far_pairs) for piece in near]

    fine = angle_tables(jnp.arange(FINE, dtype=jnp.int32), lag_half, frequency_values)
    coarse = angle_tables(
        base + FINE * jnp.arange(half // FINE, dtype=jnp.int32), lag_half, frequency_values
    )
    slots = jnp.concatenate([pair_slots, other_slots], axis=0)
    slot_chip = slots >> 1
    group = jnp.where(slot_chip == chip, 0, jnp.where(slot_chip == (chip ^ 1), 1, 2))
    other_core = ((slots & 1) != core).astype(jnp.int32)
    live = (slots[:, :1] >= 0).astype(jnp.int32)
    table = jnp.concatenate([group * 2 + other_core, live], axis=1)
    acc = None
    for at in range(len(splits) - 1):
        low, high = splits[at], splits[at + 1]
        last = at == len(splits) - 2
        if at == 0:
            sources = [own_lead, par, near[0], near[1], far[0], far[1]]
            views_at = [(which, None, LANES) for which in range(6)]
        else:
            sources = [own[at - 1], par, near[at + 1], far[at + 1]]
            views_at = [(0, None, 0), (1, None, LANES + low), (2, 0, 0), (2, 1, 0), (3, 0, 0), (3, 1, 0)]
        tables = list(fine) + list(coarse)
        acc = chunk_call(
            table, sources, views_at, tables, acc, last, low, high - low, lag_half, windows, stations
        )
        if not last:
            acc = acc[0]
    mine, other = acc
    other = permute(other, core_pairs)
    marked = [own_lead, par, near[0], near[1], far[0], far[1]]
    out = finish_call(table, mine, other, marked, windows, stations, frequency_values)
    return out.reshape(slot_count, stations, stations, LAGS)


def solution(mesh):
    placed = (P(("day", "sta"), None, None, None), P(("day", "sta"), None), P("sta", None))
    return jax.shard_map(
        owner_stacks,
        mesh=mesh,
        in_specs=placed,
        out_specs=P(("day", "sta"), None, None, None),
        check_vma=False,
    )
```

time: 79.4 us -> 50.5 us (0.64)
  the two profiles are of different devices: /device:TPU:23 before, /device:TPU:17 now
where the time goes in v1:
time: 50.5 us; the launch traced here: 50.2 us
  starting transfers between devices  19.4 us (38%)
  Pallas kernels  13.4 us (27%)
  waiting for transfers between devices  12.2 us (24%)
  other arithmetic  4.11 us (8%)
  local copies, waits for them, and re-layouts  0.92 us (2%)
    ppermute x11, starting transfers between devices, permute(): return lax.ppermute(array, 'sta', pairs)  19.4 us
    ppermute x11, waiting for transfers between devices, permute(): return lax.ppermute(array, 'sta', pairs)  12.2 us
    pallas_call x3, Pallas kernels, chunk_call(): pl.pallas_call(functools.partial(chunk_kernel, views_at=views_at, slot_co...  11.8 us
    mul x3, other arithmetic, rows_of(): piece.transpose(1, 2, 0, 3) * valid  2.15 us
    pallas_call x1, Pallas kernels, finish_call(): pl.pallas_call(functools.partial(finish_kernel, windows=windows, stations...  1.63 us
    sin x1, other arithmetic, angle_tables(): return (jnp.cos(phase_angle), jnp.sin(phase_angle))  1.06 us
  transfers between devices with their start and end apart: 11, of which 6 were waited for; matrix products, arithmetic and copies ran while one was open for 4% of the time, Pallas kernels for 17%

profile of v1, /device:TPU:17, one launch (start us, length us, event | category | flops | bytes accessed | tf_op | source)
XLA Modules:
  0.0 50.2 jit_solution(3823618982669567175)
XLA Ops:
  0.0 0.7 %convert_bitcast_fusion = bf16[4,8]{1,0:T(4,128)(2,1)S(1)} fusion(s32[8,4]{0,1:T(4,128)} %param.4), kind=kLoop, calls=%fused_computation.44 | loop fusion | flops 32 | bytes 192 | tf_op jit(solution)/shard_map/transpose | solution.py:250
  0.7 0.1 copy.5
  0.8 1.6 %bitcast_multiply_fusion = bf16[4,2,8,4096]{3,1,0,2:T(2,128)(2,1)S(1)} fusion(bf16[8,4,2,8192]{3,2,1,0:T(2,128)(2,1)} %param.3, s32[]{:T(128)S(6)} %select_n.44, bf16[4,8]{0,1:T(8,128)(2,1)S(1)} %copy.5), kind=kLoop, calls=%fused_computation.1 | loop fusion | flops 1048576 | bytes 1048644 | tf_op jit(solution)/shard_map/mul | solution.py:257
  2.4 0.0 copy-start
  2.4 0.3 copy.20
  2.7 0.1 broadcast_in_dim.27
  2.8 0.1 broadcast_in_dim.28
  2.9 0.0 copy-start.1
  2.9 0.7 %collective-permute-start.1 = (bf16[4,16,4224]{2,1,0:T(8,128)(2,1)S(1)}, bf16[4,16,4224]{2,1,0:T(8,128)(2,1)S(1)}, u32[]{:S(2)}, u32[]{:S(2)}) collective-permute-start(bf16[4,16,4224]{2,1,0:T(8,128)(2,1)S(1)} %pad_maximum_fusion), channel_id=1, source_target_pairs={{0,1},{1,0},{2,3},{3,2},{4,5},{5,4},{6,7},{7,6},{8,9},{9,8},{10,11... | collective-permute-start | bytes 1622024 | tf_op jit(solution)/shard_map/ppermute | solution.py:21
  3.7 0.0 copy-done
  3.7 0.3 bitcast_multiply_fusion.1
  4.0 0.2 copy.21
  4.2 1.3 %collective-permute-start.6 = (bf16[4,16,2176]{2,1,0:T(8,128)(2,1)S(1)}, bf16[4,16,2176]{2,1,0:T(8,128)(2,1)S(1)}, u32[]{:S(2)}, u32[]{:S(2)}) collective-permute-start(bf16[4,16,2176]{2,1,0:T(8,128)(2,1)S(1)} %pad_maximum_fusion.1.refs_1_.own_ref), channel_id=1, source_target_pairs={{0,2},{1,3},{2,0},{3,1},{4,6},{5,7},{6,4},{7,5},{8,10},{9,11},{10,... | collective-permute-start | bytes 835592 | tf_op jit(solution)/shard_map/ppermute | solution.py:21
  5.5 0.0 copy-done.1
  5.5 0.9 %collective-permute-start = (s32[2,2]{1,0:T(2,128)S(1)}, s32[2,2]{1,0:T(2,128)S(1)}, u32[]{:S(2)}, u32[]{:S(2)}) collective-permute-start(s32[2,2]{1,0:T(2,128)S(1)} %copy-done.1), channel_id=1, source_target_pairs={{0,1},{1,0},{2,3},{3,2},{4,5},{5,4},{6,7},{7,6},{8,9},{9,8},{10,11... | collective-permute-start | bytes 56 | tf_op jit(solution)/shard_map/ppermute | solution.py:21
  6.4 0.3 bitcast_multiply_fusion.2
  6.6 0.1 copy.23
  6.7 0.1 copy.22
  6.8 0.4 collective-permute-done
  7.2 0.0 collective-permute-done.1.refs_2_.par_ref
  7.3 0.3 collective-permute-start.7
  7.6 1.3 %collective-permute-start.4 = (bf16[2,4,16,1024]{3,2,1,0:T(8,128)(2,1)S(1)}, bf16[2,4,16,1024]{3,2,1,0:T(8,128)(2,1)S(1)}, u32[]{:S(2)}, u32[]{:S(2)}) collective-permute-start(bf16[2,4,16,1024]{3,2,1,0:T(8,128)(2,1)S(1)} %pad_maximum_fusion.3), channel_id=1, source_target_pairs={{0,2},{1,3},{2,0},{3,1},{4,6},{5,7},{6,4},{7,5},{8,10},{9,11},{10,... | collective-permute-start | bytes 786440 | tf_op jit(solution)/shard_map/ppermute | solution.py:21
  8.9 0.2 collective-permute-start.2
  9.2 0.1 pad_add_fusion.1.refs_0_.slots_ref
  9.2 2.6 %collective-permute-done.6.refs_3_.near_own = bf16[4,16,2176]{2,1,0:T(8,128)(2,1)S(1)} collective-permute-done((bf16[4,16,2176]{2,1,0:T(8,128)(2,1)S(1)}, bf16[4,16,2176]{2,1,0:T(8,128)(2,1)S(1)}, u32[]{:S(2)}, u32[]{:S(2)}) %collective-permute-start.6) | collective-permute-done | bytes 278560 | tf_op jit(solution)/shard_map/ppermute | solution.py:21
  11.8 3.2 %collective-permute-start.8 = (bf16[4,16,2176]{2,1,0:T(8,128)(2,1)S(1)}, bf16[4,16,2176]{2,1,0:T(8,128)(2,1)S(1)}, u32[]{:S(2)}, u32[]{:S(2)}) collective-permute-start(bf16[4,16,2176]{2,1,0:T(8,128)(2,1)S(1)} %collective-permute-done.6.refs_3_.near_own), channel_id=1, source_target_pairs={{0,4},{1,5},{4,8},{5,9},{6,2},{7,3},{8,12},{9,13},{10,6},{11,7},{1... | collective-permute-start | bytes 835592 | tf_op jit(solution)/shard_map/ppermute | solution.py:21
  15.0 2.8 %collective-permute-done.7.refs_4_.near_par = bf16[4,16,2176]{2,1,0:T(8,128)(2,1)S(1)} collective-permute-done((bf16[4,16,2176]{2,1,0:T(8,128)(2,1)S(1)}, bf16[4,16,2176]{2,1,0:T(8,128)(2,1)S(1)}, u32[]{:S(2)}, u32[]{:S(2)}) %collective-permute-start.7) | collective-permute-done | bytes 278560 | tf_op jit(solution)/shard_map/ppermute | solution.py:21
  17.8 3.2 %collective-permute-start.9 = (bf16[4,16,2176]{2,1,0:T(8,128)(2,1)S(1)}, bf16[4,16,2176]{2,1,0:T(8,128)(2,1)S(1)}, u32[]{:S(2)}, u32[]{:S(2)}) collective-permute-start(bf16[4,16,2176]{2,1,0:T(8,128)(2,1)S(1)} %collective-permute-done.7.refs_4_.near_par), channel_id=1, source_target_pairs={{0,4},{1,5},{4,8},{5,9},{6,2},{7,3},{8,12},{9,13},{10,6},{11,7},{1... | collective-permute-start | bytes 835592 | tf_op jit(solution)/shard_map/ppermute | solution.py:21
  21.0 2.4 %collective-permute-done.4.refs_3_ = bf16[2,4,16,1024]{3,2,1,0:T(8,128)(2,1)S(1)} collective-permute-done((bf16[2,4,16,1024]{3,2,1,0:T(8,128)(2,1)S(1)}, bf16[2,4,16,1024]{3,2,1,0:T(8,128)(2,1)S(1)}, u32[]{:S(2)}, u32[]{:S(2)}) %collective-permute-start.4) | collective-permute-done | bytes 262176 | tf_op jit(solution)/shard_map/ppermute | solution.py:21
  23.4 3.2 %collective-permute-start.5 = (bf16[2,4,16,1024]{3,2,1,0:T(8,128)(2,1)S(1)}, bf16[2,4,16,1024]{3,2,1,0:T(8,128)(2,1)S(1)}, u32[]{:S(2)}, u32[]{:S(2)}) collective-permute-start(bf16[2,4,16,1024]{3,2,1,0:T(8,128)(2,1)S(1)} %collective-permute-done.4.refs_3_), channel_id=1, source_target_pairs={{0,4},{1,5},{4,8},{5,9},{6,2},{7,3},{8,12},{9,13},{10,6},{11,7},{1... | collective-permute-start | bytes 786440 | tf_op jit(solution)/shard_map/ppermute | solution.py:21
  26.6 2.4 %collective-permute-done.2.refs_3_ = bf16[2,4,16,1024]{3,2,1,0:T(8,128)(2,1)S(1)} collective-permute-done((bf16[2,4,16,1024]{3,2,1,0:T(8,128)(2,1)S(1)}, bf16[2,4,16,1024]{3,2,1,0:T(8,128)(2,1)S(1)}, u32[]{:S(2)}, u32[]{:S(2)}) %collective-permute-start.2) | collective-permute-done | bytes 262176 | tf_op jit(solution)/shard_map/ppermute | solution.py:21
  29.0 3.2 %collective-permute-start.3 = (bf16[2,4,16,1024]{3,2,1,0:T(8,128)(2,1)S(1)}, bf16[2,4,16,1024]{3,2,1,0:T(8,128)(2,1)S(1)}, u32[]{:S(2)}, u32[]{:S(2)}) collective-permute-start(bf16[2,4,16,1024]{3,2,1,0:T(8,128)(2,1)S(1)} %collective-permute-done.2.refs_3_), channel_id=1, source_target_pairs={{0,4},{1,5},{4,8},{5,9},{6,2},{7,3},{8,12},{9,13},{10,6},{11,7},{1... | collective-permute-start | bytes 786440 | tf_op jit(solution)/shard_map/ppermute | solution.py:21
  32.2 1.1 %fusion.11 = (f32[64,512]{1,0:T(8,128)S(1)}, f32[64,512]{1,0:T(8,128)S(1)}, f32[64,512]{1,0:T(8,128)S(1)}, f32[64,512]{1,0:T(8,128)S(1)}) fusion(s32[512]{0:T(512)S(1)} %iota_add_fusion, s32[64]{0:T(128)S(1)} %multiply_add_fusion), kind=kLoop, calls=%fused_computation.35 | loop fusion | flops 917504 | bytes 526592 | tf_op jit(solution)/shard_map/sin | solution.py:28
  33.3 0.0 collective-permute-done.8.refs_5_.far_own
  33.3 0.0 collective-permute-done.9.refs_6_.far_par
  33.3 5.4 %shard_map.37.refs_9_ = f32[256,1152]{1,0:T(8,128)S(1)} custom-call(s32[4,3]{1,0:T(4,128)S(1)} %pad_add_fusion.1.refs_0_.slots_ref, bf16[4,16,2176]{2,1,0:T(8,128)(2,1)S(1)} %pad_maximum_fusion.1.refs_1_.own_ref, bf16[4,16,4224]{2,1,0:T(8,128)(2,1)S(1)} %collective-permute-done.1.refs_2_.par_ref, ...), custom_call_target="tpu_custom_call" | custom-call | flops 1073741824 | bytes 4194304 | tf_op jit(solution)/shard_map/pallas_call | solution.py:140
  38.7 0.0 collective-permute-done.5.refs_4_
  38.7 3.2 %shard_map.38.refs_9_ = f32[256,1152]{1,0:T(8,128)S(1)} custom-call(s32[4,3]{1,0:T(4,128)S(1)} %pad_add_fusion.1.refs_0_.slots_ref, bf16[4,16,1024]{2,1,0:T(8,128)(2,1)S(1)} %bitcast.34, bf16[4,16,4224]{2,1,0:T(8,128)(2,1)S(1)} %collective-permute-done.1.refs_2_.par_ref, ...), custom_call_target="tpu_custom_call", output_to_operand_aliasing={{}: (9, {})} | custom-call | flops 536870912 | bytes 2097152 | tf_op jit(solution)/shard_map/pallas_call | solution.py:140
  41.9 0.0 collective-permute-done.3.refs_4_
  42.0 3.1 %shard_map.39 = (f32[128,1152]{1,0:T(8,128)S(1)}, f32[128,1152]{1,0:T(8,128)S(1)}) custom-call(s32[4,3]{1,0:T(4,128)S(1)} %pad_add_fusion.1.refs_0_.slots_ref, bf16[4,16,1024]{2,1,0:T(8,128)(2,1)S(1)} %bitcast.32, bf16[4,16,4224]{2,1,0:T(8,128)(2,1)S(1)} %collective-permute-done.1.refs_2_.par_ref, ...), custom_call_target="tpu_custom_call" | custom-call | flops 536870912 | bytes 2097152 | tf_op jit(solution)/shard_map/pallas_call | solution.py:140
  45.1 1.8 %collective-permute-start.10 = (f32[128,1152]{1,0:T(8,128)S(1)}, f32[128,1152]{1,0:T(8,128)S(1)}, u32[]{:S(2)}, u32[]{:S(2)}) collective-permute-start(f32[128,1152]{1,0:T(8,128)S(1)} %get-tuple-element.12), channel_id=1, source_target_pairs={{0,1},{1,0},{2,3},{3,2},{4,5},{5,4},{6,7},{7,6},{8,9},{9,8},{10,11... | collective-permute-start | bytes 1769480 | tf_op jit(solution)/shard_map/ppermute | solution.py:21
  46.9 1.6 %collective-permute-done.10.other_ref = f32[128,1152]{1,0:T(8,128)S(1)} collective-permute-done((f32[128,1152]{1,0:T(8,128)S(1)}, f32[128,1152]{1,0:T(8,128)S(1)}, u32[]{:S(2)}, u32[]{:S(2)}) %collective-permute-start.10) | collective-permute-done | bytes 589856 | tf_op jit(solution)/shard_map/ppermute | solution.py:21
  48.6 1.6 %finish.1 = bf16[128,1024]{1,0:T(8,128)(2,1)} custom-call(s32[4,3]{1,0:T(4,128)S(1)} %pad_add_fusion.1.refs_0_.slots_ref, f32[128,1152]{1,0:T(8,128)S(1)} %get-tuple-element.11.mine_ref, f32[128,1152]{1,0:T(8,128)S(1)} %collective-permute-done.10.other_ref, bf16[4,16,2176]{2,1,0:T(8,128)(2,1)S(1)} %pad_maximum_fusion.1.refs_1_.own_ref, ...), custom_call_target="tpu_custom_call" | custom-call | flops 524288 | bytes 1310720 | tf_op jit(solution)/shard_map/finish/pallas_call | solution.py:218
  (11 shorter events, 0.2 us)
Async XLA Ops:
  2.4 1.3 %copy-start = (bf16[8,4,2,8192]{3,2,1,0:T(2,128)(2,1)S(1)}, bf16[8,4,2,8192]{3,2,1,0:T(2,128)(2,1)}, u32[]{:S(2)}) copy-start(bf16[8,4,2,8192]{3,2,1,0:T(2,128)(2,1)} %param.3) | copy-start | bytes 3145732
  2.9 2.6 %copy-start.1 = (s32[2,2]{1,0:T(2,128)S(1)}, s32[2,2]{1,0:T(2,128)}, u32[]{:S(2)}) copy-start(s32[2,2]{1,0:T(2,128)} %param.5) | copy-start | bytes 52
  2.9 4.3 %collective-permute-start.1 = (bf16[4,16,4224]{2,1,0:T(8,128)(2,1)S(1)}, bf16[4,16,4224]{2,1,0:T(8,128)(2,1)S(1)}, u32[]{:S(2)}, u32[]{:S(2)}) collective-permute-start(bf16[4,16,4224]{2,1,0:T(8,128)(2,1)S(1)} %pad_maximum_fusion), channel_id=1, source_target_pairs={{0,1},{1,0},{2,3},{3,2},{4,5},{5,4},{6,7},{7,6},{8,9},{9,8},{10,11... | collective-permute-start | bytes 1622024 | tf_op jit(solution)/shard_map/ppermute | solution.py:21
  4.2 7.7 %collective-permute-start.6 = (bf16[4,16,2176]{2,1,0:T(8,128)(2,1)S(1)}, bf16[4,16,2176]{2,1,0:T(8,128)(2,1)S(1)}, u32[]{:S(2)}, u32[]{:S(2)}) collective-permute-start(bf16[4,16,2176]{2,1,0:T(8,128)(2,1)S(1)} %pad_maximum_fusion.1.refs_1_.own_ref), channel_id=1, source_target_pairs={{0,2},{1,3},{2,0},{3,1},{4,6},{5,7},{6,4},{7,5},{8,10},{9,11},{10,... | collective-permute-start | bytes 835592 | tf_op jit(solution)/shard_map/ppermute | solution.py:21
  5.5 1.7 %collective-permute-start = (s32[2,2]{1,0:T(2,128)S(1)}, s32[2,2]{1,0:T(2,128)S(1)}, u32[]{:S(2)}, u32[]{:S(2)}) collective-permute-start(s32[2,2]{1,0:T(2,128)S(1)} %copy-done.1), channel_id=1, source_target_pairs={{0,1},{1,0},{2,3},{3,2},{4,5},{5,4},{6,7},{7,6},{8,9},{9,8},{10,11... | collective-permute-start | bytes 56 | tf_op jit(solution)/shard_map/ppermute | solution.py:21
  7.3 10.5 %collective-permute-start.7 = (bf16[4,16,2176]{2,1,0:T(8,128)(2,1)S(1)}, bf16[4,16,2176]{2,1,0:T(8,128)(2,1)S(1)}, u32[]{:S(2)}, u32[]{:S(2)}) collective-permute-start(bf16[4,16,2176]{2,1,0:T(8,128)(2,1)S(1)} %slice.18), channel_id=1, source_target_pairs={{0,2},{1,3},{2,0},{3,1},{4,6},{5,7},{6,4},{7,5},{8,10},{9,11},{10,... | collective-permute-start | bytes 835592 | tf_op jit(solution)/shard_map/ppermute | solution.py:21
  7.6 15.8 %collective-permute-start.4 = (bf16[2,4,16,1024]{3,2,1,0:T(8,128)(2,1)S(1)}, bf16[2,4,16,1024]{3,2,1,0:T(8,128)(2,1)S(1)}, u32[]{:S(2)}, u32[]{:S(2)}) collective-permute-start(bf16[2,4,16,1024]{3,2,1,0:T(8,128)(2,1)S(1)} %pad_maximum_fusion.3), channel_id=1, source_target_pairs={{0,2},{1,3},{2,0},{3,1},{4,6},{5,7},{6,4},{7,5},{8,10},{9,11},{10,... | collective-permute-start | bytes 786440 | tf_op jit(solution)/shard_map/ppermute | solution.py:21
  8.9 20.1 %collective-permute-start.2 = (bf16[2,4,16,1024]{3,2,1,0:T(8,128)(2,1)S(1)}, bf16[2,4,16,1024]{3,2,1,0:T(8,128)(2,1)S(1)}, u32[]{:S(2)}, u32[]{:S(2)}) collective-permute-start(bf16[2,4,16,1024]{3,2,1,0:T(8,128)(2,1)S(1)} %pad_maximum_fusion.2), channel_id=1, source_target_pairs={{0,2},{1,3},{2,0},{3,1},{4,6},{5,7},{6,4},{7,5},{8,10},{9,11},{10,... | collective-permute-start | bytes 786440 | tf_op jit(solution)/shard_map/ppermute | solution.py:21
  11.8 21.5 %collective-permute-start.8 = (bf16[4,16,2176]{2,1,0:T(8,128)(2,1)S(1)}, bf16[4,16,2176]{2,1,0:T(8,128)(2,1)S(1)}, u32[]{:S(2)}, u32[]{:S(2)}) collective-permute-start(bf16[4,16,2176]{2,1,0:T(8,128)(2,1)S(1)} %collective-permute-done.6.refs_3_.near_own), channel_id=1, source_target_pairs={{0,4},{1,5},{4,8},{5,9},{6,2},{7,3},{8,12},{9,13},{10,6},{11,7},{1... | collective-permute-start | bytes 835592 | tf_op jit(solution)/shard_map/ppermute | solution.py:21
  17.8 15.5 %collective-permute-start.9 = (bf16[4,16,2176]{2,1,0:T(8,128)(2,1)S(1)}, bf16[4,16,2176]{2,1,0:T(8,128)(2,1)S(1)}, u32[]{:S(2)}, u32[]{:S(2)}) collective-permute-start(bf16[4,16,2176]{2,1,0:T(8,128)(2,1)S(1)} %collective-permute-done.7.refs_4_.near_par), channel_id=1, source_target_pairs={{0,4},{1,5},{4,8},{5,9},{6,2},{7,3},{8,12},{9,13},{10,6},{11,7},{1... | collective-permute-start | bytes 835592 | tf_op jit(solution)/shard_map/ppermute | solution.py:21
  23.4 15.3 %collective-permute-start.5 = (bf16[2,4,16,1024]{3,2,1,0:T(8,128)(2,1)S(1)}, bf16[2,4,16,1024]{3,2,1,0:T(8,128)(2,1)S(1)}, u32[]{:S(2)}, u32[]{:S(2)}) collective-permute-start(bf16[2,4,16,1024]{3,2,1,0:T(8,128)(2,1)S(1)} %collective-permute-done.4.refs_3_), channel_id=1, source_target_pairs={{0,4},{1,5},{4,8},{5,9},{6,2},{7,3},{8,12},{9,13},{10,6},{11,7},{1... | collective-permute-start | bytes 786440 | tf_op jit(solution)/shard_map/ppermute | solution.py:21
  29.0 12.9 %collective-permute-start.3 = (bf16[2,4,16,1024]{3,2,1,0:T(8,128)(2,1)S(1)}, bf16[2,4,16,1024]{3,2,1,0:T(8,128)(2,1)S(1)}, u32[]{:S(2)}, u32[]{:S(2)}) collective-permute-start(bf16[2,4,16,1024]{3,2,1,0:T(8,128)(2,1)S(1)} %collective-permute-done.2.refs_3_), channel_id=1, source_target_pairs={{0,4},{1,5},{4,8},{5,9},{6,2},{7,3},{8,12},{9,13},{10,6},{11,7},{1... | collective-permute-start | bytes 786440 | tf_op jit(solution)/shard_map/ppermute | solution.py:21
  45.1 3.5 %collective-permute-start.10 = (f32[128,1152]{1,0:T(8,128)S(1)}, f32[128,1152]{1,0:T(8,128)S(1)}, u32[]{:S(2)}, u32[]{:S(2)}) collective-permute-start(f32[128,1152]{1,0:T(8,128)S(1)} %get-tuple-element.12), channel_id=1, source_target_pairs={{0,1},{1,0},{2,3},{3,2},{4,5},{5,4},{6,7},{7,6},{8,9},{9,8},{10,11... | collective-permute-start | bytes 1769480 | tf_op jit(solution)/shard_map/ppermute | solution.py:21

commit v2 on v1

v2 whole, which is shorter than its diff:
```python
import functools
import math

import jax
import jax.numpy as jnp
from jax import lax
from jax.experimental import pallas as pl
from jax.experimental.pallas import tpu as pltpu
from jax.sharding import PartitionSpec as P


LAGS = 1024
CUTS = (0, 8, 12, 16)
SUB = 512
FINE = 64
LANES = 128
GRANT = 24 << 20


def permute(array, pairs):
    return lax.ppermute(array, "sta", pairs)


def angle_tables(index, lag_half, frequency_values):
    lag_index = jnp.arange(1, lag_half + 1, dtype=jnp.int32)
    phase_index = jnp.mod(index[:, None] * lag_index[None, :], 2 * frequency_values)
    phase_angle = phase_index.astype(jnp.float32) * (math.pi / frequency_values)
    return jnp.cos(phase_angle), jnp.sin(phase_angle)


def table_kernel(fine_cos, fine_sin, coarse_cos, coarse_sin, cos_ref, sin_ref):
    fc = fine_cos[...]
    fs = fine_sin[...]

    def one_group(group, carry):
        cc = coarse_cos[pl.ds(group, 1), :]
        cs = coarse_sin[pl.ds(group, 1), :]
        at = pl.ds(pl.multiple_of(group * FINE, FINE), FINE)
        cos_ref[at, :] = (cc * fc - cs * fs).astype(jnp.bfloat16)
        sin_ref[at, :] = (cs * fc + cc * fs).astype(jnp.bfloat16)
        return carry

    lax.fori_loop(0, cos_ref.shape[0] // FINE, one_group, 0)


def lag_tables(fine, coarse):
    count = coarse[0].shape[0] * FINE
    lag_half = fine[0].shape[1]
    vmem = pl.BlockSpec(memory_space=pltpu.VMEM)
    table = jax.ShapeDtypeStruct((count, lag_half), jnp.bfloat16)
    return pl.pallas_call(
        table_kernel,
        in_specs=[vmem] * 4,
        out_specs=[vmem] * 2,
        out_shape=[table, table],
        compiler_params=pltpu.CompilerParams(vmem_limit_bytes=GRANT),
        cost_estimate=pl.CostEstimate(
            flops=6 * count * lag_half, bytes_accessed=4 * count * lag_half, transcendentals=0
        ),
        name="tables",
    )(*fine, *coarse)


def pair_weights(slots_ref, sources, marks, weight_ref, slot_count, windows, stations, norm):
    pairs = stations * stations
    for at, view in enumerate(sources):
        for window in range(windows):
            marks[at, window] = view[window, :, :LANES].astype(jnp.float32)[:stations]
    for slot in range(slot_count):
        first_at = slots_ref[slot, 0]
        second_at = slots_ref[slot, 1]
        live = slots_ref[slot, 2].astype(jnp.float32)
        for station in range(stations):
            count = None
            for window in range(windows):
                term = marks[first_at, window, pl.ds(station, 1), :] * marks[second_at, window]
                count = term if count is None else count + term
            rows = pl.ds(slot * pairs + station * stations, stations)
            weight_ref[rows, :] = live / (norm * jnp.maximum(count, 1.0))


def flip_matrix(size):
    rows_at = lax.broadcasted_iota(jnp.int32, (size, size), 0)
    lanes_at = lax.broadcasted_iota(jnp.int32, (size, size), 1)
    return (rows_at + lanes_at == size - 1).astype(jnp.bfloat16)


def lay_out(acc_ref, weight_ref, out_ref, start):
    rows = out_ref.shape[0]
    lag_half = out_ref.shape[1] // 2
    size = 256
    flip = flip_matrix(size)
    at = pl.ds(start, rows)
    even = acc_ref[at, :lag_half]
    odd = acc_ref[at, lag_half : 2 * lag_half]
    weight = weight_ref[at, :][:, :1]
    still = jnp.sum(acc_ref[at, 2 * lag_half :], axis=1, keepdims=True)
    lane = lax.broadcasted_iota(jnp.int32, (rows, lag_half), 1)
    right = jnp.where(lane == 0, still, pltpu.roll(even - odd, 1, 1))
    out_ref[:, lag_half:] = (right * weight).astype(out_ref.dtype)
    left = (even + odd) * weight
    parts = [left.astype(jnp.bfloat16)]
    if out_ref.dtype == jnp.float32:
        parts.append((left - parts[0].astype(jnp.float32)).astype(jnp.bfloat16))
    for lane in range(0, lag_half, size):
        flipped = sum(
            jnp.dot(part[:, lane : lane + size], flip, preferred_element_type=jnp.float32)
            for part in parts
        )
        out_ref[:, lag_half - lane - size : lag_half - lane] = flipped.astype(out_ref.dtype)


def chunk_kernel(*refs, views_at, slot_count, windows, stations, first, last, low, norm):
    refs = list(refs)
    slots_ref = refs.pop(0)
    sources = [refs.pop(0) for _ in range(1 + max(which for which, _, _ in views_at))]
    cos_ref, sin_ref = (refs.pop(0) for _ in range(2))
    if not first:
        before_ref = refs.pop(0)
    if last:
        weight_ref, mine_ref, theirs_ref = (refs.pop(0) for _ in range(3))
        acc_ref = refs.pop()
    else:
        acc_ref = refs.pop(0)
    if first:
        weight_ref = refs.pop(0)
        marks = refs.pop()
    stage = refs.pop(0)
    buffers = [(refs[0], refs[1]), (refs[2], refs[3])]
    count = stage.shape[-1]
    lag_half = cos_ref.shape[1]
    pairs = stations * stations
    width = buffers[0][0].shape[1]
    wide = 256

    if first:
        pair_weights(slots_ref, sources, marks, weight_ref, slot_count, windows, stations, norm)
        acc_ref[:, 2 * lag_half :] = jnp.zeros((slot_count * pairs, LANES), jnp.float32)
    else:
        acc_ref[:, 2 * lag_half :] = before_ref[:, 2 * lag_half :]

    for at, (which, part, lane) in enumerate(views_at):
        view = sources[which] if part is None else sources[which].at[part]
        for window in range(windows):
            stage[at, window] = view[window, :, lane : lane + count].astype(jnp.float32)

    index = [(slots_ref[slot, 0], slots_ref[slot, 1]) for slot in range(slot_count)]

    def cross(start, real_rows, imag_rows):
        for slot in range(slot_count):
            first_at, second_at = index[slot]
            for tile in range(width // wide):
                lanes = pl.ds(start + tile * wide, wide)
                held = pl.ds(tile * wide, wide)
                second = [
                    [
                        stage[second_at, window, pl.ds(part * stations, stations), lanes]
                        for part in range(2)
                    ]
                    for window in range(windows)
                ]
                for couple in range(0, stations, 2):
                    real_out = []
                    imag_out = []
                    for station in (couple, couple + 1):
                        real = imag = None
                        for window in range(windows):
                            xr = stage[first_at, window, pl.ds(station, 1), lanes]
                            xi = stage[first_at, window, pl.ds(stations + station, 1), lanes]
                            yr, yi = second[window]
                            r = xr * yr + xi * yi
                            i = xi * yr - xr * yi
                            real = r if real is None else real + r
                            imag = i if imag is None else imag + i
                        real_out.append(real)
                        imag_out.append(imag)
                    at = pl.ds(slot * pairs + couple * stations, 2 * stations)
                    real = jnp.concatenate(real_out, axis=0)
                    imag = jnp.concatenate(imag_out, axis=0)
                    real_rows[at, held] = real.astype(jnp.bfloat16)
                    imag_rows[at, held] = imag.astype(jnp.bfloat16)
                    total = real[:, :LANES]
                    for lane in range(LANES, wide, LANES):
                        total = total + real[:, lane : lane + LANES]
                    acc_ref[at, pl.ds(2 * lag_half, LANES)] += total

    def gather_lags(start, real_rows, imag_rows):
        at = pl.ds(low + start, width)
        for lane, rows, table in ((0, real_rows, cos_ref), (lag_half, imag_rows, sin_ref)):
            lanes = slice(lane, lane + lag_half)
            value = jnp.dot(rows[...], table[at, :], preferred_element_type=jnp.float32)
            if start > 0:
                value = value + acc_ref[:, lanes]
            elif not first:
                value = value + before_ref[:, lanes]
            acc_ref[:, lanes] = value

    steps = count // width
    for step in range(steps):
        cross(step * width, *buffers[step % 2])
        if step > 0:
            gather_lags((step - 1) * width, *buffers[(step - 1) % 2])
    gather_lags((steps - 1) * width, *buffers[(steps - 1) % 2])
    if last:
        half = slot_count * pairs // 2
        lay_out(acc_ref, weight_ref, theirs_ref, half)
        mine_ref[...] = acc_ref[:half, :]


def chunk_call(slots, sources, views_at, tables, before, weights, last, low, count, width, windows, stations, norm):
    slot_count = slots.shape[0]
    lag_half = tables[0].shape[1]
    rows = slot_count * stations * stations
    first = before is None
    acc = jax.ShapeDtypeStruct((rows, 2 * lag_half + LANES), jnp.float32)
    operands = list(sources) + list(tables)
    if not first:
        operands.append(before)
    if last:
        operands.append(weights)
    vmem = pl.BlockSpec(memory_space=pltpu.VMEM)
    scratch = [pltpu.VMEM((6, windows, 2 * stations, count), jnp.float32)]
    scratch += [pltpu.VMEM((rows, width), jnp.bfloat16)] * 4
    outs = [acc]
    if first:
        outs.append(jax.ShapeDtypeStruct((rows, LANES), jnp.float32))
        scratch.append(pltpu.VMEM((6, windows, stations, LANES), jnp.float32))
    if last:
        outs = [
            jax.ShapeDtypeStruct((rows // 2, 2 * lag_half + LANES), jnp.float32),
            jax.ShapeDtypeStruct((rows // 2, 2 * lag_half), jnp.bfloat16),
        ]
        scratch.append(pltpu.VMEM(acc.shape, jnp.float32))
    return pl.pallas_call(
        functools.partial(
            chunk_kernel,
            views_at=views_at,
            slot_count=slot_count,
            windows=windows,
            stations=stations,
            first=first,
            last=last,
            low=low,
            norm=norm,
        ),
        in_specs=[pl.BlockSpec(memory_space=pltpu.SMEM)] + [vmem] * len(operands),
        out_specs=[vmem] * len(outs),
        scratch_shapes=scratch,
        out_shape=outs,
        input_output_aliases={} if first or last else {len(operands): 0},
        cost_estimate=pl.CostEstimate(
            flops=4 * rows * count * lag_half, bytes_accessed=4 * count * lag_half, transcendentals=0
        ),
        compiler_params=pltpu.CompilerParams(vmem_limit_bytes=GRANT),
    )(slots, *operands)


def mine_kernel(acc_ref, weight_ref, out_ref):
    lay_out(acc_ref, weight_ref, out_ref, 0)


def mine_call(mine, weights):
    rows = mine.shape[0]
    lag_count = mine.shape[1] - LANES
    vmem = pl.BlockSpec(memory_space=pltpu.VMEM)
    return pl.pallas_call(
        mine_kernel,
        in_specs=[vmem] * 2,
        out_specs=vmem,
        out_shape=jax.ShapeDtypeStruct((rows, lag_count), jnp.float32),
        compiler_params=pltpu.CompilerParams(vmem_limit_bytes=GRANT),
        cost_estimate=pl.CostEstimate(
            flops=2 * rows * lag_count * 256, bytes_accessed=8 * rows * lag_count, transcendentals=0
        ),
        name="mine",
    )(mine, weights)


def owner_stacks(spectra, window_mask, pair_slots):
    stations, windows, _, frequency_values = spectra.shape
    slot_count = pair_slots.shape[0]
    half = frequency_values // 2
    lag_half = LAGS // 2
    peers = lax.axis_size("sta")
    me = lax.axis_index("sta")
    core = me & 1
    chip = me >> 1
    core_pairs = [(i, i ^ 1) for i in range(peers)]
    near_pairs = [(i, i ^ 2) for i in range(peers)]
    far_pairs = [(i, (i + 4 - 8 * ((i // 2) % 2)) % peers) for i in range(peers)]
    valid = window_mask.astype(jnp.bfloat16).T[:, None, :, None]
    mark = jnp.broadcast_to(valid, (windows, 2, stations, LANES)).reshape(
        windows, 2 * stations, LANES
    )

    def rows_of(start, size):
        piece = lax.dynamic_slice_in_dim(spectra, start, size, 3)
        return (piece.transpose(1, 2, 0, 3) * valid).reshape(windows, 2 * stations, size)

    splits = [half * cut // 16 for cut in CUTS]
    lead = splits[1]
    own_lead = jnp.concatenate([mark, rows_of(core * half, lead)], axis=2)
    sent = jnp.concatenate([mark, rows_of((1 - core) * half, half)], axis=2)
    par = permute(sent, core_pairs)
    other_slots = permute(pair_slots, core_pairs)
    near = [permute(own_lead, near_pairs), permute(par[:, :, : LANES + lead], near_pairs)]
    own = []
    for at in range(1, len(splits) - 1):
        low, high = splits[at], splits[at + 1]
        own.append(rows_of(core * half + low, high - low))
        piece = jnp.stack([own[-1], par[:, :, LANES + low : LANES + high]])
        if high == half:
            piece, base = lax.optimization_barrier((piece, core * half))
        near.append(permute(piece, near_pairs))
    far = [permute(piece, far_pairs) for piece in near]

    fine = angle_tables(jnp.arange(FINE, dtype=jnp.int32), lag_half, frequency_values)
    coarse = angle_tables(
        base + FINE * jnp.arange(half // FINE, dtype=jnp.int32), lag_half, frequency_values
    )
    slots = jnp.concatenate([pair_slots, other_slots], axis=0)
    slot_chip = slots >> 1
    group = jnp.where(slot_chip == chip, 0, jnp.where(slot_chip == (chip ^ 1), 1, 2))
    other_core = ((slots & 1) != core).astype(jnp.int32)
    live = (slots[:, :1] >= 0).astype(jnp.int32)
    table = jnp.concatenate([group * 2 + other_core, live], axis=1)
    tables = lag_tables(fine, coarse)
    norm = math.sqrt(frequency_values)
    acc = weights = None
    for at in range(len(splits) - 1):
        low, high = splits[at], splits[at + 1]
        last = at == len(splits) - 2
        if at == 0:
            sources = [own_lead, par, near[0], near[1], far[0], far[1]]
            views_at = [(which, None, LANES) for which in range(6)]
        else:
            sources = [own[at - 1], par, near[at + 1], far[at + 1]]
            views_at = [(0, None, 0), (1, None, LANES + low), (2, 0, 0), (2, 1, 0), (3, 0, 0), (3, 1, 0)]
        width = min(SUB, (high - low) // 2)
        made = chunk_call(
            table, sources, views_at, tables, acc, weights, last, low, high - low, width, windows, stations, norm
        )
        if at == 0:
            acc, weights = made
        elif not last:
            (acc,) = made
        else:
            mine, theirs = made
    other = permute(theirs, core_pairs)
    out = (mine_call(mine, weights) + other.astype(jnp.float32)).astype(jnp.bfloat16)
    return out.reshape(slot_count, stations, stations, LAGS)


def solution(mesh):
    placed = (P(("day", "sta"), None, None, None), P(("day", "sta"), None), P("sta", None))
    return jax.shard_map(
        owner_stacks,
        mesh=mesh,
        in_specs=placed,
        out_specs=P(("day", "sta"), None, None, None),
        check_vma=False,
    )
```

time: 50.5 us -> 47.6 us (0.943)
  the two profiles are of different devices: /device:TPU:17 before, /device:TPU:5 now
where the time goes in v2:
time: 47.6 us; the launch traced here: 47.4 us
  starting transfers between devices  19.9 us (42%)
  waiting for transfers between devices  11 us (23%)
  Pallas kernels  10.5 us (22%)
  other arithmetic  4.87 us (10%)
  local copies, waits for them, and re-layouts  0.92 us (2%)
    ppermute x11, starting transfers between devices, permute(): return lax.ppermute(array, 'sta', pairs)  19.9 us
    ppermute x11, waiting for transfers between devices, permute(): return lax.ppermute(array, 'sta', pairs)  11 us
    pallas_call x3, Pallas kernels, chunk_call(): pl.pallas_call(functools.partial(chunk_kernel, views_at=views_at, slot_co...  7.96 us
    pallas_call x1, Pallas kernels, lag_tables(): pl.pallas_call(table_kernel, in_specs=[vmem] * 4, out_specs=[vmem] * 2, o...  2.24 us
    mul x3, other arithmetic, rows_of(): piece.transpose(1, 2, 0, 3) * valid  2.15 us
    sin x1, other arithmetic, angle_tables(): return (jnp.cos(phase_angle), jnp.sin(phase_angle))  1.06 us
  transfers between devices with their start and end apart: 11, of which 6 were waited for; matrix products, arithmetic and copies ran while one was open for 4% of the time, Pallas kernels for 17%

profile of v2, /device:TPU:5, one launch (start us, length us, event | category | flops | bytes accessed | tf_op | source)
XLA Modules:
  0.0 47.4 jit_solution(16325546792928062036)
XLA Ops:
  0.0 0.7 %convert_bitcast_fusion = bf16[4,8]{1,0:T(4,128)(2,1)S(1)} fusion(s32[8,4]{0,1:T(4,128)} %param.4), kind=kLoop, calls=%fused_computation.45 | loop fusion | flops 32 | bytes 192 | tf_op jit(solution)/shard_map/transpose | solution.py:291
  0.7 0.1 copy.5
  0.8 1.6 %bitcast_multiply_fusion = bf16[4,2,8,4096]{3,1,0,2:T(2,128)(2,1)S(1)} fusion(bf16[8,4,2,8192]{3,2,1,0:T(2,128)(2,1)} %param.3, s32[]{:T(128)S(6)} %select_n.36, bf16[4,8]{0,1:T(8,128)(2,1)S(1)} %copy.5), kind=kLoop, calls=%fused_computation.1 | loop fusion | flops 1048576 | bytes 1048644 | tf_op jit(solution)/shard_map/mul | solution.py:298
  2.4 0.0 copy-start
  2.4 0.3 copy.20
  2.7 0.1 broadcast_in_dim.27
  2.8 0.1 broadcast_in_dim.28
  2.9 0.0 copy-start.1
  2.9 0.7 %collective-permute-start.1 = (bf16[4,16,4224]{2,1,0:T(8,128)(2,1)S(1)}, bf16[4,16,4224]{2,1,0:T(8,128)(2,1)S(1)}, u32[]{:S(2)}, u32[]{:S(2)}) collective-permute-start(bf16[4,16,4224]{2,1,0:T(8,128)(2,1)S(1)} %pad_maximum_fusion), channel_id=1, source_target_pairs={{0,1},{1,0},{2,3},{3,2},{4,5},{5,4},{6,7},{7,6},{8,9},{9,8},{10,11... | collective-permute-start | bytes 1622024 | tf_op jit(solution)/shard_map/ppermute | solution.py:21
  3.7 0.0 copy-done
  3.7 0.3 bitcast_multiply_fusion.1
  4.0 0.2 copy.21
  4.2 0.1 collective-permute-start.6
  4.2 0.0 copy-done.1
  4.2 0.7 %collective-permute-start = (s32[2,2]{1,0:T(2,128)S(1)}, s32[2,2]{1,0:T(2,128)S(1)}, u32[]{:S(2)}, u32[]{:S(2)}) collective-permute-start(s32[2,2]{1,0:T(2,128)S(1)} %copy-done.1), channel_id=1, source_target_pairs={{0,1},{1,0},{2,3},{3,2},{4,5},{5,4},{6,7},{7,6},{8,9},{9,8},{10,11... | collective-permute-start | bytes 56 | tf_op jit(solution)/shard_map/ppermute | solution.py:21
  4.9 0.3 bitcast_multiply_fusion.2
  5.2 0.1 copy.23
  5.3 0.1 copy.22
  5.4 0.4 collective-permute-done
  5.8 0.0 collective-permute-done.1.refs_2_
  5.9 1.7 %collective-permute-start.7 = (bf16[4,16,2176]{2,1,0:T(8,128)(2,1)S(1)}, bf16[4,16,2176]{2,1,0:T(8,128)(2,1)S(1)}, u32[]{:S(2)}, u32[]{:S(2)}) collective-permute-start(bf16[4,16,2176]{2,1,0:T(8,128)(2,1)S(1)} %slice.18), channel_id=1, source_target_pairs={{0,2},{1,3},{2,0},{3,1},{4,6},{5,7},{6,4},{7,5},{8,10},{9,11},{10,... | collective-permute-start | bytes 835592 | tf_op jit(solution)/shard_map/ppermute | solution.py:21
  7.6 0.1 collective-permute-start.4
  7.7 1.4 %collective-permute-start.2 = (bf16[2,4,16,1024]{3,2,1,0:T(8,128)(2,1)S(1)}, bf16[2,4,16,1024]{3,2,1,0:T(8,128)(2,1)S(1)}, u32[]{:S(2)}, u32[]{:S(2)}) collective-permute-start(bf16[2,4,16,1024]{3,2,1,0:T(8,128)(2,1)S(1)} %pad_maximum_fusion.2), channel_id=1, source_target_pairs={{0,2},{1,3},{2,0},{3,1},{4,6},{5,7},{6,4},{7,5},{8,10},{9,11},{10,... | collective-permute-start | bytes 786440 | tf_op jit(solution)/shard_map/ppermute | solution.py:21
  9.2 0.1 pad_add_fusion.1.refs_0_
  9.2 2.6 %collective-permute-done.6.refs_3_ = bf16[4,16,2176]{2,1,0:T(8,128)(2,1)S(1)} collective-permute-done((bf16[4,16,2176]{2,1,0:T(8,128)(2,1)S(1)}, bf16[4,16,2176]{2,1,0:T(8,128)(2,1)S(1)}, u32[]{:S(2)}, u32[]{:S(2)}) %collective-permute-start.6) | collective-permute-done | bytes 278560 | tf_op jit(solution)/shard_map/ppermute | solution.py:21
  11.8 3.3 %collective-permute-start.8 = (bf16[4,16,2176]{2,1,0:T(8,128)(2,1)S(1)}, bf16[4,16,2176]{2,1,0:T(8,128)(2,1)S(1)}, u32[]{:S(2)}, u32[]{:S(2)}) collective-permute-start(bf16[4,16,2176]{2,1,0:T(8,128)(2,1)S(1)} %collective-permute-done.6.refs_3_), channel_id=1, source_target_pairs={{0,4},{1,5},{2,14},{3,15},{4,8},{5,9},{6,2},{7,3},{8,12},{9,13},{1... | collective-permute-start | bytes 835592 | tf_op jit(solution)/shard_map/ppermute | solution.py:21
  15.1 2.6 %collective-permute-done.7.refs_4_ = bf16[4,16,2176]{2,1,0:T(8,128)(2,1)S(1)} collective-permute-done((bf16[4,16,2176]{2,1,0:T(8,128)(2,1)S(1)}, bf16[4,16,2176]{2,1,0:T(8,128)(2,1)S(1)}, u32[]{:S(2)}, u32[]{:S(2)}) %collective-permute-start.7) | collective-permute-done | bytes 278560 | tf_op jit(solution)/shard_map/ppermute | solution.py:21
  17.8 3.3 %collective-permute-start.9 = (bf16[4,16,2176]{2,1,0:T(8,128)(2,1)S(1)}, bf16[4,16,2176]{2,1,0:T(8,128)(2,1)S(1)}, u32[]{:S(2)}, u32[]{:S(2)}) collective-permute-start(bf16[4,16,2176]{2,1,0:T(8,128)(2,1)S(1)} %collective-permute-done.7.refs_4_), channel_id=1, source_target_pairs={{0,4},{1,5},{2,14},{3,15},{4,8},{5,9},{6,2},{7,3},{8,12},{9,13},{1... | collective-permute-start | bytes 835592 | tf_op jit(solution)/shard_map/ppermute | solution.py:21
  21.1 2.3 %collective-permute-done.4.refs_3_ = bf16[2,4,16,1024]{3,2,1,0:T(8,128)(2,1)S(1)} collective-permute-done((bf16[2,4,16,1024]{3,2,1,0:T(8,128)(2,1)S(1)}, bf16[2,4,16,1024]{3,2,1,0:T(8,128)(2,1)S(1)}, u32[]{:S(2)}, u32[]{:S(2)}) %collective-permute-start.4) | collective-permute-done | bytes 262176 | tf_op jit(solution)/shard_map/ppermute | solution.py:21
  23.4 3.3 %collective-permute-start.5 = (bf16[2,4,16,1024]{3,2,1,0:T(8,128)(2,1)S(1)}, bf16[2,4,16,1024]{3,2,1,0:T(8,128)(2,1)S(1)}, u32[]{:S(2)}, u32[]{:S(2)}) collective-permute-start(bf16[2,4,16,1024]{3,2,1,0:T(8,128)(2,1)S(1)} %collective-permute-done.4.refs_3_), channel_id=1, source_target_pairs={{0,4},{1,5},{2,14},{3,15},{4,8},{5,9},{6,2},{7,3},{8,12},{9,13},{1... | collective-permute-start | bytes 786440 | tf_op jit(solution)/shard_map/ppermute | solution.py:21
  26.7 2.3 %collective-permute-done.2.refs_3_ = bf16[2,4,16,1024]{3,2,1,0:T(8,128)(2,1)S(1)} collective-permute-done((bf16[2,4,16,1024]{3,2,1,0:T(8,128)(2,1)S(1)}, bf16[2,4,16,1024]{3,2,1,0:T(8,128)(2,1)S(1)}, u32[]{:S(2)}, u32[]{:S(2)}) %collective-permute-start.2) | collective-permute-done | bytes 262176 | tf_op jit(solution)/shard_map/ppermute | solution.py:21
  29.0 3.3 %collective-permute-start.3 = (bf16[2,4,16,1024]{3,2,1,0:T(8,128)(2,1)S(1)}, bf16[2,4,16,1024]{3,2,1,0:T(8,128)(2,1)S(1)}, u32[]{:S(2)}, u32[]{:S(2)}) collective-permute-start(bf16[2,4,16,1024]{3,2,1,0:T(8,128)(2,1)S(1)} %collective-permute-done.2.refs_3_), channel_id=1, source_target_pairs={{0,4},{1,5},{2,14},{3,15},{4,8},{5,9},{6,2},{7,3},{8,12},{9,13},{1... | collective-permute-start | bytes 786440 | tf_op jit(solution)/shard_map/ppermute | solution.py:21
  32.3 1.1 %fusion.11 = (f32[64,512]{1,0:T(8,128)S(1)}, f32[64,512]{1,0:T(8,128)S(1)}, f32[64,512]{1,0:T(8,128)S(1)}, f32[64,512]{1,0:T(8,128)S(1)}) fusion(s32[512]{0:T(512)S(1)} %iota_add_fusion, s32[64]{0:T(128)S(1)} %multiply_add_fusion), kind=kLoop, calls=%fused_computation.36 | loop fusion | flops 917504 | bytes 526592 | tf_op jit(solution)/shard_map/sin | solution.py:28
  33.4 2.2 %tables.1 = (bf16[4096,512]{1,0:T(8,128)(2,1)S(1)}, bf16[4096,512]{1,0:T(8,128)(2,1)S(1)}) custom-call(f32[64,512]{1,0:T(8,128)S(1)} %get-tuple-element.32.fine_cos, f32[64,512]{1,0:T(8,128)S(1)} %get-tuple-element.31.fine_sin, f32[64,512]{1,0:T(8,128)S(1)} %get-tuple-element.30.coarse_cos, f32[64,512]{1,0:T(8,128)S(1)} %get-tuple-element.29.coarse_sin), custom_call_target="tpu_custom_call" | custom-call | flops 12582912 | bytes 8388608 | tf_op jit(solution)/shard_map/tables/pallas_call | solution.py:51
  35.6 0.0 collective-permute-done.8.refs_5_
  35.7 0.0 collective-permute-done.9.refs_6_
  35.7 3.5 %shard_map.37 = (f32[256,1152]{1,0:T(8,128)S(1)}, f32[256,128]{1,0:T(8,128)S(1)}) custom-call(s32[4,3]{1,0:T(4,128)S(1)} %pad_add_fusion.1.refs_0_, bf16[4,16,2176]{2,1,0:T(8,128)(2,1)S(1)} %pad_maximum_fusion.1.refs_1_, bf16[4,16,4224]{2,1,0:T(8,128)(2,1)S(1)} %collective-permute-done.1.refs_2_, bf16[4,16,2176]{2,1,0:T(8,128)(2,1)S(1)} %collective-permute-done.6.refs_3_, ...), custom_call_target="tpu_custom_call" | custom-call | flops 1073741824 | bytes 4194304 | tf_op jit(solution)/shard_map/pallas_call | solution.py:234
  39.2 0.0 collective-permute-done.5.refs_4_
  39.2 2.2 %shard_map.38.refs_7_ = f32[256,1152]{1,0:T(8,128)S(1)} custom-call(s32[4,3]{1,0:T(4,128)S(1)} %pad_add_fusion.1.refs_0_, bf16[4,16,1024]{2,1,0:T(8,128)(2,1)S(1)} %bitcast.34, bf16[4,16,4224]{2,1,0:T(8,128)(2,1)S(1)} %collective-permute-done.1.refs_2_, bf16[2,4,16,1024]{3,2,1,0:T(8,128)(2,1)S(1)} %collective-permute-done.4.refs_3_, ...), custom_call_target="tpu_custom_call", output_to_operand_aliasing={{}: (7, {})} | custom-call | flops 536870912 | bytes 2097152 | tf_op jit(solution)/shard_map/pallas_call | solution.py:234
  41.3 0.0 collective-permute-done.3.refs_4_
  41.4 2.3 %shard_map.39 = (f32[128,1152]{1,0:T(8,128)S(1)}, bf16[128,1024]{1,0:T(8,128)(2,1)S(1)}) custom-call(s32[4,3]{1,0:T(4,128)S(1)} %pad_add_fusion.1.refs_0_, bf16[4,16,1024]{2,1,0:T(8,128)(2,1)S(1)} %bitcast.32, bf16[4,16,4224]{2,1,0:T(8,128)(2,1)S(1)} %collective-permute-done.1.refs_2_, bf16[2,4,16,1024]{3,2,1,0:T(8,128)(2,1)S(1)} %collective-permute-done.2.refs_3_, ...), custom_call_target="tpu_custom_call" | custom-call | flops 536870912 | bytes 2097152 | tf_op jit(solution)/shard_map/pallas_call | solution.py:234
  43.6 1.8 %collective-permute-start.10 = (bf16[128,1024]{1,0:T(8,128)(2,1)S(1)}, bf16[128,1024]{1,0:T(8,128)(2,1)S(1)}, u32[]{:S(2)}, u32[]{:S(2)}) collective-permute-start(bf16[128,1024]{1,0:T(8,128)(2,1)S(1)} %get-tuple-element.20), channel_id=1, source_target_pairs={{0,1},{1,0},{2,3},{3,2},{4,5},{5,4},{6,7},{7,6},{8,9},{9,8},{10,11... | collective-permute-start | bytes 786440 | tf_op jit(solution)/shard_map/ppermute | solution.py:21
  45.5 0.3 mine.1
  45.8 0.9 %collective-permute-done.10 = bf16[128,1024]{1,0:T(8,128)(2,1)S(1)} collective-permute-done((bf16[128,1024]{1,0:T(8,128)(2,1)S(1)}, bf16[128,1024]{1,0:T(8,128)(2,1)S(1)}, u32[]{:S(2)}, u32[]{:S(2)}) %collective-permute-start.10) | collective-permute-done | bytes 262176 | tf_op jit(solution)/shard_map/ppermute | solution.py:21
  46.6 0.8 %add_convert_fusion = bf16[128,1024]{1,0:T(8,128)(2,1)} fusion(f32[128,1024]{1,0:T(8,128)S(1)} %mine.1, bf16[128,1024]{1,0:T(8,128)(2,1)S(1)} %collective-permute-done.10), kind=kLoop, calls=%fused_computation.3 | loop fusion | flops 393216 | bytes 1048576 | tf_op jit(solution)/shard_map/convert_element_type | solution.py:350
  (11 shorter events, 0.2 us)
Async XLA Ops:
  2.4 1.3 %copy-start = (bf16[8,4,2,8192]{3,2,1,0:T(2,128)(2,1)S(1)}, bf16[8,4,2,8192]{3,2,1,0:T(2,128)(2,1)}, u32[]{:S(2)}) copy-start(bf16[8,4,2,8192]{3,2,1,0:T(2,128)(2,1)} %param.3) | copy-start | bytes 3145732
  2.9 1.3 %copy-start.1 = (s32[2,2]{1,0:T(2,128)S(1)}, s32[2,2]{1,0:T(2,128)}, u32[]{:S(2)}) copy-start(s32[2,2]{1,0:T(2,128)} %param.5) | copy-start | bytes 52
  2.9 2.8 %collective-permute-start.1 = (bf16[4,16,4224]{2,1,0:T(8,128)(2,1)S(1)}, bf16[4,16,4224]{2,1,0:T(8,128)(2,1)S(1)}, u32[]{:S(2)}, u32[]{:S(2)}) collective-permute-start(bf16[4,16,4224]{2,1,0:T(8,128)(2,1)S(1)} %pad_maximum_fusion), channel_id=1, source_target_pairs={{0,1},{1,0},{2,3},{3,2},{4,5},{5,4},{6,7},{7,6},{8,9},{9,8},{10,11... | collective-permute-start | bytes 1622024 | tf_op jit(solution)/shard_map/ppermute | solution.py:21
  4.2 7.7 %collective-permute-start.6 = (bf16[4,16,2176]{2,1,0:T(8,128)(2,1)S(1)}, bf16[4,16,2176]{2,1,0:T(8,128)(2,1)S(1)}, u32[]{:S(2)}, u32[]{:S(2)}) collective-permute-start(bf16[4,16,2176]{2,1,0:T(8,128)(2,1)S(1)} %pad_maximum_fusion.1.refs_1_), channel_id=1, source_target_pairs={{0,2},{1,3},{2,0},{3,1},{4,6},{5,7},{6,4},{7,5},{8,10},{9,11},{10,... | collective-permute-start | bytes 835592 | tf_op jit(solution)/shard_map/ppermute | solution.py:21
  4.2 1.5 %collective-permute-start = (s32[2,2]{1,0:T(2,128)S(1)}, s32[2,2]{1,0:T(2,128)S(1)}, u32[]{:S(2)}, u32[]{:S(2)}) collective-permute-start(s32[2,2]{1,0:T(2,128)S(1)} %copy-done.1), channel_id=1, source_target_pairs={{0,1},{1,0},{2,3},{3,2},{4,5},{5,4},{6,7},{7,6},{8,9},{9,8},{10,11... | collective-permute-start | bytes 56 | tf_op jit(solution)/shard_map/ppermute | solution.py:21
  5.9 11.9 %collective-permute-start.7 = (bf16[4,16,2176]{2,1,0:T(8,128)(2,1)S(1)}, bf16[4,16,2176]{2,1,0:T(8,128)(2,1)S(1)}, u32[]{:S(2)}, u32[]{:S(2)}) collective-permute-start(bf16[4,16,2176]{2,1,0:T(8,128)(2,1)S(1)} %slice.18), channel_id=1, source_target_pairs={{0,2},{1,3},{2,0},{3,1},{4,6},{5,7},{6,4},{7,5},{8,10},{9,11},{10,... | collective-permute-start | bytes 835592 | tf_op jit(solution)/shard_map/ppermute | solution.py:21
  7.6 15.8 %collective-permute-start.4 = (bf16[2,4,16,1024]{3,2,1,0:T(8,128)(2,1)S(1)}, bf16[2,4,16,1024]{3,2,1,0:T(8,128)(2,1)S(1)}, u32[]{:S(2)}, u32[]{:S(2)}) collective-permute-start(bf16[2,4,16,1024]{3,2,1,0:T(8,128)(2,1)S(1)} %pad_maximum_fusion.3), channel_id=1, source_target_pairs={{0,2},{1,3},{2,0},{3,1},{4,6},{5,7},{6,4},{7,5},{8,10},{9,11},{10,... | collective-permute-start | bytes 786440 | tf_op jit(solution)/shard_map/ppermute | solution.py:21
  7.7 21.3 %collective-permute-start.2 = (bf16[2,4,16,1024]{3,2,1,0:T(8,128)(2,1)S(1)}, bf16[2,4,16,1024]{3,2,1,0:T(8,128)(2,1)S(1)}, u32[]{:S(2)}, u32[]{:S(2)}) collective-permute-start(bf16[2,4,16,1024]{3,2,1,0:T(8,128)(2,1)S(1)} %pad_maximum_fusion.2), channel_id=1, source_target_pairs={{0,2},{1,3},{2,0},{3,1},{4,6},{5,7},{6,4},{7,5},{8,10},{9,11},{10,... | collective-permute-start | bytes 786440 | tf_op jit(solution)/shard_map/ppermute | solution.py:21
  11.8 23.8 %collective-permute-start.8 = (bf16[4,16,2176]{2,1,0:T(8,128)(2,1)S(1)}, bf16[4,16,2176]{2,1,0:T(8,128)(2,1)S(1)}, u32[]{:S(2)}, u32[]{:S(2)}) collective-permute-start(bf16[4,16,2176]{2,1,0:T(8,128)(2,1)S(1)} %collective-permute-done.6.refs_3_), channel_id=1, source_target_pairs={{0,4},{1,5},{2,14},{3,15},{4,8},{5,9},{6,2},{7,3},{8,12},{9,13},{1... | collective-permute-start | bytes 835592 | tf_op jit(solution)/shard_map/ppermute | solution.py:21
  17.8 17.9 %collective-permute-start.9 = (bf16[4,16,2176]{2,1,0:T(8,128)(2,1)S(1)}, bf16[4,16,2176]{2,1,0:T(8,128)(2,1)S(1)}, u32[]{:S(2)}, u32[]{:S(2)}) collective-permute-start(bf16[4,16,2176]{2,1,0:T(8,128)(2,1)S(1)} %collective-permute-done.7.refs_4_), channel_id=1, source_target_pairs={{0,4},{1,5},{2,14},{3,15},{4,8},{5,9},{6,2},{7,3},{8,12},{9,13},{1... | collective-permute-start | bytes 835592 | tf_op jit(solution)/shard_map/ppermute | solution.py:21
  23.4 15.8 %collective-permute-start.5 = (bf16[2,4,16,1024]{3,2,1,0:T(8,128)(2,1)S(1)}, bf16[2,4,16,1024]{3,2,1,0:T(8,128)(2,1)S(1)}, u32[]{:S(2)}, u32[]{:S(2)}) collective-permute-start(bf16[2,4,16,1024]{3,2,1,0:T(8,128)(2,1)S(1)} %collective-permute-done.4.refs_3_), channel_id=1, source_target_pairs={{0,4},{1,5},{2,14},{3,15},{4,8},{5,9},{6,2},{7,3},{8,12},{9,13},{1... | collective-permute-start | bytes 786440 | tf_op jit(solution)/shard_map/ppermute | solution.py:21
  29.0 12.3 %collective-permute-start.3 = (bf16[2,4,16,1024]{3,2,1,0:T(8,128)(2,1)S(1)}, bf16[2,4,16,1024]{3,2,1,0:T(8,128)(2,1)S(1)}, u32[]{:S(2)}, u32[]{:S(2)}) collective-permute-start(bf16[2,4,16,1024]{3,2,1,0:T(8,128)(2,1)S(1)} %collective-permute-done.2.refs_3_), channel_id=1, source_target_pairs={{0,4},{1,5},{2,14},{3,15},{4,8},{5,9},{6,2},{7,3},{8,12},{9,13},{1... | collective-permute-start | bytes 786440 | tf_op jit(solution)/shard_map/ppermute | solution.py:21
  43.6 3.0 %collective-permute-start.10 = (bf16[128,1024]{1,0:T(8,128)(2,1)S(1)}, bf16[128,1024]{1,0:T(8,128)(2,1)S(1)}, u32[]{:S(2)}, u32[]{:S(2)}) collective-permute-start(bf16[128,1024]{1,0:T(8,128)(2,1)S(1)} %get-tuple-element.20), channel_id=1, source_target_pairs={{0,1},{1,0},{2,3},{3,2},{4,5},{5,4},{6,7},{7,6},{8,9},{9,8},{10,11... | collective-permute-start | bytes 786440 | tf_op jit(solution)/shard_map/ppermute | solution.py:21

commit v3 on v2

--- a/solution.py
+++ b/solution.py
@@ -288,6 +288,9 @@
     core_pairs = [(i, i ^ 1) for i in range(peers)]
     near_pairs = [(i, i ^ 2) for i in range(peers)]
     far_pairs = [(i, (i + 4 - 8 * ((i // 2) % 2)) % peers) for i in range(peers)]
+    split_pairs = dict(far_pairs)
+    split_pairs.update({2: 0, peers - 3: peers - 1, 3: peers - 2, peers - 4: 1})
+    split_pairs = sorted(split_pairs.items())
     valid = window_mask.astype(jnp.bfloat16).T[:, None, :, None]
     mark = jnp.broadcast_to(valid, (windows, 2, stations, LANES)).reshape(
         windows, 2 * stations, LANES
@@ -312,7 +315,7 @@
         if high == half:
             piece, base = lax.optimization_barrier((piece, core * half))
         near.append(permute(piece, near_pairs))
-    far = [permute(piece, far_pairs) for piece in near]
+    far = [permute(piece, split_pairs if at >= 3 else far_pairs) for at, piece in enumerate(near)]
 
     fine = angle_tables(jnp.arange(FINE, dtype=jnp.int32), lag_half, frequency_values)
     coarse = angle_tables(
@@ -327,20 +330,21 @@
     tables = lag_tables(fine, coarse)
     norm = math.sqrt(frequency_values)
     acc = weights = None
-    for at in range(len(splits) - 1):
-        low, high = splits[at], splits[at + 1]
-        last = at == len(splits) - 2
+    units = [(0, 0, lead // 2), (0, lead // 2, lead)]
+    units += [(at, splits[at], splits[at + 1]) for at in range(1, len(splits) - 1)]
+    for unit, (at, low, high) in enumerate(units):
+        last = unit == len(units) - 1
         if at == 0:
             sources = [own_lead, par, near[0], near[1], far[0], far[1]]
-            views_at = [(which, None, LANES) for which in range(6)]
+            views_at = [(which, None, LANES + low) for which in range(6)]
         else:
             sources = [own[at - 1], par, near[at + 1], far[at + 1]]
             views_at = [(0, None, 0), (1, None, LANES + low), (2, 0, 0), (2, 1, 0), (3, 0, 0), (3, 1, 0)]
-        width = min(SUB, (high - low) // 2)
+        width = SUB // 2 if last else SUB
         made = chunk_call(
             table, sources, views_at, tables, acc, weights, last, low, high - low, width, windows, stations, norm
         )
-        if at == 0:
+        if unit == 0:
             acc, weights = made
         elif not last:
             (acc,) = made

time: 47.6 us -> 48.3 us (1.015)
  the two profiles are of different devices: /device:TPU:5 before, /device:TPU:7 now
where the time goes in v3:
time: 48.3 us; the launch traced here: 48.1 us
  starting transfers between devices  19.5 us (40%)
  waiting for transfers between devices  11.4 us (24%)
  Pallas kernels  11.2 us (23%)
  other arithmetic  4.88 us (10%)
  local copies, waits for them, and re-layouts  0.92 us (2%)
    ppermute x11, starting transfers between devices, permute(): return lax.ppermute(array, 'sta', pairs)  19.5 us
    ppermute x11, waiting for transfers between devices, permute(): return lax.ppermute(array, 'sta', pairs)  11.4 us
    pallas_call x4, Pallas kernels, chunk_call(): pl.pallas_call(functools.partial(chunk_kernel, views_at=views_at, slot_co...  8.71 us
    pallas_call x1, Pallas kernels, lag_tables(): pl.pallas_call(table_kernel, in_specs=[vmem] * 4, out_specs=[vmem] * 2, o...  2.24 us
    mul x3, other arithmetic, rows_of(): piece.transpose(1, 2, 0, 3) * valid  2.15 us
    sin x1, other arithmetic, angle_tables(): return (jnp.cos(phase_angle), jnp.sin(phase_angle))  1.06 us
  transfers between devices with their start and end apart: 11, of which 6 were waited for; matrix products, arithmetic and copies ran while one was open for 4% of the time, Pallas kernels for 19%

profile of v3, /device:TPU:7, one launch (start us, length us, event | category | flops | bytes accessed | tf_op | source)
XLA Modules:
  0.0 48.1 jit_solution(1069543854605718880)
XLA Ops:
  0.0 0.7 %convert_bitcast_fusion = bf16[4,8]{1,0:T(4,128)(2,1)S(1)} fusion(s32[8,4]{0,1:T(4,128)} %param.4), kind=kLoop, calls=%fused_computation.45 | loop fusion | flops 32 | bytes 192 | tf_op jit(solution)/shard_map/transpose | solution.py:294
  0.7 0.1 copy.6
  0.8 1.6 %bitcast_multiply_fusion = bf16[4,2,8,4096]{3,1,0,2:T(2,128)(2,1)S(1)} fusion(bf16[8,4,2,8192]{3,2,1,0:T(2,128)(2,1)} %param.3, s32[]{:T(128)S(6)} %select_n.36, bf16[4,8]{0,1:T(8,128)(2,1)S(1)} %copy.6), kind=kLoop, calls=%fused_computation.1 | loop fusion | flops 1048576 | bytes 1048644 | tf_op jit(solution)/shard_map/mul | solution.py:301
  2.4 0.0 copy-start
  2.4 0.3 copy.21
  2.7 0.1 broadcast_in_dim.27
  2.8 0.1 broadcast_in_dim.28
  2.9 0.0 copy-start.1
  2.9 0.7 %collective-permute-start.1 = (bf16[4,16,4224]{2,1,0:T(8,128)(2,1)S(1)}, bf16[4,16,4224]{2,1,0:T(8,128)(2,1)S(1)}, u32[]{:S(2)}, u32[]{:S(2)}) collective-permute-start(bf16[4,16,4224]{2,1,0:T(8,128)(2,1)S(1)} %pad_maximum_fusion), channel_id=1, source_target_pairs={{0,1},{1,0},{2,3},{3,2},{4,5},{5,4},{6,7},{7,6},{8,9},{9,8},{10,11... | collective-permute-start | bytes 1622024 | tf_op jit(solution)/shard_map/ppermute | solution.py:21
  3.7 0.0 copy-done
  3.7 0.3 bitcast_multiply_fusion.1
  4.0 0.2 copy.22
  4.2 0.3 collective-permute-start.6
  4.4 0.0 copy-done.1
  4.4 0.9 %collective-permute-start = (s32[2,2]{1,0:T(2,128)S(1)}, s32[2,2]{1,0:T(2,128)S(1)}, u32[]{:S(2)}, u32[]{:S(2)}) collective-permute-start(s32[2,2]{1,0:T(2,128)S(1)} %copy-done.1), channel_id=1, source_target_pairs={{0,1},{1,0},{2,3},{3,2},{4,5},{5,4},{6,7},{7,6},{8,9},{9,8},{10,11... | collective-permute-start | bytes 56 | tf_op jit(solution)/shard_map/ppermute | solution.py:21
  5.3 0.3 bitcast_multiply_fusion.2
  5.6 0.1 copy.24
  5.7 0.1 copy.23
  5.8 0.4 collective-permute-done
  6.2 0.0 collective-permute-done.1.refs_2_
  6.3 1.3 %collective-permute-start.7 = (bf16[4,16,2176]{2,1,0:T(8,128)(2,1)S(1)}, bf16[4,16,2176]{2,1,0:T(8,128)(2,1)S(1)}, u32[]{:S(2)}, u32[]{:S(2)}) collective-permute-start(bf16[4,16,2176]{2,1,0:T(8,128)(2,1)S(1)} %slice.18), channel_id=1, source_target_pairs={{0,2},{1,3},{2,0},{3,1},{4,6},{5,7},{6,4},{7,5},{8,10},{9,11},{10,... | collective-permute-start | bytes 835592 | tf_op jit(solution)/shard_map/ppermute | solution.py:21
  7.6 0.3 collective-permute-start.4
  7.9 1.2 %collective-permute-start.2 = (bf16[2,4,16,1024]{3,2,1,0:T(8,128)(2,1)S(1)}, bf16[2,4,16,1024]{3,2,1,0:T(8,128)(2,1)S(1)}, u32[]{:S(2)}, u32[]{:S(2)}) collective-permute-start(bf16[2,4,16,1024]{3,2,1,0:T(8,128)(2,1)S(1)} %pad_maximum_fusion.2), channel_id=1, source_target_pairs={{0,2},{1,3},{2,0},{3,1},{4,6},{5,7},{6,4},{7,5},{8,10},{9,11},{10,... | collective-permute-start | bytes 786440 | tf_op jit(solution)/shard_map/ppermute | solution.py:21
  9.2 0.1 pad_add_fusion.1.refs_0_
  9.2 2.6 %collective-permute-done.6.refs_3_ = bf16[4,16,2176]{2,1,0:T(8,128)(2,1)S(1)} collective-permute-done((bf16[4,16,2176]{2,1,0:T(8,128)(2,1)S(1)}, bf16[4,16,2176]{2,1,0:T(8,128)(2,1)S(1)}, u32[]{:S(2)}, u32[]{:S(2)}) %collective-permute-start.6) | collective-permute-done | bytes 278560 | tf_op jit(solution)/shard_map/ppermute | solution.py:21
  11.8 3.3 %collective-permute-start.8 = (bf16[4,16,2176]{2,1,0:T(8,128)(2,1)S(1)}, bf16[4,16,2176]{2,1,0:T(8,128)(2,1)S(1)}, u32[]{:S(2)}, u32[]{:S(2)}) collective-permute-start(bf16[4,16,2176]{2,1,0:T(8,128)(2,1)S(1)} %collective-permute-done.6.refs_3_), channel_id=1, source_target_pairs={{0,4},{1,5},{2,14},{3,15},{4,8},{5,9},{6,2},{7,3},{8,12},{9,13},{1... | collective-permute-start | bytes 835592 | tf_op jit(solution)/shard_map/ppermute | solution.py:21
  15.1 2.6 %collective-permute-done.7.refs_4_ = bf16[4,16,2176]{2,1,0:T(8,128)(2,1)S(1)} collective-permute-done((bf16[4,16,2176]{2,1,0:T(8,128)(2,1)S(1)}, bf16[4,16,2176]{2,1,0:T(8,128)(2,1)S(1)}, u32[]{:S(2)}, u32[]{:S(2)}) %collective-permute-start.7) | collective-permute-done | bytes 278560 | tf_op jit(solution)/shard_map/ppermute | solution.py:21
  17.8 3.3 %collective-permute-start.9 = (bf16[4,16,2176]{2,1,0:T(8,128)(2,1)S(1)}, bf16[4,16,2176]{2,1,0:T(8,128)(2,1)S(1)}, u32[]{:S(2)}, u32[]{:S(2)}) collective-permute-start(bf16[4,16,2176]{2,1,0:T(8,128)(2,1)S(1)} %collective-permute-done.7.refs_4_), channel_id=1, source_target_pairs={{0,4},{1,5},{2,14},{3,15},{4,8},{5,9},{6,2},{7,3},{8,12},{9,13},{1... | collective-permute-start | bytes 835592 | tf_op jit(solution)/shard_map/ppermute | solution.py:21
  21.1 2.3 %collective-permute-done.4.refs_3_ = bf16[2,4,16,1024]{3,2,1,0:T(8,128)(2,1)S(1)} collective-permute-done((bf16[2,4,16,1024]{3,2,1,0:T(8,128)(2,1)S(1)}, bf16[2,4,16,1024]{3,2,1,0:T(8,128)(2,1)S(1)}, u32[]{:S(2)}, u32[]{:S(2)}) %collective-permute-start.4) | collective-permute-done | bytes 262176 | tf_op jit(solution)/shard_map/ppermute | solution.py:21
  23.4 3.3 %collective-permute-start.5 = (bf16[2,4,16,1024]{3,2,1,0:T(8,128)(2,1)S(1)}, bf16[2,4,16,1024]{3,2,1,0:T(8,128)(2,1)S(1)}, u32[]{:S(2)}, u32[]{:S(2)}) collective-permute-start(bf16[2,4,16,1024]{3,2,1,0:T(8,128)(2,1)S(1)} %collective-permute-done.4.refs_3_), channel_id=1, source_target_pairs={{0,4},{1,5},{2,14},{3,15},{4,8},{5,9},{6,2},{7,3},{8,12},{9,13},{1... | collective-permute-start | bytes 786440 | tf_op jit(solution)/shard_map/ppermute | solution.py:21
  26.7 2.3 %collective-permute-done.2.refs_3_ = bf16[2,4,16,1024]{3,2,1,0:T(8,128)(2,1)S(1)} collective-permute-done((bf16[2,4,16,1024]{3,2,1,0:T(8,128)(2,1)S(1)}, bf16[2,4,16,1024]{3,2,1,0:T(8,128)(2,1)S(1)}, u32[]{:S(2)}, u32[]{:S(2)}) %collective-permute-start.2) | collective-permute-done | bytes 262176 | tf_op jit(solution)/shard_map/ppermute | solution.py:21
  29.0 4.7 %collective-permute-start.3 = (bf16[2,4,16,1024]{3,2,1,0:T(8,128)(2,1)S(1)}, bf16[2,4,16,1024]{3,2,1,0:T(8,128)(2,1)S(1)}, u32[]{:S(2)}, u32[]{:S(2)}) collective-permute-start(bf16[2,4,16,1024]{3,2,1,0:T(8,128)(2,1)S(1)} %collective-permute-done.2.refs_3_), channel_id=1, source_target_pairs={{0,4},{1,5},{2,0},{3,14},{4,8},{5,9},{6,2},{7,3},{8,12},{9,13},{10... | collective-permute-start | bytes 786440 | tf_op jit(solution)/shard_map/ppermute | solution.py:21
  33.7 1.1 %fusion.11 = (f32[64,512]{1,0:T(8,128)S(1)}, f32[64,512]{1,0:T(8,128)S(1)}, f32[64,512]{1,0:T(8,128)S(1)}, f32[64,512]{1,0:T(8,128)S(1)}) fusion(s32[512]{0:T(512)S(1)} %iota_add_fusion, s32[64]{0:T(128)S(1)} %multiply_add_fusion), kind=kLoop, calls=%fused_computation.36 | loop fusion | flops 917504 | bytes 526592 | tf_op jit(solution)/shard_map/sin | solution.py:28
  34.8 2.2 %tables.1 = (bf16[4096,512]{1,0:T(8,128)(2,1)S(1)}, bf16[4096,512]{1,0:T(8,128)(2,1)S(1)}) custom-call(f32[64,512]{1,0:T(8,128)S(1)} %get-tuple-element.32.fine_cos, f32[64,512]{1,0:T(8,128)S(1)} %get-tuple-element.31.fine_sin, f32[64,512]{1,0:T(8,128)S(1)} %get-tuple-element.30.coarse_cos, f32[64,512]{1,0:T(8,128)S(1)} %get-tuple-element.29.coarse_sin), custom_call_target="tpu_custom_call" | custom-call | flops 12582912 | bytes 8388608 | tf_op jit(solution)/shard_map/tables/pallas_call | solution.py:51
  37.0 0.0 collective-permute-done.8.refs_5_
  37.0 0.0 collective-permute-done.9.refs_6_
  37.0 2.1 %shard_map.37 = (f32[256,1152]{1,0:T(8,128)S(1)}, f32[256,128]{1,0:T(8,128)S(1)}) custom-call(s32[4,3]{1,0:T(4,128)S(1)} %pad_add_fusion.1.refs_0_, bf16[4,16,2176]{2,1,0:T(8,128)(2,1)S(1)} %pad_maximum_fusion.1.refs_1_, bf16[4,16,4224]{2,1,0:T(8,128)(2,1)S(1)} %collective-permute-done.1.refs_2_, bf16[4,16,2176]{2,1,0:T(8,128)(2,1)S(1)} %collective-permute-done.6.refs_3_, ...), custom_call_target="tpu_custom_call" | custom-call | flops 536870912 | bytes 2097152 | tf_op jit(solution)/shard_map/pallas_call | solution.py:234
  39.2 2.2 %shard_map.38.refs_7_ = f32[256,1152]{1,0:T(8,128)S(1)} custom-call(s32[4,3]{1,0:T(4,128)S(1)} %pad_add_fusion.1.refs_0_, bf16[4,16,2176]{2,1,0:T(8,128)(2,1)S(1)} %pad_maximum_fusion.1.refs_1_, bf16[4,16,4224]{2,1,0:T(8,128)(2,1)S(1)} %collective-permute-done.1.refs_2_, ...), custom_call_target="tpu_custom_call", output_to_operand_aliasing={{}: (9, {})} | custom-call | flops 536870912 | bytes 2097152 | tf_op jit(solution)/shard_map/pallas_call | solution.py:234
  41.3 0.0 collective-permute-done.5.refs_4_
  41.3 2.2 %shard_map.39.refs_7_ = f32[256,1152]{1,0:T(8,128)S(1)} custom-call(s32[4,3]{1,0:T(4,128)S(1)} %pad_add_fusion.1.refs_0_, bf16[4,16,1024]{2,1,0:T(8,128)(2,1)S(1)} %bitcast.34, bf16[4,16,4224]{2,1,0:T(8,128)(2,1)S(1)} %collective-permute-done.1.refs_2_, bf16[2,4,16,1024]{3,2,1,0:T(8,128)(2,1)S(1)} %collective-permute-done.4.refs_3_, ...), custom_call_target="tpu_custom_call", output_to_operand_aliasing={{}: (7, {})} | custom-call | flops 536870912 | bytes 2097152 | tf_op jit(solution)/shard_map/pallas_call | solution.py:234
  43.5 0.0 collective-permute-done.3.refs_4_
  43.5 2.2 %shard_map.40 = (f32[128,1152]{1,0:T(8,128)S(1)}, bf16[128,1024]{1,0:T(8,128)(2,1)S(1)}) custom-call(s32[4,3]{1,0:T(4,128)S(1)} %pad_add_fusion.1.refs_0_, bf16[4,16,1024]{2,1,0:T(8,128)(2,1)S(1)} %bitcast.32, bf16[4,16,4224]{2,1,0:T(8,128)(2,1)S(1)} %collective-permute-done.1.refs_2_, bf16[2,4,16,1024]{3,2,1,0:T(8,128)(2,1)S(1)} %collective-permute-done.2.refs_3_, ...), custom_call_target="tpu_custom_call" | custom-call | flops 536870912 | bytes 2097152 | tf_op jit(solution)/shard_map/pallas_call | solution.py:234
  45.8 0.1 collective-permute-start.10
  45.8 0.3 mine.1
  46.1 1.2 %collective-permute-done.10 = bf16[128,1024]{1,0:T(8,128)(2,1)S(1)} collective-permute-done((bf16[128,1024]{1,0:T(8,128)(2,1)S(1)}, bf16[128,1024]{1,0:T(8,128)(2,1)S(1)}, u32[]{:S(2)}, u32[]{:S(2)}) %collective-permute-start.10) | collective-permute-done | bytes 262176 | tf_op jit(solution)/shard_map/ppermute | solution.py:21
  47.4 0.8 %add_convert_fusion = bf16[128,1024]{1,0:T(8,128)(2,1)} fusion(f32[128,1024]{1,0:T(8,128)S(1)} %mine.1, bf16[128,1024]{1,0:T(8,128)(2,1)S(1)} %collective-permute-done.10), kind=kLoop, calls=%fused_computation.3 | loop fusion | flops 393216 | bytes 1048576 | tf_op jit(solution)/shard_map/convert_element_type | solution.py:354
  (11 shorter events, 0.2 us)
Async XLA Ops:
  2.4 1.3 %copy-start = (bf16[8,4,2,8192]{3,2,1,0:T(2,128)(2,1)S(1)}, bf16[8,4,2,8192]{3,2,1,0:T(2,128)(2,1)}, u32[]{:S(2)}) copy-start(bf16[8,4,2,8192]{3,2,1,0:T(2,128)(2,1)} %param.3) | copy-start | bytes 3145732
  2.9 1.6 %copy-start.1 = (s32[2,2]{1,0:T(2,128)S(1)}, s32[2,2]{1,0:T(2,128)}, u32[]{:S(2)}) copy-start(s32[2,2]{1,0:T(2,128)} %param.5) | copy-start | bytes 52
  2.9 3.2 %collective-permute-start.1 = (bf16[4,16,4224]{2,1,0:T(8,128)(2,1)S(1)}, bf16[4,16,4224]{2,1,0:T(8,128)(2,1)S(1)}, u32[]{:S(2)}, u32[]{:S(2)}) collective-permute-start(bf16[4,16,4224]{2,1,0:T(8,128)(2,1)S(1)} %pad_maximum_fusion), channel_id=1, source_target_pairs={{0,1},{1,0},{2,3},{3,2},{4,5},{5,4},{6,7},{7,6},{8,9},{9,8},{10,11... | collective-permute-start | bytes 1622024 | tf_op jit(solution)/shard_map/ppermute | solution.py:21
  4.2 7.7 %collective-permute-start.6 = (bf16[4,16,2176]{2,1,0:T(8,128)(2,1)S(1)}, bf16[4,16,2176]{2,1,0:T(8,128)(2,1)S(1)}, u32[]{:S(2)}, u32[]{:S(2)}) collective-permute-start(bf16[4,16,2176]{2,1,0:T(8,128)(2,1)S(1)} %pad_maximum_fusion.1.refs_1_), channel_id=1, source_target_pairs={{0,2},{1,3},{2,0},{3,1},{4,6},{5,7},{6,4},{7,5},{8,10},{9,11},{10,... | collective-permute-start | bytes 835592 | tf_op jit(solution)/shard_map/ppermute | solution.py:21
  4.4 1.7 %collective-permute-start = (s32[2,2]{1,0:T(2,128)S(1)}, s32[2,2]{1,0:T(2,128)S(1)}, u32[]{:S(2)}, u32[]{:S(2)}) collective-permute-start(s32[2,2]{1,0:T(2,128)S(1)} %copy-done.1), channel_id=1, source_target_pairs={{0,1},{1,0},{2,3},{3,2},{4,5},{5,4},{6,7},{7,6},{8,9},{9,8},{10,11... | collective-permute-start | bytes 56 | tf_op jit(solution)/shard_map/ppermute | solution.py:21
  6.3 11.5 %collective-permute-start.7 = (bf16[4,16,2176]{2,1,0:T(8,128)(2,1)S(1)}, bf16[4,16,2176]{2,1,0:T(8,128)(2,1)S(1)}, u32[]{:S(2)}, u32[]{:S(2)}) collective-permute-start(bf16[4,16,2176]{2,1,0:T(8,128)(2,1)S(1)} %slice.18), channel_id=1, source_target_pairs={{0,2},{1,3},{2,0},{3,1},{4,6},{5,7},{6,4},{7,5},{8,10},{9,11},{10,... | collective-permute-start | bytes 835592 | tf_op jit(solution)/shard_map/ppermute | solution.py:21
  7.6 15.8 %collective-permute-start.4 = (bf16[2,4,16,1024]{3,2,1,0:T(8,128)(2,1)S(1)}, bf16[2,4,16,1024]{3,2,1,0:T(8,128)(2,1)S(1)}, u32[]{:S(2)}, u32[]{:S(2)}) collective-permute-start(bf16[2,4,16,1024]{3,2,1,0:T(8,128)(2,1)S(1)} %pad_maximum_fusion.3), channel_id=1, source_target_pairs={{0,2},{1,3},{2,0},{3,1},{4,6},{5,7},{6,4},{7,5},{8,10},{9,11},{10,... | collective-permute-start | bytes 786440 | tf_op jit(solution)/shard_map/ppermute | solution.py:21
  7.9 21.1 %collective-permute-start.2 = (bf16[2,4,16,1024]{3,2,1,0:T(8,128)(2,1)S(1)}, bf16[2,4,16,1024]{3,2,1,0:T(8,128)(2,1)S(1)}, u32[]{:S(2)}, u32[]{:S(2)}) collective-permute-start(bf16[2,4,16,1024]{3,2,1,0:T(8,128)(2,1)S(1)} %pad_maximum_fusion.2), channel_id=1, source_target_pairs={{0,2},{1,3},{2,0},{3,1},{4,6},{5,7},{6,4},{7,5},{8,10},{9,11},{10,... | collective-permute-start | bytes 786440 | tf_op jit(solution)/shard_map/ppermute | solution.py:21
  11.8 25.2 %collective-permute-start.8 = (bf16[4,16,2176]{2,1,0:T(8,128)(2,1)S(1)}, bf16[4,16,2176]{2,1,0:T(8,128)(2,1)S(1)}, u32[]{:S(2)}, u32[]{:S(2)}) collective-permute-start(bf16[4,16,2176]{2,1,0:T(8,128)(2,1)S(1)} %collective-permute-done.6.refs_3_), channel_id=1, source_target_pairs={{0,4},{1,5},{2,14},{3,15},{4,8},{5,9},{6,2},{7,3},{8,12},{9,13},{1... | collective-permute-start | bytes 835592 | tf_op jit(solution)/shard_map/ppermute | solution.py:21
  17.8 19.2 %collective-permute-start.9 = (bf16[4,16,2176]{2,1,0:T(8,128)(2,1)S(1)}, bf16[4,16,2176]{2,1,0:T(8,128)(2,1)S(1)}, u32[]{:S(2)}, u32[]{:S(2)}) collective-permute-start(bf16[4,16,2176]{2,1,0:T(8,128)(2,1)S(1)} %collective-permute-done.7.refs_4_), channel_id=1, source_target_pairs={{0,4},{1,5},{2,14},{3,15},{4,8},{5,9},{6,2},{7,3},{8,12},{9,13},{1... | collective-permute-start | bytes 835592 | tf_op jit(solution)/shard_map/ppermute | solution.py:21
  23.4 17.9 %collective-permute-start.5 = (bf16[2,4,16,1024]{3,2,1,0:T(8,128)(2,1)S(1)}, bf16[2,4,16,1024]{3,2,1,0:T(8,128)(2,1)S(1)}, u32[]{:S(2)}, u32[]{:S(2)}) collective-permute-start(bf16[2,4,16,1024]{3,2,1,0:T(8,128)(2,1)S(1)} %collective-permute-done.4.refs_3_), channel_id=1, source_target_pairs={{0,4},{1,5},{2,14},{3,15},{4,8},{5,9},{6,2},{7,3},{8,12},{9,13},{1... | collective-permute-start | bytes 786440 | tf_op jit(solution)/shard_map/ppermute | solution.py:21
  29.0 14.5 %collective-permute-start.3 = (bf16[2,4,16,1024]{3,2,1,0:T(8,128)(2,1)S(1)}, bf16[2,4,16,1024]{3,2,1,0:T(8,128)(2,1)S(1)}, u32[]{:S(2)}, u32[]{:S(2)}) collective-permute-start(bf16[2,4,16,1024]{3,2,1,0:T(8,128)(2,1)S(1)} %collective-permute-done.2.refs_3_), channel_id=1, source_target_pairs={{0,4},{1,5},{2,0},{3,14},{4,8},{5,9},{6,2},{7,3},{8,12},{9,13},{10... | collective-permute-start | bytes 786440 | tf_op jit(solution)/shard_map/ppermute | solution.py:21
  45.8 1.6 %collective-permute-start.10 = (bf16[128,1024]{1,0:T(8,128)(2,1)S(1)}, bf16[128,1024]{1,0:T(8,128)(2,1)S(1)}, u32[]{:S(2)}, u32[]{:S(2)}) collective-permute-start(bf16[128,1024]{1,0:T(8,128)(2,1)S(1)} %get-tuple-element.20), channel_id=1, source_target_pairs={{0,1},{1,0},{2,3},{3,2},{4,5},{5,4},{6,7},{7,6},{8,9},{9,8},{10,11... | collective-permute-start | bytes 786440 | tf_op jit(solution)/shard_map/ppermute | solution.py:21

commit v4 on v3

--- a/solution.py
+++ b/solution.py
@@ -63,9 +63,12 @@
 
 def pair_weights(slots_ref, sources, marks, weight_ref, slot_count, windows, stations, norm):
     pairs = stations * stations
-    for at, view in enumerate(sources):
+    own_mark, par, near, far = sources
+    views = [(own_mark, 0), (par, 0), (near, 0), (near, 1), (far, 0), (far, 1)]
+    for at, (view, part) in enumerate(views):
         for window in range(windows):
-            marks[at, window] = view[window, :, :LANES].astype(jnp.float32)[:stations]
+            mark = view[window, :, :LANES].astype(jnp.float32)
+            marks[at, window] = mark[part * stations : (part + 1) * stations]
     for slot in range(slot_count):
         first_at = slots_ref[slot, 0]
         second_at = slots_ref[slot, 1]
@@ -114,6 +117,7 @@
     refs = list(refs)
     slots_ref = refs.pop(0)
     sources = [refs.pop(0) for _ in range(1 + max(which for which, _, _ in views_at))]
+    mark_source = refs.pop(0)
     cos_ref, sin_ref = (refs.pop(0) for _ in range(2))
     if not first:
         before_ref = refs.pop(0)
@@ -124,7 +128,7 @@
         acc_ref = refs.pop(0)
     if first:
         weight_ref = refs.pop(0)
-        marks = refs.pop()
+        marks = refs.pop(0)
     stage = refs.pop(0)
     buffers = [(refs[0], refs[1]), (refs[2], refs[3])]
     count = stage.shape[-1]
@@ -133,8 +137,10 @@
     width = buffers[0][0].shape[1]
     wide = 256
 
+    if not first:
+        marks = mark_source
     if first:
-        pair_weights(slots_ref, sources, marks, weight_ref, slot_count, windows, stations, norm)
+        pair_weights(slots_ref, [mark_source, sources[1], sources[3], sources[5]], marks, weight_ref, slot_count, windows, stations, norm)
         acc_ref[:, 2 * lag_half :] = jnp.zeros((slot_count * pairs, LANES), jnp.float32)
     else:
         acc_ref[:, 2 * lag_half :] = before_ref[:, 2 * lag_half :]
@@ -142,7 +148,11 @@
     for at, (which, part, lane) in enumerate(views_at):
         view = sources[which] if part is None else sources[which].at[part]
         for window in range(windows):
-            stage[at, window] = view[window, :, lane : lane + count].astype(jnp.float32)
+            mark = marks[at, window]
+            mark = jnp.concatenate([mark, mark], axis=0)
+            for start in range(0, count, LANES):
+                piece = view[window, :, lane + start : lane + start + LANES]
+                stage[at, window, :, start : start + LANES] = piece.astype(jnp.float32) * mark
 
     index = [(slots_ref[slot, 0], slots_ref[slot, 1]) for slot in range(slot_count)]
 
@@ -207,13 +217,13 @@
         mine_ref[...] = acc_ref[:half, :]
 
 
-def chunk_call(slots, sources, views_at, tables, before, weights, last, low, count, width, windows, stations, norm):
+def chunk_call(slots, sources, views_at, mark_source, tables, before, weights, last, low, count, width, windows, stations, norm):
     slot_count = slots.shape[0]
     lag_half = tables[0].shape[1]
     rows = slot_count * stations * stations
     first = before is None
     acc = jax.ShapeDtypeStruct((rows, 2 * lag_half + LANES), jnp.float32)
-    operands = list(sources) + list(tables)
+    operands = list(sources) + [mark_source] + list(tables)
     if not first:
         operands.append(before)
     if last:
@@ -224,7 +234,7 @@
     outs = [acc]
     if first:
         outs.append(jax.ShapeDtypeStruct((rows, LANES), jnp.float32))
-        scratch.append(pltpu.VMEM((6, windows, stations, LANES), jnp.float32))
+        outs.append(jax.ShapeDtypeStruct((6, windows, stations, LANES), jnp.float32))
     if last:
         outs = [
             jax.ShapeDtypeStruct((rows // 2, 2 * lag_half + LANES), jnp.float32),
@@ -291,22 +301,25 @@
     split_pairs = dict(far_pairs)
     split_pairs.update({2: 0, peers - 3: peers - 1, 3: peers - 2, peers - 4: 1})
     split_pairs = sorted(split_pairs.items())
+    unit_scale = lax.optimization_barrier(jnp.ones((), jnp.bfloat16))
+
+    def rows_of(start, size):
+        piece = lax.dynamic_slice_in_dim(spectra, start, size, 3)
+        return (piece.transpose(1, 2, 0, 3) * unit_scale).reshape(windows, 2 * stations, size)
+
+    splits = [half * cut // 16 for cut in CUTS]
+    lead = splits[1]
+    own_lead = rows_of(core * half, lead)
     valid = window_mask.astype(jnp.bfloat16).T[:, None, :, None]
     mark = jnp.broadcast_to(valid, (windows, 2, stations, LANES)).reshape(
         windows, 2 * stations, LANES
     )
-
-    def rows_of(start, size):
-        piece = lax.dynamic_slice_in_dim(spectra, start, size, 3)
-        return (piece.transpose(1, 2, 0, 3) * valid).reshape(windows, 2 * stations, size)
-
-    splits = [half * cut // 16 for cut in CUTS]
-    lead = splits[1]
-    own_lead = jnp.concatenate([mark, rows_of(core * half, lead)], axis=2)
     sent = jnp.concatenate([mark, rows_of((1 - core) * half, half)], axis=2)
     par = permute(sent, core_pairs)
+    both = jnp.concatenate([mark[:, :stations], par[:, :stations, :LANES]], axis=1)
+    par_lead = jnp.concatenate([both, par[:, :, LANES : LANES + lead]], axis=2)
     other_slots = permute(pair_slots, core_pairs)
-    near = [permute(own_lead, near_pairs), permute(par[:, :, : LANES + lead], near_pairs)]
+    near = [permute(own_lead, near_pairs), permute(par_lead, near_pairs)]
     own = []
     for at in range(1, len(splits) - 1):
         low, high = splits[at], splits[at + 1]
@@ -330,22 +343,23 @@
     tables = lag_tables(fine, coarse)
     norm = math.sqrt(frequency_values)
     acc = weights = None
-    units = [(0, 0, lead // 2), (0, lead // 2, lead)]
+    units = [(0, 0, lead // 512 * 256), (0, lead // 512 * 256, lead)]
+    mark_source = mark
     units += [(at, splits[at], splits[at + 1]) for at in range(1, len(splits) - 1)]
     for unit, (at, low, high) in enumerate(units):
         last = unit == len(units) - 1
         if at == 0:
             sources = [own_lead, par, near[0], near[1], far[0], far[1]]
-            views_at = [(which, None, LANES + low) for which in range(6)]
+            views_at = [(which, None, low + LANES * (which in (1, 3, 5))) for which in range(6)]
         else:
             sources = [own[at - 1], par, near[at + 1], far[at + 1]]
             views_at = [(0, None, 0), (1, None, LANES + low), (2, 0, 0), (2, 1, 0), (3, 0, 0), (3, 1, 0)]
-        width = SUB // 2 if last else SUB
+        width = SUB // 2 if last or (high - low) % SUB else SUB
         made = chunk_call(
-            table, sources, views_at, tables, acc, weights, last, low, high - low, width, windows, stations, norm
+            table, sources, views_at, mark_source, tables, acc, weights, last, low, high - low, width, windows, stations, norm
         )
         if unit == 0:
-            acc, weights = made
+            acc, weights, mark_source = made
         elif not last:
             (acc,) = made
         else:

time: 48.3 us -> 47.1 us (0.975)
  other arithmetic: 4.88 us -> 4.13 us
    transpose x1, other arithmetic: 0.68 us -> 0.01 us  [owner_stacks(): valid = window_mask.astype(jnp.bfloat16).T[:, None, :, None]]
  transfers between devices with their start and end apart: 11 -> 11, of which waited for: 6 -> 6; matrix products, arithmetic and copies ran while one was open for 4% -> 5% of each run, Pallas kernels for 19% -> 19%
where the time goes in v4:
time: 47.1 us; the launch traced here: 47 us
  starting transfers between devices  19.4 us (41%)
  Pallas kernels  11.2 us (24%)
  waiting for transfers between devices  11.1 us (24%)
  other arithmetic  4.13 us (9%)
  local copies, waits for them, and re-layouts  0.9 us (2%)
    ppermute x11, starting transfers between devices, permute(): return lax.ppermute(array, 'sta', pairs)  19.4 us
    ppermute x11, waiting for transfers between devices, permute(): return lax.ppermute(array, 'sta', pairs)  11.1 us
    pallas_call x4, Pallas kernels, chunk_call(): pl.pallas_call(functools.partial(chunk_kernel, views_at=views_at, slot_co...  8.7 us
    pallas_call x1, Pallas kernels, lag_tables(): pl.pallas_call(table_kernel, in_specs=[vmem] * 4, out_specs=[vmem] * 2, o...  2.24 us
    mul x3, other arithmetic, rows_of(): piece.transpose(1, 2, 0, 3) * unit_scale  2.09 us
    sin x1, other arithmetic, angle_tables(): return (jnp.cos(phase_angle), jnp.sin(phase_angle))  1.06 us
  transfers between devices with their start and end apart: 11, of which 6 were waited for; matrix products, arithmetic and copies ran while one was open for 5% of the time, Pallas kernels for 19%

profile of v4, /device:TPU:7, one launch (start us, length us, event | category | flops | bytes accessed | tf_op | source)
XLA Modules:
  0.0 47.0 jit_solution(839928961846325035)
XLA Ops:
  0.0 0.0 copy-start.1
  0.0 1.6 %multiply_bitcast_fusion = bf16[4,2,8,4096]{3,1,0,2:T(2,128)(2,1)S(1)} fusion(bf16[8,4,2,8192]{3,2,1,0:T(2,128)(2,1)} %param.3, s32[]{:T(128)S(6)} %select_n.36, bf16[]{:T(256)} %constant.43.clone.1), kind=kLoop, calls=%fused_computation.3 | loop fusion | flops 1048576 | bytes 1048582 | tf_op jit(solution)/shard_map/mul | solution.py:308
  1.6 0.0 copy-start
  1.6 0.3 copy.18
  1.9 0.0 copy-done.1
  1.9 0.0 copy-start.2
  2.0 0.1 broadcast_in_dim.29
  2.1 0.1 broadcast_in_dim.30.refs_7_
  2.2 0.7 %collective-permute-start.1 = (bf16[4,16,4224]{2,1,0:T(8,128)(2,1)S(1)}, bf16[4,16,4224]{2,1,0:T(8,128)(2,1)S(1)}, u32[]{:S(2)}, u32[]{:S(2)}) collective-permute-start(bf16[4,16,4224]{2,1,0:T(8,128)(2,1)S(1)} %pad_maximum_fusion), channel_id=1, source_target_pairs={{0,1},{1,0},{2,3},{3,2},{4,5},{5,4},{6,7},{7,6},{8,9},{9,8},{10,11... | collective-permute-start | bytes 1622024 | tf_op jit(solution)/shard_map/ppermute | solution.py:21
  2.9 0.0 copy-done
  2.9 0.3 multiply_bitcast_fusion.1
  3.2 0.2 copy.19
  3.3 0.3 collective-permute-start.4
  3.6 0.0 copy-done.2
  3.6 0.8 %collective-permute-start = (s32[2,2]{1,0:T(2,128)S(1)}, s32[2,2]{1,0:T(2,128)S(1)}, u32[]{:S(2)}, u32[]{:S(2)}) collective-permute-start(s32[2,2]{1,0:T(2,128)S(1)} %copy-done.2), channel_id=1, source_target_pairs={{0,1},{1,0},{2,3},{3,2},{4,5},{5,4},{6,7},{7,6},{8,9},{9,8},{10,11... | collective-permute-start | bytes 56 | tf_op jit(solution)/shard_map/ppermute | solution.py:21
  4.5 0.2 multiply_bitcast_fusion.2
  4.7 0.1 copy.21
  4.8 0.1 copy.20
  4.9 0.4 collective-permute-done
  5.3 0.0 collective-permute-done.1.refs_2_
  5.4 0.1 broadcast_in_dim.31
  5.5 1.3 %collective-permute-start.5 = (bf16[4,16,2176]{2,1,0:T(8,128)(2,1)S(1)}, bf16[4,16,2176]{2,1,0:T(8,128)(2,1)S(1)}, u32[]{:S(2)}, u32[]{:S(2)}) collective-permute-start(bf16[4,16,2176]{2,1,0:T(8,128)(2,1)S(1)} %pad_maximum_fusion.1), channel_id=1, source_target_pairs={{0,2},{1,3},{2,0},{3,1},{4,6},{5,7},{6,4},{7,5},{8,10},{9,11},{10,... | collective-permute-start | bytes 835592 | tf_op jit(solution)/shard_map/ppermute | solution.py:21
  6.9 0.3 collective-permute-start.8
  7.1 1.2 %collective-permute-start.2 = (bf16[2,4,16,1024]{3,2,1,0:T(8,128)(2,1)S(1)}, bf16[2,4,16,1024]{3,2,1,0:T(8,128)(2,1)S(1)}, u32[]{:S(2)}, u32[]{:S(2)}) collective-permute-start(bf16[2,4,16,1024]{3,2,1,0:T(8,128)(2,1)S(1)} %pad_maximum_fusion.2), channel_id=1, source_target_pairs={{0,2},{1,3},{2,0},{3,1},{4,6},{5,7},{6,4},{7,5},{8,10},{9,11},{10,... | collective-permute-start | bytes 786440 | tf_op jit(solution)/shard_map/ppermute | solution.py:21
  8.4 0.1 pad_add_fusion.1.refs_0_
  8.5 2.3 %collective-permute-done.4.refs_3_ = bf16[4,16,2048]{2,1,0:T(8,128)(2,1)S(1)} collective-permute-done((bf16[4,16,2048]{2,1,0:T(8,128)(2,1)S(1)}, bf16[4,16,2048]{2,1,0:T(8,128)(2,1)S(1)}, u32[]{:S(2)}, u32[]{:S(2)}) %collective-permute-start.4) | collective-permute-done | bytes 262176 | tf_op jit(solution)/shard_map/ppermute | solution.py:21
  10.7 3.3 %collective-permute-start.6 = (bf16[4,16,2048]{2,1,0:T(8,128)(2,1)S(1)}, bf16[4,16,2048]{2,1,0:T(8,128)(2,1)S(1)}, u32[]{:S(2)}, u32[]{:S(2)}) collective-permute-start(bf16[4,16,2048]{2,1,0:T(8,128)(2,1)S(1)} %collective-permute-done.4.refs_3_), channel_id=1, source_target_pairs={{0,4},{1,5},{2,14},{3,15},{4,8},{5,9},{6,2},{7,3},{8,12},{9,13},{1... | collective-permute-start | bytes 786440 | tf_op jit(solution)/shard_map/ppermute | solution.py:21
  14.0 2.6 %collective-permute-done.5.refs_4_ = bf16[4,16,2176]{2,1,0:T(8,128)(2,1)S(1)} collective-permute-done((bf16[4,16,2176]{2,1,0:T(8,128)(2,1)S(1)}, bf16[4,16,2176]{2,1,0:T(8,128)(2,1)S(1)}, u32[]{:S(2)}, u32[]{:S(2)}) %collective-permute-start.5) | collective-permute-done | bytes 278560 | tf_op jit(solution)/shard_map/ppermute | solution.py:21
  16.7 3.3 %collective-permute-start.7 = (bf16[4,16,2176]{2,1,0:T(8,128)(2,1)S(1)}, bf16[4,16,2176]{2,1,0:T(8,128)(2,1)S(1)}, u32[]{:S(2)}, u32[]{:S(2)}) collective-permute-start(bf16[4,16,2176]{2,1,0:T(8,128)(2,1)S(1)} %collective-permute-done.5.refs_4_), channel_id=1, source_target_pairs={{0,4},{1,5},{2,14},{3,15},{4,8},{5,9},{6,2},{7,3},{8,12},{9,13},{1... | collective-permute-start | bytes 835592 | tf_op jit(solution)/shard_map/ppermute | solution.py:21
  20.0 2.3 %collective-permute-done.8.refs_3_ = bf16[2,4,16,1024]{3,2,1,0:T(8,128)(2,1)S(1)} collective-permute-done((bf16[2,4,16,1024]{3,2,1,0:T(8,128)(2,1)S(1)}, bf16[2,4,16,1024]{3,2,1,0:T(8,128)(2,1)S(1)}, u32[]{:S(2)}, u32[]{:S(2)}) %collective-permute-start.8) | collective-permute-done | bytes 262176 | tf_op jit(solution)/shard_map/ppermute | solution.py:21
  22.3 3.3 %collective-permute-start.9 = (bf16[2,4,16,1024]{3,2,1,0:T(8,128)(2,1)S(1)}, bf16[2,4,16,1024]{3,2,1,0:T(8,128)(2,1)S(1)}, u32[]{:S(2)}, u32[]{:S(2)}) collective-permute-start(bf16[2,4,16,1024]{3,2,1,0:T(8,128)(2,1)S(1)} %collective-permute-done.8.refs_3_), channel_id=1, source_target_pairs={{0,4},{1,5},{2,14},{3,15},{4,8},{5,9},{6,2},{7,3},{8,12},{9,13},{1... | collective-permute-start | bytes 786440 | tf_op jit(solution)/shard_map/ppermute | solution.py:21
  25.6 2.3 %collective-permute-done.2.refs_3_ = bf16[2,4,16,1024]{3,2,1,0:T(8,128)(2,1)S(1)} collective-permute-done((bf16[2,4,16,1024]{3,2,1,0:T(8,128)(2,1)S(1)}, bf16[2,4,16,1024]{3,2,1,0:T(8,128)(2,1)S(1)}, u32[]{:S(2)}, u32[]{:S(2)}) %collective-permute-start.2) | collective-permute-done | bytes 262176 | tf_op jit(solution)/shard_map/ppermute | solution.py:21
  27.9 4.6 %collective-permute-start.3 = (bf16[2,4,16,1024]{3,2,1,0:T(8,128)(2,1)S(1)}, bf16[2,4,16,1024]{3,2,1,0:T(8,128)(2,1)S(1)}, u32[]{:S(2)}, u32[]{:S(2)}) collective-permute-start(bf16[2,4,16,1024]{3,2,1,0:T(8,128)(2,1)S(1)} %collective-permute-done.2.refs_3_), channel_id=1, source_target_pairs={{0,4},{1,5},{2,0},{3,14},{4,8},{5,9},{6,2},{7,3},{8,12},{9,13},{10... | collective-permute-start | bytes 786440 | tf_op jit(solution)/shard_map/ppermute | solution.py:21
  32.5 1.1 %fusion.11 = (f32[64,512]{1,0:T(8,128)S(1)}, f32[64,512]{1,0:T(8,128)S(1)}, f32[64,512]{1,0:T(8,128)S(1)}, f32[64,512]{1,0:T(8,128)S(1)}) fusion(s32[512]{0:T(512)S(1)} %iota_add_fusion, s32[64]{0:T(128)S(1)} %multiply_add_fusion), kind=kLoop, calls=%fused_computation.36 | loop fusion | flops 917504 | bytes 526592 | tf_op jit(solution)/shard_map/sin | solution.py:28
  33.6 2.2 %tables.1 = (bf16[4096,512]{1,0:T(8,128)(2,1)S(1)}, bf16[4096,512]{1,0:T(8,128)(2,1)S(1)}) custom-call(f32[64,512]{1,0:T(8,128)S(1)} %get-tuple-element.34.fine_cos, f32[64,512]{1,0:T(8,128)S(1)} %get-tuple-element.33.fine_sin, f32[64,512]{1,0:T(8,128)S(1)} %get-tuple-element.32.coarse_cos, f32[64,512]{1,0:T(8,128)S(1)} %get-tuple-element.31.coarse_sin), custom_call_target="tpu_custom_call" | custom-call | flops 12582912 | bytes 8388608 | tf_op jit(solution)/shard_map/tables/pallas_call | solution.py:51
  35.9 0.0 collective-permute-done.6.refs_5_
  35.9 0.0 collective-permute-done.7.refs_6_
  35.9 2.2 %shard_map.37 = (f32[256,1152]{1,0:T(8,128)S(1)}, f32[256,128]{1,0:T(8,128)S(1)}, f32[6,4,8,128]{3,2,1,0:T(8,128)S(1)}) custom-call(s32[4,3]{1,0:T(4,128)S(1)} %pad_add_fusion.1.refs_0_, bf16[4,16,2048]{2,1,0:T(8,128)(2,1)S(1)} %bitcast.33, bf16[4,16,4224]{2,1,0:T(8,128)(2,1)S(1)} %collective-permute-done.1.refs_2_, ...), custom_call_target="tpu_custom_call" | custom-call | flops 536870912 | bytes 2097152 | tf_op jit(solution)/shard_map/pallas_call | solution.py:244
  38.0 2.2 %shard_map.38.refs_8_ = f32[256,1152]{1,0:T(8,128)S(1)} custom-call(s32[4,3]{1,0:T(4,128)S(1)} %pad_add_fusion.1.refs_0_, bf16[4,16,2048]{2,1,0:T(8,128)(2,1)S(1)} %bitcast.34, bf16[4,16,4224]{2,1,0:T(8,128)(2,1)S(1)} %collective-permute-done.1.refs_2_, bf16[4,16,2048]{2,1,0:T(8,128)(2,1)S(1)} %collective-permute-done.4.refs_3_, ...), custom_call_target="tpu_custom_call", output_to_operand_aliasing={{}: (10, {})} | custom-call | flops 536870912 | bytes 2097152 | tf_op jit(solution)/shard_map/pallas_call | solution.py:244
  40.2 0.0 collective-permute-done.9.refs_4_
  40.2 2.1 %shard_map.39.refs_8_ = f32[256,1152]{1,0:T(8,128)S(1)} custom-call(s32[4,3]{1,0:T(4,128)S(1)} %pad_add_fusion.1.refs_0_, bf16[4,16,1024]{2,1,0:T(8,128)(2,1)S(1)} %bitcast.38, bf16[4,16,4224]{2,1,0:T(8,128)(2,1)S(1)} %collective-permute-done.1.refs_2_, bf16[2,4,16,1024]{3,2,1,0:T(8,128)(2,1)S(1)} %collective-permute-done.8.refs_3_, ...), custom_call_target="tpu_custom_call", output_to_operand_aliasing={{}: (8, {})} | custom-call | flops 536870912 | bytes 2097152 | tf_op jit(solution)/shard_map/pallas_call | solution.py:244
  42.3 0.0 collective-permute-done.3.refs_4_
  42.4 2.2 %shard_map.40 = (f32[128,1152]{1,0:T(8,128)S(1)}, bf16[128,1024]{1,0:T(8,128)(2,1)S(1)}) custom-call(s32[4,3]{1,0:T(4,128)S(1)} %pad_add_fusion.1.refs_0_, bf16[4,16,1024]{2,1,0:T(8,128)(2,1)S(1)} %bitcast.36, bf16[4,16,4224]{2,1,0:T(8,128)(2,1)S(1)} %collective-permute-done.1.refs_2_, bf16[2,4,16,1024]{3,2,1,0:T(8,128)(2,1)S(1)} %collective-permute-done.2.refs_3_, ...), custom_call_target="tpu_custom_call" | custom-call | flops 536870912 | bytes 2097152 | tf_op jit(solution)/shard_map/pallas_call | solution.py:244
  44.6 0.1 collective-permute-start.10
  44.7 0.3 mine.1
  45.0 1.2 %collective-permute-done.10 = bf16[128,1024]{1,0:T(8,128)(2,1)S(1)} collective-permute-done((bf16[128,1024]{1,0:T(8,128)(2,1)S(1)}, bf16[128,1024]{1,0:T(8,128)(2,1)S(1)}, u32[]{:S(2)}, u32[]{:S(2)}) %collective-permute-start.10) | collective-permute-done | bytes 262176 | tf_op jit(solution)/shard_map/ppermute | solution.py:21
  46.2 0.8 %add_convert_fusion = bf16[128,1024]{1,0:T(8,128)(2,1)} fusion(f32[128,1024]{1,0:T(8,128)S(1)} %mine.1, bf16[128,1024]{1,0:T(8,128)(2,1)S(1)} %collective-permute-done.10), kind=kLoop, calls=%fused_computation.2 | loop fusion | flops 393216 | bytes 1048576 | tf_op jit(solution)/shard_map/convert_element_type | solution.py:368
  (13 shorter events, 0.2 us)
Async XLA Ops:
  0.0 1.9 %copy-start.1 = (s32[8,4]{0,1:T(4,128)S(1)}, s32[8,4]{0,1:T(4,128)}, u32[]{:S(2)}) copy-start(s32[8,4]{0,1:T(4,128)} %param.4) | copy-start | bytes 388
  1.6 1.3 %copy-start = (bf16[8,4,2,8192]{3,2,1,0:T(2,128)(2,1)S(1)}, bf16[8,4,2,8192]{3,2,1,0:T(2,128)(2,1)}, u32[]{:S(2)}) copy-start(bf16[8,4,2,8192]{3,2,1,0:T(2,128)(2,1)} %param.3) | copy-start | bytes 3145732
  1.9 1.7 %copy-start.2 = (s32[2,2]{1,0:T(2,128)S(1)}, s32[2,2]{1,0:T(2,128)}, u32[]{:S(2)}) copy-start(s32[2,2]{1,0:T(2,128)} %param.5) | copy-start | bytes 52
  2.2 3.1 %collective-permute-start.1 = (bf16[4,16,4224]{2,1,0:T(8,128)(2,1)S(1)}, bf16[4,16,4224]{2,1,0:T(8,128)(2,1)S(1)}, u32[]{:S(2)}, u32[]{:S(2)}) collective-permute-start(bf16[4,16,4224]{2,1,0:T(8,128)(2,1)S(1)} %pad_maximum_fusion), channel_id=1, source_target_pairs={{0,1},{1,0},{2,3},{3,2},{4,5},{5,4},{6,7},{7,6},{8,9},{9,8},{10,11... | collective-permute-start | bytes 1622024 | tf_op jit(solution)/shard_map/ppermute | solution.py:21
  3.3 7.4 %collective-permute-start.4 = (bf16[4,16,2048]{2,1,0:T(8,128)(2,1)S(1)}, bf16[4,16,2048]{2,1,0:T(8,128)(2,1)S(1)}, u32[]{:S(2)}, u32[]{:S(2)}) collective-permute-start(bf16[4,16,2048]{2,1,0:T(8,128)(2,1)S(1)} %bitcast.32), channel_id=1, source_target_pairs={{0,2},{1,3},{2,0},{3,1},{4,6},{5,7},{6,4},{7,5},{8,10},{9,11},{10,... | collective-permute-start | bytes 786440 | tf_op jit(solution)/shard_map/ppermute | solution.py:21
  3.6 1.7 %collective-permute-start = (s32[2,2]{1,0:T(2,128)S(1)}, s32[2,2]{1,0:T(2,128)S(1)}, u32[]{:S(2)}, u32[]{:S(2)}) collective-permute-start(s32[2,2]{1,0:T(2,128)S(1)} %copy-done.2), channel_id=1, source_target_pairs={{0,1},{1,0},{2,3},{3,2},{4,5},{5,4},{6,7},{7,6},{8,9},{9,8},{10,11... | collective-permute-start | bytes 56 | tf_op jit(solution)/shard_map/ppermute | solution.py:21
  5.5 11.2 %collective-permute-start.5 = (bf16[4,16,2176]{2,1,0:T(8,128)(2,1)S(1)}, bf16[4,16,2176]{2,1,0:T(8,128)(2,1)S(1)}, u32[]{:S(2)}, u32[]{:S(2)}) collective-permute-start(bf16[4,16,2176]{2,1,0:T(8,128)(2,1)S(1)} %pad_maximum_fusion.1), channel_id=1, source_target_pairs={{0,2},{1,3},{2,0},{3,1},{4,6},{5,7},{6,4},{7,5},{8,10},{9,11},{10,... | collective-permute-start | bytes 835592 | tf_op jit(solution)/shard_map/ppermute | solution.py:21
  6.9 15.5 %collective-permute-start.8 = (bf16[2,4,16,1024]{3,2,1,0:T(8,128)(2,1)S(1)}, bf16[2,4,16,1024]{3,2,1,0:T(8,128)(2,1)S(1)}, u32[]{:S(2)}, u32[]{:S(2)}) collective-permute-start(bf16[2,4,16,1024]{3,2,1,0:T(8,128)(2,1)S(1)} %pad_maximum_fusion.3), channel_id=1, source_target_pairs={{0,2},{1,3},{2,0},{3,1},{4,6},{5,7},{6,4},{7,5},{8,10},{9,11},{10,... | collective-permute-start | bytes 786440 | tf_op jit(solution)/shard_map/ppermute | solution.py:21
  7.1 20.8 %collective-permute-start.2 = (bf16[2,4,16,1024]{3,2,1,0:T(8,128)(2,1)S(1)}, bf16[2,4,16,1024]{3,2,1,0:T(8,128)(2,1)S(1)}, u32[]{:S(2)}, u32[]{:S(2)}) collective-permute-start(bf16[2,4,16,1024]{3,2,1,0:T(8,128)(2,1)S(1)} %pad_maximum_fusion.2), channel_id=1, source_target_pairs={{0,2},{1,3},{2,0},{3,1},{4,6},{5,7},{6,4},{7,5},{8,10},{9,11},{10,... | collective-permute-start | bytes 786440 | tf_op jit(solution)/shard_map/ppermute | solution.py:21
  10.7 25.1 %collective-permute-start.6 = (bf16[4,16,2048]{2,1,0:T(8,128)(2,1)S(1)}, bf16[4,16,2048]{2,1,0:T(8,128)(2,1)S(1)}, u32[]{:S(2)}, u32[]{:S(2)}) collective-permute-start(bf16[4,16,2048]{2,1,0:T(8,128)(2,1)S(1)} %collective-permute-done.4.refs_3_), channel_id=1, source_target_pairs={{0,4},{1,5},{2,14},{3,15},{4,8},{5,9},{6,2},{7,3},{8,12},{9,13},{1... | collective-permute-start | bytes 786440 | tf_op jit(solution)/shard_map/ppermute | solution.py:21
  16.7 19.2 %collective-permute-start.7 = (bf16[4,16,2176]{2,1,0:T(8,128)(2,1)S(1)}, bf16[4,16,2176]{2,1,0:T(8,128)(2,1)S(1)}, u32[]{:S(2)}, u32[]{:S(2)}) collective-permute-start(bf16[4,16,2176]{2,1,0:T(8,128)(2,1)S(1)} %collective-permute-done.5.refs_4_), channel_id=1, source_target_pairs={{0,4},{1,5},{2,14},{3,15},{4,8},{5,9},{6,2},{7,3},{8,12},{9,13},{1... | collective-permute-start | bytes 835592 | tf_op jit(solution)/shard_map/ppermute | solution.py:21
  22.3 17.9 %collective-permute-start.9 = (bf16[2,4,16,1024]{3,2,1,0:T(8,128)(2,1)S(1)}, bf16[2,4,16,1024]{3,2,1,0:T(8,128)(2,1)S(1)}, u32[]{:S(2)}, u32[]{:S(2)}) collective-permute-start(bf16[2,4,16,1024]{3,2,1,0:T(8,128)(2,1)S(1)} %collective-permute-done.8.refs_3_), channel_id=1, source_target_pairs={{0,4},{1,5},{2,14},{3,15},{4,8},{5,9},{6,2},{7,3},{8,12},{9,13},{1... | collective-permute-start | bytes 786440 | tf_op jit(solution)/shard_map/ppermute | solution.py:21
  27.9 14.4 %collective-permute-start.3 = (bf16[2,4,16,1024]{3,2,1,0:T(8,128)(2,1)S(1)}, bf16[2,4,16,1024]{3,2,1,0:T(8,128)(2,1)S(1)}, u32[]{:S(2)}, u32[]{:S(2)}) collective-permute-start(bf16[2,4,16,1024]{3,2,1,0:T(8,128)(2,1)S(1)} %collective-permute-done.2.refs_3_), channel_id=1, source_target_pairs={{0,4},{1,5},{2,0},{3,14},{4,8},{5,9},{6,2},{7,3},{8,12},{9,13},{10... | collective-permute-start | bytes 786440 | tf_op jit(solution)/shard_map/ppermute | solution.py:21
  44.6 1.6 %collective-permute-start.10 = (bf16[128,1024]{1,0:T(8,128)(2,1)S(1)}, bf16[128,1024]{1,0:T(8,128)(2,1)S(1)}, u32[]{:S(2)}, u32[]{:S(2)}) collective-permute-start(bf16[128,1024]{1,0:T(8,128)(2,1)S(1)} %get-tuple-element.22), channel_id=1, source_target_pairs={{0,1},{1,0},{2,3},{3,2},{4,5},{5,4},{6,7},{7,6},{8,9},{9,8},{10,11... | collective-permute-start | bytes 786440 | tf_op jit(solution)/shard_map/ppermute | solution.py:21

commit v5 on v4

--- a/solution.py
+++ b/solution.py
@@ -93,11 +93,10 @@
     lag_half = out_ref.shape[1] // 2
     size = 256
     flip = flip_matrix(size)
-    at = pl.ds(start, rows)
-    even = acc_ref[at, :lag_half]
-    odd = acc_ref[at, lag_half : 2 * lag_half]
-    weight = weight_ref[at, :][:, :1]
-    still = jnp.sum(acc_ref[at, 2 * lag_half :], axis=1, keepdims=True)
+    even = acc_ref[:, :lag_half]
+    odd = acc_ref[:, lag_half : 2 * lag_half]
+    weight = weight_ref[start : start + rows, :][:, :1]
+    still = jnp.sum(acc_ref[:, 2 * lag_half :], axis=1, keepdims=True)
     lane = lax.broadcasted_iota(jnp.int32, (rows, lag_half), 1)
     right = jnp.where(lane == 0, still, pltpu.roll(even - odd, 1, 1))
     out_ref[:, lag_half:] = (right * weight).astype(out_ref.dtype)
@@ -113,7 +112,7 @@
         out_ref[:, lag_half - lane - size : lag_half - lane] = flipped.astype(out_ref.dtype)
 
 
-def chunk_kernel(*refs, views_at, slot_count, windows, stations, first, last, low, norm):
+def chunk_kernel(*refs, views_at, slot_count, slot_base, windows, stations, first, last, low, norm):
     refs = list(refs)
     slots_ref = refs.pop(0)
     sources = [refs.pop(0) for _ in range(1 + max(which for which, _, _ in views_at))]
@@ -122,7 +121,7 @@
     if not first:
         before_ref = refs.pop(0)
     if last:
-        weight_ref, mine_ref, theirs_ref = (refs.pop(0) for _ in range(3))
+        weight_ref, out_ref = (refs.pop(0) for _ in range(2))
         acc_ref = refs.pop()
     else:
         acc_ref = refs.pop(0)
@@ -136,6 +135,7 @@
     pairs = stations * stations
     width = buffers[0][0].shape[1]
     wide = 256
+    held_rows = slice(slot_base * pairs, (slot_base + slot_count) * pairs)
 
     if not first:
         marks = mark_source
@@ -143,7 +143,7 @@
         pair_weights(slots_ref, [mark_source, sources[1], sources[3], sources[5]], marks, weight_ref, slot_count, windows, stations, norm)
         acc_ref[:, 2 * lag_half :] = jnp.zeros((slot_count * pairs, LANES), jnp.float32)
     else:
-        acc_ref[:, 2 * lag_half :] = before_ref[:, 2 * lag_half :]
+        acc_ref[:, 2 * lag_half :] = before_ref[held_rows, 2 * lag_half :]
 
     for at, (which, part, lane) in enumerate(views_at):
         view = sources[which] if part is None else sources[which].at[part]
@@ -154,7 +154,7 @@
                 piece = view[window, :, lane + start : lane + start + LANES]
                 stage[at, window, :, start : start + LANES] = piece.astype(jnp.float32) * mark
 
-    index = [(slots_ref[slot, 0], slots_ref[slot, 1]) for slot in range(slot_count)]
+    index = [(slots_ref[slot_base + slot, 0], slots_ref[slot_base + slot, 1]) for slot in range(slot_count)]
 
     def cross(start, real_rows, imag_rows):
         for slot in range(slot_count):
@@ -202,7 +202,7 @@
             if start > 0:
                 value = value + acc_ref[:, lanes]
             elif not first:
-                value = value + before_ref[:, lanes]
+                value = value + before_ref[held_rows, lanes]
             acc_ref[:, lanes] = value
 
     steps = count // width
@@ -212,13 +212,10 @@
             gather_lags((step - 1) * width, *buffers[(step - 1) % 2])
     gather_lags((steps - 1) * width, *buffers[(steps - 1) % 2])
     if last:
-        half = slot_count * pairs // 2
-        lay_out(acc_ref, weight_ref, theirs_ref, half)
-        mine_ref[...] = acc_ref[:half, :]
-
-
-def chunk_call(slots, sources, views_at, mark_source, tables, before, weights, last, low, count, width, windows, stations, norm):
-    slot_count = slots.shape[0]
+        lay_out(acc_ref, weight_ref, out_ref, slot_base * pairs)
+
+
+def chunk_call(slots, sources, views_at, mark_source, tables, before, weights, last, slot_base, slot_count, low, count, width, windows, stations, norm):
     lag_half = tables[0].shape[1]
     rows = slot_count * stations * stations
     first = before is None
@@ -236,16 +233,14 @@
         outs.append(jax.ShapeDtypeStruct((rows, LANES), jnp.float32))
         outs.append(jax.ShapeDtypeStruct((6, windows, stations, LANES), jnp.float32))
     if last:
-        outs = [
-            jax.ShapeDtypeStruct((rows // 2, 2 * lag_half + LANES), jnp.float32),
-            jax.ShapeDtypeStruct((rows // 2, 2 * lag_half), jnp.bfloat16),
-        ]
+        outs = [jax.ShapeDtypeStruct((rows, 2 * lag_half), last)]
         scratch.append(pltpu.VMEM(acc.shape, jnp.float32))
     return pl.pallas_call(
         functools.partial(
             chunk_kernel,
             views_at=views_at,
             slot_count=slot_count,
+            slot_base=slot_base,
             windows=windows,
             stations=stations,
             first=first,
@@ -263,27 +258,6 @@
         ),
         compiler_params=pltpu.CompilerParams(vmem_limit_bytes=GRANT),
     )(slots, *operands)
-
-
-def mine_kernel(acc_ref, weight_ref, out_ref):
-    lay_out(acc_ref, weight_ref, out_ref, 0)
-
-
-def mine_call(mine, weights):
-    rows = mine.shape[0]
-    lag_count = mine.shape[1] - LANES
-    vmem = pl.BlockSpec(memory_space=pltpu.VMEM)
-    return pl.pallas_call(
-        mine_kernel,
-        in_specs=[vmem] * 2,
-        out_specs=vmem,
-        out_shape=jax.ShapeDtypeStruct((rows, lag_count), jnp.float32),
-        compiler_params=pltpu.CompilerParams(vmem_limit_bytes=GRANT),
-        cost_estimate=pl.CostEstimate(
-            flops=2 * rows * lag_count * 256, bytes_accessed=8 * rows * lag_count, transcendentals=0
-        ),
-        name="mine",
-    )(mine, weights)
 
 
 def owner_stacks(spectra, window_mask, pair_slots):
@@ -355,17 +329,22 @@
             sources = [own[at - 1], par, near[at + 1], far[at + 1]]
             views_at = [(0, None, 0), (1, None, LANES + low), (2, 0, 0), (2, 1, 0), (3, 0, 0), (3, 1, 0)]
         width = SUB // 2 if last or (high - low) % SUB else SUB
-        made = chunk_call(
-            table, sources, views_at, mark_source, tables, acc, weights, last, low, high - low, width, windows, stations, norm
-        )
-        if unit == 0:
-            acc, weights, mark_source = made
-        elif not last:
-            (acc,) = made
+
+        def part(kind, slot_base, slots_here):
+            return chunk_call(
+                table, sources, views_at, mark_source, tables, acc, weights, kind,
+                slot_base, slots_here, low, high - low, width, windows, stations, norm,
+            )
+
+        if last:
+            (theirs,) = part(jnp.bfloat16, slot_count, slot_count)
+            other = permute(theirs, core_pairs)
+            (mine,) = part(jnp.float32, 0, slot_count)
+        elif unit == 0:
+            acc, weights, mark_source = part(None, 0, 2 * slot_count)
         else:
-            mine, theirs = made
-    other = permute(theirs, core_pairs)
-    out = (mine_call(mine, weights) + other.astype(jnp.float32)).astype(jnp.bfloat16)
+            (acc,) = part(None, 0, 2 * slot_count)
+    out = (mine + other.astype(jnp.float32)).astype(jnp.bfloat16)
     return out.reshape(slot_count, stations, stations, LAGS)
 
 

time: 47.1 us -> 46.7 us (level)
  waiting for transfers between devices: 11.1 us -> 9.9 us
  Pallas kernels: 11.2 us -> 12 us
    ppermute x11, waiting for transfers between devices: 11.1 us -> 9.9 us  [permute(): return lax.ppermute(array, 'sta', pairs)]
    pallas_call x4 -> x5, Pallas kernels: 8.7 us -> 9.8 us  [chunk_call(): pl.pallas_call(functools.partial(chunk_kernel, views_at=views_at, slot_co...]
  transfers between devices with their start and end apart: 11 -> 11, of which waited for: 6 -> 5; matrix products, arithmetic and copies ran while one was open for 5% -> 5% of each run, Pallas kernels for 19% -> 22%
where the time goes in v5:
time: 46.7 us; the launch traced here: 46.6 us
  starting transfers between devices  19.4 us (42%)
  Pallas kernels  12 us (26%)
  waiting for transfers between devices  9.9 us (21%)
  other arithmetic  4.14 us (9%)
  local copies, waits for them, and re-layouts  0.9 us (2%)
    ppermute x11, starting transfers between devices, permute(): return lax.ppermute(array, 'sta', pairs)  19.4 us
    ppermute x11, waiting for transfers between devices, permute(): return lax.ppermute(array, 'sta', pairs)  9.9 us
    pallas_call x5, Pallas kernels, chunk_call(): pl.pallas_call(functools.partial(chunk_kernel, views_at=views_at, slot_co...  9.8 us
    pallas_call x1, Pallas kernels, lag_tables(): pl.pallas_call(table_kernel, in_specs=[vmem] * 4, out_specs=[vmem] * 2, o...  2.24 us
    mul x3, other arithmetic, rows_of(): piece.transpose(1, 2, 0, 3) * unit_scale  2.09 us
    sin x1, other arithmetic, angle_tables(): return (jnp.cos(phase_angle), jnp.sin(phase_angle))  1.06 us
  transfers between devices with their start and end apart: 11, of which 5 were waited for; matrix products, arithmetic and copies ran while one was open for 5% of the time, Pallas kernels for 22%

profile of v5, /device:TPU:7, one launch (start us, length us, event | category | flops | bytes accessed | tf_op | source)
XLA Modules:
  0.0 46.6 jit_solution(10265848137758088986)
XLA Ops:
  0.0 0.0 copy-start.1
  0.0 1.6 %multiply_bitcast_fusion = bf16[4,2,8,4096]{3,1,0,2:T(2,128)(2,1)S(1)} fusion(bf16[8,4,2,8192]{3,2,1,0:T(2,128)(2,1)} %param.3, s32[]{:T(128)S(6)} %select_n.36, bf16[]{:T(256)} %constant.43.clone.1), kind=kLoop, calls=%fused_computation.3 | loop fusion | flops 1048576 | bytes 1048582 | tf_op jit(solution)/shard_map/mul | solution.py:282
  1.6 0.0 copy-start
  1.6 0.3 copy.18
  1.9 0.0 copy-done.1
  1.9 0.0 copy-start.2
  2.0 0.1 broadcast_in_dim.29
  2.1 0.1 broadcast_in_dim.30.refs_7_
  2.2 0.7 %collective-permute-start.1 = (bf16[4,16,4224]{2,1,0:T(8,128)(2,1)S(1)}, bf16[4,16,4224]{2,1,0:T(8,128)(2,1)S(1)}, u32[]{:S(2)}, u32[]{:S(2)}) collective-permute-start(bf16[4,16,4224]{2,1,0:T(8,128)(2,1)S(1)} %pad_maximum_fusion), channel_id=1, source_target_pairs={{0,1},{1,0},{2,3},{3,2},{4,5},{5,4},{6,7},{7,6},{8,9},{9,8},{10,11... | collective-permute-start | bytes 1622024 | tf_op jit(solution)/shard_map/ppermute | solution.py:21
  2.9 0.0 copy-done
  2.9 0.3 multiply_bitcast_fusion.1
  3.2 0.2 copy.19
  3.3 0.3 collective-permute-start.4
  3.6 0.0 copy-done.2
  3.6 0.8 %collective-permute-start = (s32[2,2]{1,0:T(2,128)S(1)}, s32[2,2]{1,0:T(2,128)S(1)}, u32[]{:S(2)}, u32[]{:S(2)}) collective-permute-start(s32[2,2]{1,0:T(2,128)S(1)} %copy-done.2), channel_id=1, source_target_pairs={{0,1},{1,0},{2,3},{3,2},{4,5},{5,4},{6,7},{7,6},{8,9},{9,8},{10,11... | collective-permute-start | bytes 56 | tf_op jit(solution)/shard_map/ppermute | solution.py:21
  4.5 0.2 multiply_bitcast_fusion.2
  4.7 0.1 copy.21
  4.8 0.1 copy.20
  4.9 0.4 collective-permute-done
  5.3 0.0 collective-permute-done.1.refs_2_
  5.4 0.1 broadcast_in_dim.31
  5.5 1.3 %collective-permute-start.5 = (bf16[4,16,2176]{2,1,0:T(8,128)(2,1)S(1)}, bf16[4,16,2176]{2,1,0:T(8,128)(2,1)S(1)}, u32[]{:S(2)}, u32[]{:S(2)}) collective-permute-start(bf16[4,16,2176]{2,1,0:T(8,128)(2,1)S(1)} %pad_maximum_fusion.1), channel_id=1, source_target_pairs={{0,2},{1,3},{2,0},{3,1},{4,6},{5,7},{6,4},{7,5},{8,10},{9,11},{10,... | collective-permute-start | bytes 835592 | tf_op jit(solution)/shard_map/ppermute | solution.py:21
  6.9 0.3 collective-permute-start.8
  7.1 1.2 %collective-permute-start.2 = (bf16[2,4,16,1024]{3,2,1,0:T(8,128)(2,1)S(1)}, bf16[2,4,16,1024]{3,2,1,0:T(8,128)(2,1)S(1)}, u32[]{:S(2)}, u32[]{:S(2)}) collective-permute-start(bf16[2,4,16,1024]{3,2,1,0:T(8,128)(2,1)S(1)} %pad_maximum_fusion.2), channel_id=1, source_target_pairs={{0,2},{1,3},{2,0},{3,1},{4,6},{5,7},{6,4},{7,5},{8,10},{9,11},{10,... | collective-permute-start | bytes 786440 | tf_op jit(solution)/shard_map/ppermute | solution.py:21
  8.4 0.1 pad_add_fusion.1.refs_0_
  8.5 2.3 %collective-permute-done.4.refs_3_ = bf16[4,16,2048]{2,1,0:T(8,128)(2,1)S(1)} collective-permute-done((bf16[4,16,2048]{2,1,0:T(8,128)(2,1)S(1)}, bf16[4,16,2048]{2,1,0:T(8,128)(2,1)S(1)}, u32[]{:S(2)}, u32[]{:S(2)}) %collective-permute-start.4) | collective-permute-done | bytes 262176 | tf_op jit(solution)/shard_map/ppermute | solution.py:21
  10.7 3.3 %collective-permute-start.6 = (bf16[4,16,2048]{2,1,0:T(8,128)(2,1)S(1)}, bf16[4,16,2048]{2,1,0:T(8,128)(2,1)S(1)}, u32[]{:S(2)}, u32[]{:S(2)}) collective-permute-start(bf16[4,16,2048]{2,1,0:T(8,128)(2,1)S(1)} %collective-permute-done.4.refs_3_), channel_id=1, source_target_pairs={{0,4},{1,5},{2,14},{3,15},{4,8},{5,9},{6,2},{7,3},{8,12},{9,13},{1... | collective-permute-start | bytes 786440 | tf_op jit(solution)/shard_map/ppermute | solution.py:21
  14.0 2.6 %collective-permute-done.5.refs_4_ = bf16[4,16,2176]{2,1,0:T(8,128)(2,1)S(1)} collective-permute-done((bf16[4,16,2176]{2,1,0:T(8,128)(2,1)S(1)}, bf16[4,16,2176]{2,1,0:T(8,128)(2,1)S(1)}, u32[]{:S(2)}, u32[]{:S(2)}) %collective-permute-start.5) | collective-permute-done | bytes 278560 | tf_op jit(solution)/shard_map/ppermute | solution.py:21
  16.7 3.3 %collective-permute-start.7 = (bf16[4,16,2176]{2,1,0:T(8,128)(2,1)S(1)}, bf16[4,16,2176]{2,1,0:T(8,128)(2,1)S(1)}, u32[]{:S(2)}, u32[]{:S(2)}) collective-permute-start(bf16[4,16,2176]{2,1,0:T(8,128)(2,1)S(1)} %collective-permute-done.5.refs_4_), channel_id=1, source_target_pairs={{0,4},{1,5},{2,14},{3,15},{4,8},{5,9},{6,2},{7,3},{8,12},{9,13},{1... | collective-permute-start | bytes 835592 | tf_op jit(solution)/shard_map/ppermute | solution.py:21
  20.0 2.3 %collective-permute-done.8.refs_3_ = bf16[2,4,16,1024]{3,2,1,0:T(8,128)(2,1)S(1)} collective-permute-done((bf16[2,4,16,1024]{3,2,1,0:T(8,128)(2,1)S(1)}, bf16[2,4,16,1024]{3,2,1,0:T(8,128)(2,1)S(1)}, u32[]{:S(2)}, u32[]{:S(2)}) %collective-permute-start.8) | collective-permute-done | bytes 262176 | tf_op jit(solution)/shard_map/ppermute | solution.py:21
  22.3 3.3 %collective-permute-start.9 = (bf16[2,4,16,1024]{3,2,1,0:T(8,128)(2,1)S(1)}, bf16[2,4,16,1024]{3,2,1,0:T(8,128)(2,1)S(1)}, u32[]{:S(2)}, u32[]{:S(2)}) collective-permute-start(bf16[2,4,16,1024]{3,2,1,0:T(8,128)(2,1)S(1)} %collective-permute-done.8.refs_3_), channel_id=1, source_target_pairs={{0,4},{1,5},{2,14},{3,15},{4,8},{5,9},{6,2},{7,3},{8,12},{9,13},{1... | collective-permute-start | bytes 786440 | tf_op jit(solution)/shard_map/ppermute | solution.py:21
  25.6 2.3 %collective-permute-done.2.refs_3_ = bf16[2,4,16,1024]{3,2,1,0:T(8,128)(2,1)S(1)} collective-permute-done((bf16[2,4,16,1024]{3,2,1,0:T(8,128)(2,1)S(1)}, bf16[2,4,16,1024]{3,2,1,0:T(8,128)(2,1)S(1)}, u32[]{:S(2)}, u32[]{:S(2)}) %collective-permute-start.2) | collective-permute-done | bytes 262176 | tf_op jit(solution)/shard_map/ppermute | solution.py:21
  27.9 4.6 %collective-permute-start.3 = (bf16[2,4,16,1024]{3,2,1,0:T(8,128)(2,1)S(1)}, bf16[2,4,16,1024]{3,2,1,0:T(8,128)(2,1)S(1)}, u32[]{:S(2)}, u32[]{:S(2)}) collective-permute-start(bf16[2,4,16,1024]{3,2,1,0:T(8,128)(2,1)S(1)} %collective-permute-done.2.refs_3_), channel_id=1, source_target_pairs={{0,4},{1,5},{2,0},{3,14},{4,8},{5,9},{6,2},{7,3},{8,12},{9,13},{10... | collective-permute-start | bytes 786440 | tf_op jit(solution)/shard_map/ppermute | solution.py:21
  32.5 1.1 %fusion.11 = (f32[64,512]{1,0:T(8,128)S(1)}, f32[64,512]{1,0:T(8,128)S(1)}, f32[64,512]{1,0:T(8,128)S(1)}, f32[64,512]{1,0:T(8,128)S(1)}) fusion(s32[512]{0:T(512)S(1)} %iota_add_fusion, s32[64]{0:T(128)S(1)} %multiply_add_fusion), kind=kLoop, calls=%fused_computation.36 | loop fusion | flops 917504 | bytes 526592 | tf_op jit(solution)/shard_map/sin | solution.py:28
  33.6 2.2 %tables.1 = (bf16[4096,512]{1,0:T(8,128)(2,1)S(1)}, bf16[4096,512]{1,0:T(8,128)(2,1)S(1)}) custom-call(f32[64,512]{1,0:T(8,128)S(1)} %get-tuple-element.30.fine_cos, f32[64,512]{1,0:T(8,128)S(1)} %get-tuple-element.29.fine_sin, f32[64,512]{1,0:T(8,128)S(1)} %get-tuple-element.28.coarse_cos, f32[64,512]{1,0:T(8,128)S(1)} %get-tuple-element.27.coarse_sin), custom_call_target="tpu_custom_call" | custom-call | flops 12582912 | bytes 8388608 | tf_op jit(solution)/shard_map/tables/pallas_call | solution.py:51
  35.9 0.0 collective-permute-done.6.refs_5_
  35.9 0.0 collective-permute-done.7.refs_6_
  35.9 2.2 %shard_map.37 = (f32[256,1152]{1,0:T(8,128)S(1)}, f32[256,128]{1,0:T(8,128)S(1)}, f32[6,4,8,128]{3,2,1,0:T(8,128)S(1)}) custom-call(s32[4,3]{1,0:T(4,128)S(1)} %pad_add_fusion.1.refs_0_, bf16[4,16,2048]{2,1,0:T(8,128)(2,1)S(1)} %bitcast.33, bf16[4,16,4224]{2,1,0:T(8,128)(2,1)S(1)} %collective-permute-done.1.refs_2_, ...), custom_call_target="tpu_custom_call" | custom-call | flops 536870912 | bytes 2097152 | tf_op jit(solution)/shard_map/pallas_call | solution.py:238
  38.0 2.2 %shard_map.38.refs_8_ = f32[256,1152]{1,0:T(8,128)S(1)} custom-call(s32[4,3]{1,0:T(4,128)S(1)} %pad_add_fusion.1.refs_0_, bf16[4,16,2048]{2,1,0:T(8,128)(2,1)S(1)} %bitcast.34, bf16[4,16,4224]{2,1,0:T(8,128)(2,1)S(1)} %collective-permute-done.1.refs_2_, bf16[4,16,2048]{2,1,0:T(8,128)(2,1)S(1)} %collective-permute-done.4.refs_3_, ...), custom_call_target="tpu_custom_call", output_to_operand_aliasing={{}: (10, {})} | custom-call | flops 536870912 | bytes 2097152 | tf_op jit(solution)/shard_map/pallas_call | solution.py:238
  40.2 0.0 collective-permute-done.9.refs_4_
  40.2 2.1 %shard_map.39.refs_8_ = f32[256,1152]{1,0:T(8,128)S(1)} custom-call(s32[4,3]{1,0:T(4,128)S(1)} %pad_add_fusion.1.refs_0_, bf16[4,16,1024]{2,1,0:T(8,128)(2,1)S(1)} %bitcast.39, bf16[4,16,4224]{2,1,0:T(8,128)(2,1)S(1)} %collective-permute-done.1.refs_2_, bf16[2,4,16,1024]{3,2,1,0:T(8,128)(2,1)S(1)} %collective-permute-done.8.refs_3_, ...), custom_call_target="tpu_custom_call", output_to_operand_aliasing={{}: (8, {})} | custom-call | flops 536870912 | bytes 2097152 | tf_op jit(solution)/shard_map/pallas_call | solution.py:238
  42.3 0.0 collective-permute-done.3.refs_4_
  42.4 1.7 %shard_map.41 = bf16[128,1024]{1,0:T(8,128)(2,1)S(1)} custom-call(s32[4,3]{1,0:T(4,128)S(1)} %pad_add_fusion.1.refs_0_, bf16[4,16,1024]{2,1,0:T(8,128)(2,1)S(1)} %bitcast.36, bf16[4,16,4224]{2,1,0:T(8,128)(2,1)S(1)} %collective-permute-done.1.refs_2_, bf16[2,4,16,1024]{3,2,1,0:T(8,128)(2,1)S(1)} %collective-permute-done.2.refs_3_, ...), custom_call_target="tpu_custom_call" | custom-call | flops 268435456 | bytes 2097152 | tf_op jit(solution)/shard_map/pallas_call | solution.py:238
  44.0 0.1 collective-permute-start.10
  44.1 1.7 %shard_map.40 = f32[128,1024]{1,0:T(8,128)S(1)} custom-call(s32[4,3]{1,0:T(4,128)S(1)} %pad_add_fusion.1.refs_0_, bf16[4,16,1024]{2,1,0:T(8,128)(2,1)S(1)} %bitcast.37, bf16[4,16,4224]{2,1,0:T(8,128)(2,1)S(1)} %collective-permute-done.1.refs_2_, bf16[2,4,16,1024]{3,2,1,0:T(8,128)(2,1)S(1)} %collective-permute-done.2.refs_3_, ...), custom_call_target="tpu_custom_call" | custom-call | flops 268435456 | bytes 2097152 | tf_op jit(solution)/shard_map/pallas_call | solution.py:238
  45.8 0.0 collective-permute-done.10
  45.8 0.8 %add_convert_fusion = bf16[128,1024]{1,0:T(8,128)(2,1)} fusion(f32[128,1024]{1,0:T(8,128)S(1)} %shard_map.40, bf16[128,1024]{1,0:T(8,128)(2,1)S(1)} %collective-permute-done.10), kind=kLoop, calls=%fused_computation.2 | loop fusion | flops 393216 | bytes 1048576 | tf_op jit(solution)/shard_map/convert_element_type | solution.py:347
  (13 shorter events, 0.2 us)
Async XLA Ops:
  0.0 1.9 %copy-start.1 = (s32[8,4]{0,1:T(4,128)S(1)}, s32[8,4]{0,1:T(4,128)}, u32[]{:S(2)}) copy-start(s32[8,4]{0,1:T(4,128)} %param.4) | copy-start | bytes 388
  1.6 1.3 %copy-start = (bf16[8,4,2,8192]{3,2,1,0:T(2,128)(2,1)S(1)}, bf16[8,4,2,8192]{3,2,1,0:T(2,128)(2,1)}, u32[]{:S(2)}) copy-start(bf16[8,4,2,8192]{3,2,1,0:T(2,128)(2,1)} %param.3) | copy-start | bytes 3145732
  1.9 1.7 %copy-start.2 = (s32[2,2]{1,0:T(2,128)S(1)}, s32[2,2]{1,0:T(2,128)}, u32[]{:S(2)}) copy-start(s32[2,2]{1,0:T(2,128)} %param.5) | copy-start | bytes 52
  2.2 3.1 %collective-permute-start.1 = (bf16[4,16,4224]{2,1,0:T(8,128)(2,1)S(1)}, bf16[4,16,4224]{2,1,0:T(8,128)(2,1)S(1)}, u32[]{:S(2)}, u32[]{:S(2)}) collective-permute-start(bf16[4,16,4224]{2,1,0:T(8,128)(2,1)S(1)} %pad_maximum_fusion), channel_id=1, source_target_pairs={{0,1},{1,0},{2,3},{3,2},{4,5},{5,4},{6,7},{7,6},{8,9},{9,8},{10,11... | collective-permute-start | bytes 1622024 | tf_op jit(solution)/shard_map/ppermute | solution.py:21
  3.3 7.4 %collective-permute-start.4 = (bf16[4,16,2048]{2,1,0:T(8,128)(2,1)S(1)}, bf16[4,16,2048]{2,1,0:T(8,128)(2,1)S(1)}, u32[]{:S(2)}, u32[]{:S(2)}) collective-permute-start(bf16[4,16,2048]{2,1,0:T(8,128)(2,1)S(1)} %bitcast.32), channel_id=1, source_target_pairs={{0,2},{1,3},{2,0},{3,1},{4,6},{5,7},{6,4},{7,5},{8,10},{9,11},{10,... | collective-permute-start | bytes 786440 | tf_op jit(solution)/shard_map/ppermute | solution.py:21
  3.6 1.7 %collective-permute-start = (s32[2,2]{1,0:T(2,128)S(1)}, s32[2,2]{1,0:T(2,128)S(1)}, u32[]{:S(2)}, u32[]{:S(2)}) collective-permute-start(s32[2,2]{1,0:T(2,128)S(1)} %copy-done.2), channel_id=1, source_target_pairs={{0,1},{1,0},{2,3},{3,2},{4,5},{5,4},{6,7},{7,6},{8,9},{9,8},{10,11... | collective-permute-start | bytes 56 | tf_op jit(solution)/shard_map/ppermute | solution.py:21
  5.5 11.2 %collective-permute-start.5 = (bf16[4,16,2176]{2,1,0:T(8,128)(2,1)S(1)}, bf16[4,16,2176]{2,1,0:T(8,128)(2,1)S(1)}, u32[]{:S(2)}, u32[]{:S(2)}) collective-permute-start(bf16[4,16,2176]{2,1,0:T(8,128)(2,1)S(1)} %pad_maximum_fusion.1), channel_id=1, source_target_pairs={{0,2},{1,3},{2,0},{3,1},{4,6},{5,7},{6,4},{7,5},{8,10},{9,11},{10,... | collective-permute-start | bytes 835592 | tf_op jit(solution)/shard_map/ppermute | solution.py:21
  6.9 15.5 %collective-permute-start.8 = (bf16[2,4,16,1024]{3,2,1,0:T(8,128)(2,1)S(1)}, bf16[2,4,16,1024]{3,2,1,0:T(8,128)(2,1)S(1)}, u32[]{:S(2)}, u32[]{:S(2)}) collective-permute-start(bf16[2,4,16,1024]{3,2,1,0:T(8,128)(2,1)S(1)} %pad_maximum_fusion.3), channel_id=1, source_target_pairs={{0,2},{1,3},{2,0},{3,1},{4,6},{5,7},{6,4},{7,5},{8,10},{9,11},{10,... | collective-permute-start | bytes 786440 | tf_op jit(solution)/shard_map/ppermute | solution.py:21
  7.1 20.8 %collective-permute-start.2 = (bf16[2,4,16,1024]{3,2,1,0:T(8,128)(2,1)S(1)}, bf16[2,4,16,1024]{3,2,1,0:T(8,128)(2,1)S(1)}, u32[]{:S(2)}, u32[]{:S(2)}) collective-permute-start(bf16[2,4,16,1024]{3,2,1,0:T(8,128)(2,1)S(1)} %pad_maximum_fusion.2), channel_id=1, source_target_pairs={{0,2},{1,3},{2,0},{3,1},{4,6},{5,7},{6,4},{7,5},{8,10},{9,11},{10,... | collective-permute-start | bytes 786440 | tf_op jit(solution)/shard_map/ppermute | solution.py:21
  10.7 25.1 %collective-permute-start.6 = (bf16[4,16,2048]{2,1,0:T(8,128)(2,1)S(1)}, bf16[4,16,2048]{2,1,0:T(8,128)(2,1)S(1)}, u32[]{:S(2)}, u32[]{:S(2)}) collective-permute-start(bf16[4,16,2048]{2,1,0:T(8,128)(2,1)S(1)} %collective-permute-done.4.refs_3_), channel_id=1, source_target_pairs={{0,4},{1,5},{2,14},{3,15},{4,8},{5,9},{6,2},{7,3},{8,12},{9,13},{1... | collective-permute-start | bytes 786440 | tf_op jit(solution)/shard_map/ppermute | solution.py:21
  16.7 19.2 %collective-permute-start.7 = (bf16[4,16,2176]{2,1,0:T(8,128)(2,1)S(1)}, bf16[4,16,2176]{2,1,0:T(8,128)(2,1)S(1)}, u32[]{:S(2)}, u32[]{:S(2)}) collective-permute-start(bf16[4,16,2176]{2,1,0:T(8,128)(2,1)S(1)} %collective-permute-done.5.refs_4_), channel_id=1, source_target_pairs={{0,4},{1,5},{2,14},{3,15},{4,8},{5,9},{6,2},{7,3},{8,12},{9,13},{1... | collective-permute-start | bytes 835592 | tf_op jit(solution)/shard_map/ppermute | solution.py:21
  22.3 17.9 %collective-permute-start.9 = (bf16[2,4,16,1024]{3,2,1,0:T(8,128)(2,1)S(1)}, bf16[2,4,16,1024]{3,2,1,0:T(8,128)(2,1)S(1)}, u32[]{:S(2)}, u32[]{:S(2)}) collective-permute-start(bf16[2,4,16,1024]{3,2,1,0:T(8,128)(2,1)S(1)} %collective-permute-done.8.refs_3_), channel_id=1, source_target_pairs={{0,4},{1,5},{2,14},{3,15},{4,8},{5,9},{6,2},{7,3},{8,12},{9,13},{1... | collective-permute-start | bytes 786440 | tf_op jit(solution)/shard_map/ppermute | solution.py:21
  27.9 14.4 %collective-permute-start.3 = (bf16[2,4,16,1024]{3,2,1,0:T(8,128)(2,1)S(1)}, bf16[2,4,16,1024]{3,2,1,0:T(8,128)(2,1)S(1)}, u32[]{:S(2)}, u32[]{:S(2)}) collective-permute-start(bf16[2,4,16,1024]{3,2,1,0:T(8,128)(2,1)S(1)} %collective-permute-done.2.refs_3_), channel_id=1, source_target_pairs={{0,4},{1,5},{2,0},{3,14},{4,8},{5,9},{6,2},{7,3},{8,12},{9,13},{10... | collective-permute-start | bytes 786440 | tf_op jit(solution)/shard_map/ppermute | solution.py:21
  44.0 1.8 %collective-permute-start.10 = (bf16[128,1024]{1,0:T(8,128)(2,1)S(1)}, bf16[128,1024]{1,0:T(8,128)(2,1)S(1)}, u32[]{:S(2)}, u32[]{:S(2)}) collective-permute-start(bf16[128,1024]{1,0:T(8,128)(2,1)S(1)} %shard_map.41), channel_id=1, source_target_pairs={{0,1},{1,0},{2,3},{3,2},{4,5},{5,4},{6,7},{7,6},{8,9},{9,8},{10,11... | collective-permute-start | bytes 786440 | tf_op jit(solution)/shard_map/ppermute | solution.py:21

commit v6 on v5

--- a/solution.py
+++ b/solution.py
@@ -112,10 +112,10 @@
         out_ref[:, lag_half - lane - size : lag_half - lane] = flipped.astype(out_ref.dtype)
 
 
-def chunk_kernel(*refs, views_at, slot_count, slot_base, windows, stations, first, last, low, norm):
+def chunk_kernel(*refs, views_at, slot_count, slot_base, windows, stations, first, last, low, norm, staged):
     refs = list(refs)
     slots_ref = refs.pop(0)
-    sources = [refs.pop(0) for _ in range(1 + max(which for which, _, _ in views_at))]
+    sources = [refs.pop(0) for _ in range(0 if staged else 1 + max(which for which, _, _ in views_at))]
     mark_source = refs.pop(0)
     cos_ref, sin_ref = (refs.pop(0) for _ in range(2))
     if not first:
@@ -128,7 +128,7 @@
     if first:
         weight_ref = refs.pop(0)
         marks = refs.pop(0)
-    stage = refs.pop(0)
+    stage = mark_source if staged else refs.pop(0)
     buffers = [(refs[0], refs[1]), (refs[2], refs[3])]
     count = stage.shape[-1]
     lag_half = cos_ref.shape[1]
@@ -145,7 +145,7 @@
     else:
         acc_ref[:, 2 * lag_half :] = before_ref[held_rows, 2 * lag_half :]
 
-    for at, (which, part, lane) in enumerate(views_at):
+    for at, (which, part, lane) in enumerate([] if staged else views_at):
         view = sources[which] if part is None else sources[which].at[part]
         for window in range(windows):
             mark = marks[at, window]
@@ -226,7 +226,9 @@
     if last:
         operands.append(weights)
     vmem = pl.BlockSpec(memory_space=pltpu.VMEM)
-    scratch = [pltpu.VMEM((6, windows, 2 * stations, count), jnp.float32)]
+    stage_shape = (6, windows, 2 * stations, count)
+    staged = last == jnp.float32
+    scratch = [] if last else [pltpu.VMEM(stage_shape, jnp.float32)]
     scratch += [pltpu.VMEM((rows, width), jnp.bfloat16)] * 4
     outs = [acc]
     if first:
@@ -234,6 +236,8 @@
         outs.append(jax.ShapeDtypeStruct((6, windows, stations, LANES), jnp.float32))
     if last:
         outs = [jax.ShapeDtypeStruct((rows, 2 * lag_half), last)]
+        if not staged:
+            outs.append(jax.ShapeDtypeStruct(stage_shape, jnp.float32))
         scratch.append(pltpu.VMEM(acc.shape, jnp.float32))
     return pl.pallas_call(
         functools.partial(
@@ -246,6 +250,7 @@
             first=first,
             last=last,
             low=low,
+            staged=staged,
             norm=norm,
         ),
         in_specs=[pl.BlockSpec(memory_space=pltpu.SMEM)] + [vmem] * len(operands),
@@ -330,16 +335,16 @@
             views_at = [(0, None, 0), (1, None, LANES + low), (2, 0, 0), (2, 1, 0), (3, 0, 0), (3, 1, 0)]
         width = SUB // 2 if last or (high - low) % SUB else SUB
 
-        def part(kind, slot_base, slots_here):
+        def part(kind, slot_base, slots_here, stage=None):
             return chunk_call(
-                table, sources, views_at, mark_source, tables, acc, weights, kind,
+                table, sources if stage is None else [], views_at, mark_source if stage is None else stage, tables, acc, weights, kind,
                 slot_base, slots_here, low, high - low, width, windows, stations, norm,
             )
 
         if last:
-            (theirs,) = part(jnp.bfloat16, slot_count, slot_count)
+            theirs, stage = part(jnp.bfloat16, slot_count, slot_count)
             other = permute(theirs, core_pairs)
-            (mine,) = part(jnp.float32, 0, slot_count)
+            (mine,) = part(jnp.float32, 0, slot_count, stage)
         elif unit == 0:
             acc, weights, mark_source = part(None, 0, 2 * slot_count)
         else:

time: 46.7 us -> 46.4 us (level)
  no operation moved by 1% of the time
where the time goes in v6:
time: 46.4 us; the launch traced here: 46.3 us
  starting transfers between devices  19.4 us (42%)
  Pallas kernels  11.8 us (25%)
  waiting for transfers between devices  9.9 us (21%)
  other arithmetic  4.13 us (9%)
  local copies, waits for them, and re-layouts  0.9 us (2%)
    ppermute x11, starting transfers between devices, permute(): return lax.ppermute(array, 'sta', pairs)  19.4 us
    ppermute x11, waiting for transfers between devices, permute(): return lax.ppermute(array, 'sta', pairs)  9.9 us
    pallas_call x5, Pallas kernels, chunk_call(): pl.pallas_call(functools.partial(chunk_kernel, views_at=views_at, slot_co...  9.54 us
    pallas_call x1, Pallas kernels, lag_tables(): pl.pallas_call(table_kernel, in_specs=[vmem] * 4, out_specs=[vmem] * 2, o...  2.24 us
    mul x3, other arithmetic, rows_of(): piece.transpose(1, 2, 0, 3) * unit_scale  2.09 us
    sin x1, other arithmetic, angle_tables(): return (jnp.cos(phase_angle), jnp.sin(phase_angle))  1.06 us
  transfers between devices with their start and end apart: 11, of which 5 were waited for; matrix products, arithmetic and copies ran while one was open for 5% of the time, Pallas kernels for 22%

profile of v6, /device:TPU:7, one launch (start us, length us, event | category | flops | bytes accessed | tf_op | source)
XLA Modules:
  0.0 46.3 jit_solution(1957921368661743904)
XLA Ops:
  0.0 0.0 copy-start.1
  0.0 1.6 %multiply_bitcast_fusion = bf16[4,2,8,4096]{3,1,0,2:T(2,128)(2,1)S(1)} fusion(bf16[8,4,2,8192]{3,2,1,0:T(2,128)(2,1)} %param.3, s32[]{:T(128)S(6)} %select_n.36, bf16[]{:T(256)} %constant.43.clone.1), kind=kLoop, calls=%fused_computation.3 | loop fusion | flops 1048576 | bytes 1048582 | tf_op jit(solution)/shard_map/mul | solution.py:287
  1.6 0.0 copy-start
  1.6 0.3 copy.18
  1.9 0.0 copy-done.1
  1.9 0.0 copy-start.2
  2.0 0.1 broadcast_in_dim.29
  2.1 0.1 broadcast_in_dim.30.refs_7_
  2.2 0.7 %collective-permute-start.1 = (bf16[4,16,4224]{2,1,0:T(8,128)(2,1)S(1)}, bf16[4,16,4224]{2,1,0:T(8,128)(2,1)S(1)}, u32[]{:S(2)}, u32[]{:S(2)}) collective-permute-start(bf16[4,16,4224]{2,1,0:T(8,128)(2,1)S(1)} %pad_maximum_fusion), channel_id=1, source_target_pairs={{0,1},{1,0},{2,3},{3,2},{4,5},{5,4},{6,7},{7,6},{8,9},{9,8},{10,11... | collective-permute-start | bytes 1622024 | tf_op jit(solution)/shard_map/ppermute | solution.py:21
  2.9 0.0 copy-done
  2.9 0.3 multiply_bitcast_fusion.1
  3.2 0.2 copy.19
  3.3 0.3 collective-permute-start.4
  3.6 0.0 copy-done.2
  3.6 0.8 %collective-permute-start = (s32[2,2]{1,0:T(2,128)S(1)}, s32[2,2]{1,0:T(2,128)S(1)}, u32[]{:S(2)}, u32[]{:S(2)}) collective-permute-start(s32[2,2]{1,0:T(2,128)S(1)} %copy-done.2), channel_id=1, source_target_pairs={{0,1},{1,0},{2,3},{3,2},{4,5},{5,4},{6,7},{7,6},{8,9},{9,8},{10,11... | collective-permute-start | bytes 56 | tf_op jit(solution)/shard_map/ppermute | solution.py:21
  4.5 0.2 multiply_bitcast_fusion.2
  4.7 0.1 copy.21
  4.8 0.1 copy.20
  4.9 0.4 collective-permute-done
  5.3 0.0 collective-permute-done.1.refs_2_
  5.4 0.1 broadcast_in_dim.31
  5.5 1.3 %collective-permute-start.5 = (bf16[4,16,2176]{2,1,0:T(8,128)(2,1)S(1)}, bf16[4,16,2176]{2,1,0:T(8,128)(2,1)S(1)}, u32[]{:S(2)}, u32[]{:S(2)}) collective-permute-start(bf16[4,16,2176]{2,1,0:T(8,128)(2,1)S(1)} %pad_maximum_fusion.1), channel_id=1, source_target_pairs={{0,2},{1,3},{2,0},{3,1},{4,6},{5,7},{6,4},{7,5},{8,10},{9,11},{10,... | collective-permute-start | bytes 835592 | tf_op jit(solution)/shard_map/ppermute | solution.py:21
  6.9 0.3 collective-permute-start.8
  7.1 1.2 %collective-permute-start.2 = (bf16[2,4,16,1024]{3,2,1,0:T(8,128)(2,1)S(1)}, bf16[2,4,16,1024]{3,2,1,0:T(8,128)(2,1)S(1)}, u32[]{:S(2)}, u32[]{:S(2)}) collective-permute-start(bf16[2,4,16,1024]{3,2,1,0:T(8,128)(2,1)S(1)} %pad_maximum_fusion.2), channel_id=1, source_target_pairs={{0,2},{1,3},{2,0},{3,1},{4,6},{5,7},{6,4},{7,5},{8,10},{9,11},{10,... | collective-permute-start | bytes 786440 | tf_op jit(solution)/shard_map/ppermute | solution.py:21
  8.4 0.1 pad_add_fusion.1.refs_0_
  8.5 2.3 %collective-permute-done.4.refs_3_ = bf16[4,16,2048]{2,1,0:T(8,128)(2,1)S(1)} collective-permute-done((bf16[4,16,2048]{2,1,0:T(8,128)(2,1)S(1)}, bf16[4,16,2048]{2,1,0:T(8,128)(2,1)S(1)}, u32[]{:S(2)}, u32[]{:S(2)}) %collective-permute-start.4) | collective-permute-done | bytes 262176 | tf_op jit(solution)/shard_map/ppermute | solution.py:21
  10.7 3.3 %collective-permute-start.6 = (bf16[4,16,2048]{2,1,0:T(8,128)(2,1)S(1)}, bf16[4,16,2048]{2,1,0:T(8,128)(2,1)S(1)}, u32[]{:S(2)}, u32[]{:S(2)}) collective-permute-start(bf16[4,16,2048]{2,1,0:T(8,128)(2,1)S(1)} %collective-permute-done.4.refs_3_), channel_id=1, source_target_pairs={{0,4},{1,5},{2,14},{3,15},{4,8},{5,9},{6,2},{7,3},{8,12},{9,13},{1... | collective-permute-start | bytes 786440 | tf_op jit(solution)/shard_map/ppermute | solution.py:21
  14.0 2.6 %collective-permute-done.5.refs_4_ = bf16[4,16,2176]{2,1,0:T(8,128)(2,1)S(1)} collective-permute-done((bf16[4,16,2176]{2,1,0:T(8,128)(2,1)S(1)}, bf16[4,16,2176]{2,1,0:T(8,128)(2,1)S(1)}, u32[]{:S(2)}, u32[]{:S(2)}) %collective-permute-start.5) | collective-permute-done | bytes 278560 | tf_op jit(solution)/shard_map/ppermute | solution.py:21
  16.7 3.3 %collective-permute-start.7 = (bf16[4,16,2176]{2,1,0:T(8,128)(2,1)S(1)}, bf16[4,16,2176]{2,1,0:T(8,128)(2,1)S(1)}, u32[]{:S(2)}, u32[]{:S(2)}) collective-permute-start(bf16[4,16,2176]{2,1,0:T(8,128)(2,1)S(1)} %collective-permute-done.5.refs_4_), channel_id=1, source_target_pairs={{0,4},{1,5},{2,14},{3,15},{4,8},{5,9},{6,2},{7,3},{8,12},{9,13},{1... | collective-permute-start | bytes 835592 | tf_op jit(solution)/shard_map/ppermute | solution.py:21
  20.0 2.3 %collective-permute-done.8.refs_3_ = bf16[2,4,16,1024]{3,2,1,0:T(8,128)(2,1)S(1)} collective-permute-done((bf16[2,4,16,1024]{3,2,1,0:T(8,128)(2,1)S(1)}, bf16[2,4,16,1024]{3,2,1,0:T(8,128)(2,1)S(1)}, u32[]{:S(2)}, u32[]{:S(2)}) %collective-permute-start.8) | collective-permute-done | bytes 262176 | tf_op jit(solution)/shard_map/ppermute | solution.py:21
  22.3 3.3 %collective-permute-start.9 = (bf16[2,4,16,1024]{3,2,1,0:T(8,128)(2,1)S(1)}, bf16[2,4,16,1024]{3,2,1,0:T(8,128)(2,1)S(1)}, u32[]{:S(2)}, u32[]{:S(2)}) collective-permute-start(bf16[2,4,16,1024]{3,2,1,0:T(8,128)(2,1)S(1)} %collective-permute-done.8.refs_3_), channel_id=1, source_target_pairs={{0,4},{1,5},{2,14},{3,15},{4,8},{5,9},{6,2},{7,3},{8,12},{9,13},{1... | collective-permute-start | bytes 786440 | tf_op jit(solution)/shard_map/ppermute | solution.py:21
  25.6 2.3 %collective-permute-done.2.refs_3_ = bf16[2,4,16,1024]{3,2,1,0:T(8,128)(2,1)S(1)} collective-permute-done((bf16[2,4,16,1024]{3,2,1,0:T(8,128)(2,1)S(1)}, bf16[2,4,16,1024]{3,2,1,0:T(8,128)(2,1)S(1)}, u32[]{:S(2)}, u32[]{:S(2)}) %collective-permute-start.2) | collective-permute-done | bytes 262176 | tf_op jit(solution)/shard_map/ppermute | solution.py:21
  27.9 4.6 %collective-permute-start.3 = (bf16[2,4,16,1024]{3,2,1,0:T(8,128)(2,1)S(1)}, bf16[2,4,16,1024]{3,2,1,0:T(8,128)(2,1)S(1)}, u32[]{:S(2)}, u32[]{:S(2)}) collective-permute-start(bf16[2,4,16,1024]{3,2,1,0:T(8,128)(2,1)S(1)} %collective-permute-done.2.refs_3_), channel_id=1, source_target_pairs={{0,4},{1,5},{2,0},{3,14},{4,8},{5,9},{6,2},{7,3},{8,12},{9,13},{10... | collective-permute-start | bytes 786440 | tf_op jit(solution)/shard_map/ppermute | solution.py:21
  32.5 1.1 %fusion.11 = (f32[64,512]{1,0:T(8,128)S(1)}, f32[64,512]{1,0:T(8,128)S(1)}, f32[64,512]{1,0:T(8,128)S(1)}, f32[64,512]{1,0:T(8,128)S(1)}) fusion(s32[512]{0:T(512)S(1)} %iota_add_fusion, s32[64]{0:T(128)S(1)} %multiply_add_fusion), kind=kLoop, calls=%fused_computation.36 | loop fusion | flops 917504 | bytes 526592 | tf_op jit(solution)/shard_map/sin | solution.py:28
  33.6 2.2 %tables.1 = (bf16[4096,512]{1,0:T(8,128)(2,1)S(1)}, bf16[4096,512]{1,0:T(8,128)(2,1)S(1)}) custom-call(f32[64,512]{1,0:T(8,128)S(1)} %get-tuple-element.34.fine_cos, f32[64,512]{1,0:T(8,128)S(1)} %get-tuple-element.33.fine_sin, f32[64,512]{1,0:T(8,128)S(1)} %get-tuple-element.32.coarse_cos, f32[64,512]{1,0:T(8,128)S(1)} %get-tuple-element.31.coarse_sin), custom_call_target="tpu_custom_call" | custom-call | flops 12582912 | bytes 8388608 | tf_op jit(solution)/shard_map/tables/pallas_call | solution.py:51
  35.9 0.0 collective-permute-done.6.refs_5_
  35.9 0.0 collective-permute-done.7.refs_6_
  35.9 2.2 %shard_map.37 = (f32[256,1152]{1,0:T(8,128)S(1)}, f32[256,128]{1,0:T(8,128)S(1)}, f32[6,4,8,128]{3,2,1,0:T(8,128)S(1)}) custom-call(s32[4,3]{1,0:T(4,128)S(1)} %pad_add_fusion.1.refs_0_, bf16[4,16,2048]{2,1,0:T(8,128)(2,1)S(1)} %bitcast.33, bf16[4,16,4224]{2,1,0:T(8,128)(2,1)S(1)} %collective-permute-done.1.refs_2_, ...), custom_call_target="tpu_custom_call" | custom-call | flops 536870912 | bytes 2097152 | tf_op jit(solution)/shard_map/pallas_call | solution.py:242
  38.0 2.2 %shard_map.38.refs_8_ = f32[256,1152]{1,0:T(8,128)S(1)} custom-call(s32[4,3]{1,0:T(4,128)S(1)} %pad_add_fusion.1.refs_0_, bf16[4,16,2048]{2,1,0:T(8,128)(2,1)S(1)} %bitcast.34, bf16[4,16,4224]{2,1,0:T(8,128)(2,1)S(1)} %collective-permute-done.1.refs_2_, bf16[4,16,2048]{2,1,0:T(8,128)(2,1)S(1)} %collective-permute-done.4.refs_3_, ...), custom_call_target="tpu_custom_call", output_to_operand_aliasing={{}: (10, {})} | custom-call | flops 536870912 | bytes 2097152 | tf_op jit(solution)/shard_map/pallas_call | solution.py:242
  40.2 0.0 collective-permute-done.9.refs_4_
  40.2 2.1 %shard_map.39.refs_8_.refs_4_ = f32[256,1152]{1,0:T(8,128)S(1)} custom-call(s32[4,3]{1,0:T(4,128)S(1)} %pad_add_fusion.1.refs_0_, bf16[4,16,1024]{2,1,0:T(8,128)(2,1)S(1)} %bitcast.38, bf16[4,16,4224]{2,1,0:T(8,128)(2,1)S(1)} %collective-permute-done.1.refs_2_, ...), custom_call_target="tpu_custom_call", output_to_operand_aliasing={{}: (8, {})} | custom-call | flops 536870912 | bytes 2097152 | tf_op jit(solution)/shard_map/pallas_call | solution.py:242
  42.3 0.0 collective-permute-done.3.refs_4_
  42.4 1.6 %shard_map.40 = (bf16[128,1024]{1,0:T(8,128)(2,1)S(1)}, f32[6,4,16,1024]{3,2,1,0:T(8,128)S(1)}) custom-call(s32[4,3]{1,0:T(4,128)S(1)} %pad_add_fusion.1.refs_0_, bf16[4,16,1024]{2,1,0:T(8,128)(2,1)S(1)} %bitcast.36, bf16[4,16,4224]{2,1,0:T(8,128)(2,1)S(1)} %collective-permute-done.1.refs_2_, bf16[2,4,16,1024]{3,2,1,0:T(8,128)(2,1)S(1)} %collective-permute-done.2.refs_3_, ...), custom_call_target="tpu_custom_call" | custom-call | flops 268435456 | bytes 2097152 | tf_op jit(solution)/shard_map/pallas_call | solution.py:242
  43.9 0.1 collective-permute-start.10
  44.0 1.5 %shard_map.41 = f32[128,1024]{1,0:T(8,128)S(1)} custom-call(s32[4,3]{1,0:T(4,128)S(1)} %pad_add_fusion.1.refs_0_, f32[6,4,16,1024]{3,2,1,0:T(8,128)S(1)} %get-tuple-element.21.refs_1_, bf16[4096,512]{1,0:T(8,128)(2,1)S(1)} %get-tuple-element.16.refs_8_.refs_6_.refs_2_, bf16[4096,512]{1,0:T(8,128)(2,1)S(1)} %get-tuple-element.17.refs_9_.refs_7_.refs_3_, ...), custom_call_target="tpu_custom_call" | custom-call | flops 268435456 | bytes 2097152 | tf_op jit(solution)/shard_map/pallas_call | solution.py:242
  45.5 0.0 collective-permute-done.10
  45.5 0.8 %add_convert_fusion = bf16[128,1024]{1,0:T(8,128)(2,1)} fusion(f32[128,1024]{1,0:T(8,128)S(1)} %shard_map.41, bf16[128,1024]{1,0:T(8,128)(2,1)S(1)} %collective-permute-done.10), kind=kLoop, calls=%fused_computation.2 | loop fusion | flops 393216 | bytes 1048576 | tf_op jit(solution)/shard_map/convert_element_type | solution.py:352
  (13 shorter events, 0.2 us)
Async XLA Ops:
  0.0 1.9 %copy-start.1 = (s32[8,4]{0,1:T(4,128)S(1)}, s32[8,4]{0,1:T(4,128)}, u32[]{:S(2)}) copy-start(s32[8,4]{0,1:T(4,128)} %param.4) | copy-start | bytes 388
  1.6 1.3 %copy-start = (bf16[8,4,2,8192]{3,2,1,0:T(2,128)(2,1)S(1)}, bf16[8,4,2,8192]{3,2,1,0:T(2,128)(2,1)}, u32[]{:S(2)}) copy-start(bf16[8,4,2,8192]{3,2,1,0:T(2,128)(2,1)} %param.3) | copy-start | bytes 3145732
  1.9 1.7 %copy-start.2 = (s32[2,2]{1,0:T(2,128)S(1)}, s32[2,2]{1,0:T(2,128)}, u32[]{:S(2)}) copy-start(s32[2,2]{1,0:T(2,128)} %param.5) | copy-start | bytes 52
  2.2 3.1 %collective-permute-start.1 = (bf16[4,16,4224]{2,1,0:T(8,128)(2,1)S(1)}, bf16[4,16,4224]{2,1,0:T(8,128)(2,1)S(1)}, u32[]{:S(2)}, u32[]{:S(2)}) collective-permute-start(bf16[4,16,4224]{2,1,0:T(8,128)(2,1)S(1)} %pad_maximum_fusion), channel_id=1, source_target_pairs={{0,1},{1,0},{2,3},{3,2},{4,5},{5,4},{6,7},{7,6},{8,9},{9,8},{10,11... | collective-permute-start | bytes 1622024 | tf_op jit(solution)/shard_map/ppermute | solution.py:21
  3.3 7.4 %collective-permute-start.4 = (bf16[4,16,2048]{2,1,0:T(8,128)(2,1)S(1)}, bf16[4,16,2048]{2,1,0:T(8,128)(2,1)S(1)}, u32[]{:S(2)}, u32[]{:S(2)}) collective-permute-start(bf16[4,16,2048]{2,1,0:T(8,128)(2,1)S(1)} %bitcast.32), channel_id=1, source_target_pairs={{0,2},{1,3},{2,0},{3,1},{4,6},{5,7},{6,4},{7,5},{8,10},{9,11},{10,... | collective-permute-start | bytes 786440 | tf_op jit(solution)/shard_map/ppermute | solution.py:21
  3.6 1.7 %collective-permute-start = (s32[2,2]{1,0:T(2,128)S(1)}, s32[2,2]{1,0:T(2,128)S(1)}, u32[]{:S(2)}, u32[]{:S(2)}) collective-permute-start(s32[2,2]{1,0:T(2,128)S(1)} %copy-done.2), channel_id=1, source_target_pairs={{0,1},{1,0},{2,3},{3,2},{4,5},{5,4},{6,7},{7,6},{8,9},{9,8},{10,11... | collective-permute-start | bytes 56 | tf_op jit(solution)/shard_map/ppermute | solution.py:21
  5.5 11.2 %collective-permute-start.5 = (bf16[4,16,2176]{2,1,0:T(8,128)(2,1)S(1)}, bf16[4,16,2176]{2,1,0:T(8,128)(2,1)S(1)}, u32[]{:S(2)}, u32[]{:S(2)}) collective-permute-start(bf16[4,16,2176]{2,1,0:T(8,128)(2,1)S(1)} %pad_maximum_fusion.1), channel_id=1, source_target_pairs={{0,2},{1,3},{2,0},{3,1},{4,6},{5,7},{6,4},{7,5},{8,10},{9,11},{10,... | collective-permute-start | bytes 835592 | tf_op jit(solution)/shard_map/ppermute | solution.py:21
  6.9 15.5 %collective-permute-start.8 = (bf16[2,4,16,1024]{3,2,1,0:T(8,128)(2,1)S(1)}, bf16[2,4,16,1024]{3,2,1,0:T(8,128)(2,1)S(1)}, u32[]{:S(2)}, u32[]{:S(2)}) collective-permute-start(bf16[2,4,16,1024]{3,2,1,0:T(8,128)(2,1)S(1)} %pad_maximum_fusion.3), channel_id=1, source_target_pairs={{0,2},{1,3},{2,0},{3,1},{4,6},{5,7},{6,4},{7,5},{8,10},{9,11},{10,... | collective-permute-start | bytes 786440 | tf_op jit(solution)/shard_map/ppermute | solution.py:21
  7.1 20.8 %collective-permute-start.2 = (bf16[2,4,16,1024]{3,2,1,0:T(8,128)(2,1)S(1)}, bf16[2,4,16,1024]{3,2,1,0:T(8,128)(2,1)S(1)}, u32[]{:S(2)}, u32[]{:S(2)}) collective-permute-start(bf16[2,4,16,1024]{3,2,1,0:T(8,128)(2,1)S(1)} %pad_maximum_fusion.2), channel_id=1, source_target_pairs={{0,2},{1,3},{2,0},{3,1},{4,6},{5,7},{6,4},{7,5},{8,10},{9,11},{10,... | collective-permute-start | bytes 786440 | tf_op jit(solution)/shard_map/ppermute | solution.py:21
  10.7 25.1 %collective-permute-start.6 = (bf16[4,16,2048]{2,1,0:T(8,128)(2,1)S(1)}, bf16[4,16,2048]{2,1,0:T(8,128)(2,1)S(1)}, u32[]{:S(2)}, u32[]{:S(2)}) collective-permute-start(bf16[4,16,2048]{2,1,0:T(8,128)(2,1)S(1)} %collective-permute-done.4.refs_3_), channel_id=1, source_target_pairs={{0,4},{1,5},{2,14},{3,15},{4,8},{5,9},{6,2},{7,3},{8,12},{9,13},{1... | collective-permute-start | bytes 786440 | tf_op jit(solution)/shard_map/ppermute | solution.py:21
  16.7 19.2 %collective-permute-start.7 = (bf16[4,16,2176]{2,1,0:T(8,128)(2,1)S(1)}, bf16[4,16,2176]{2,1,0:T(8,128)(2,1)S(1)}, u32[]{:S(2)}, u32[]{:S(2)}) collective-permute-start(bf16[4,16,2176]{2,1,0:T(8,128)(2,1)S(1)} %collective-permute-done.5.refs_4_), channel_id=1, source_target_pairs={{0,4},{1,5},{2,14},{3,15},{4,8},{5,9},{6,2},{7,3},{8,12},{9,13},{1... | collective-permute-start | bytes 835592 | tf_op jit(solution)/shard_map/ppermute | solution.py:21
  22.3 17.9 %collective-permute-start.9 = (bf16[2,4,16,1024]{3,2,1,0:T(8,128)(2,1)S(1)}, bf16[2,4,16,1024]{3,2,1,0:T(8,128)(2,1)S(1)}, u32[]{:S(2)}, u32[]{:S(2)}) collective-permute-start(bf16[2,4,16,1024]{3,2,1,0:T(8,128)(2,1)S(1)} %collective-permute-done.8.refs_3_), channel_id=1, source_target_pairs={{0,4},{1,5},{2,14},{3,15},{4,8},{5,9},{6,2},{7,3},{8,12},{9,13},{1... | collective-permute-start | bytes 786440 | tf_op jit(solution)/shard_map/ppermute | solution.py:21
  27.9 14.4 %collective-permute-start.3 = (bf16[2,4,16,1024]{3,2,1,0:T(8,128)(2,1)S(1)}, bf16[2,4,16,1024]{3,2,1,0:T(8,128)(2,1)S(1)}, u32[]{:S(2)}, u32[]{:S(2)}) collective-permute-start(bf16[2,4,16,1024]{3,2,1,0:T(8,128)(2,1)S(1)} %collective-permute-done.2.refs_3_), channel_id=1, source_target_pairs={{0,4},{1,5},{2,0},{3,14},{4,8},{5,9},{6,2},{7,3},{8,12},{9,13},{10... | collective-permute-start | bytes 786440 | tf_op jit(solution)/shard_map/ppermute | solution.py:21
  43.9 1.6 %collective-permute-start.10 = (bf16[128,1024]{1,0:T(8,128)(2,1)S(1)}, bf16[128,1024]{1,0:T(8,128)(2,1)S(1)}, u32[]{:S(2)}, u32[]{:S(2)}) collective-permute-start(bf16[128,1024]{1,0:T(8,128)(2,1)S(1)} %get-tuple-element.22), channel_id=1, source_target_pairs={{0,1},{1,0},{2,3},{3,2},{4,5},{5,4},{6,7},{7,6},{8,9},{9,8},{10,11... | collective-permute-start | bytes 786440 | tf_op jit(solution)/shard_map/ppermute | solution.py:21
